TPU v7x, 32 devices: a whole 2x2x4 slice. The times are simulated.
32 devices in a mesh: rep: 2 (over y), seq: 8 (over z, x), head: 2 (over core).
Axes of the slice: x: 2, y: 2, z: 4, core: 2. Of those that a mesh axis runs over, the one named last changes fastest.
Arguments:
- x_in: bfloat16 [1024, 1024], P(('rep', 'seq'), 'head'), parts along dimension 0, may hold values from -6 to 6
- b_in: bfloat16 [1024, 2048], P(('rep', 'seq'), 'head'), parts along dimension 0, may hold values from -6 to 6
- c_in: bfloat16 [1024, 2048], P(('rep', 'seq'), 'head'), parts along dimension 0, may hold values from -6 to 6
- z_in: bfloat16 [1024, 1024], P(('rep', 'seq'), 'head'), parts along dimension 0, may hold values from -6 to 6
- dt_raw: bfloat16 [1024, 16], P(('rep', 'seq'), 'head'), parts along dimension 0, may hold values from -3 to 6
- dt_bias: float32 [16], P('head'), may hold values from -4 to -3
- a_log: float32 [16], P('head')
- d_skip: float32 [16], P('head'), may hold values from 0.5 to 1.5
- conv_x: bfloat16 [4, 1024], P(None, 'head'), may hold values from -3 to 3
- conv_b: bfloat16 [4, 2048], P(None, 'head'), may hold values from -3 to 3
- conv_c: bfloat16 [4, 2048], P(None, 'head'), may hold values from -3 to 3
- norm_gain: float32 [1024], P('head'), may hold values from 0.5 to 1.5
Outputs:
- mixed: bfloat16 [1024, 1024], P(('rep', 'seq'), 'head'), parts along dimension 0
There are 2 independent parts, one for each index of `rep`. A program takes and returns all parts, laid end to end along the dimension named above; an argument that names none is the same for every part. Nothing has to cross between parts.
All inputs are finite; a program needn't handle non-finite values.
Results may differ from a plain program's by a relative error of at most 0.0051.
Values may be sent and summed in bfloat16 or wider, within the bound.
No kernel may reach another device: no remote copies, remote signals or barrier semaphores. Data moves between devices by JAX's collectives and lax.ppermute only.
A program may use at most 64 MiB of HBM per device.

v0:
```python
import jax
import jax.numpy as jnp
from jax import lax
from jax.sharding import PartitionSpec as P

HEAD_DIM = 64
STATE = 256
BLOCK = 256


def causal_conv(padded, kernel, length):
    summed = jnp.zeros((length,) + padded.shape[1:], jnp.float32)
    for offset in range(kernel.shape[0]):
        summed = summed + kernel[offset].astype(jnp.float32) * padded[
            offset : offset + length
        ].astype(jnp.float32)
    return jax.nn.silu(summed).astype(jnp.bfloat16)


def blockwise_scan(x_head, b_head, c_head, rates, decays):
    length = x_head.shape[0]
    blocks = length // BLOCK
    x_part = x_head.reshape(blocks, BLOCK, -1)
    b_part = b_head.reshape(blocks, BLOCK, -1)
    c_part = c_head.reshape(blocks, BLOCK, -1)
    rate_part = rates.reshape(blocks, BLOCK)
    log_decay = jnp.cumsum(decays.reshape(blocks, BLOCK), axis=1)
    causal = jnp.arange(BLOCK)[:, None] >= jnp.arange(BLOCK)[None, :]
    scores = jnp.einsum("cin,cjn->cij", c_part, b_part, preferred_element_type=jnp.float32)
    spread = jnp.where(causal, log_decay[:, :, None] - log_decay[:, None, :], 0.0)
    mixing = jnp.where(causal, scores * jnp.exp(spread) * rate_part[:, None, :], 0.0).astype(
        jnp.bfloat16
    )
    inner = jnp.einsum("cij,cjp->cip", mixing, x_part, preferred_element_type=jnp.float32)
    weighted_b = (
        b_part.astype(jnp.float32)
        * (jnp.exp(log_decay[:, -1:] - log_decay) * rate_part)[:, :, None]
    ).astype(jnp.bfloat16)
    block_states = jnp.einsum(
        "cjn,cjp->cnp", weighted_b, x_part, preferred_element_type=jnp.float32
    )
    totals = log_decay[:, -1]

    def carry_step(state, pair):
        total, fresh = pair
        return (jnp.exp(total) * state + fresh, state)

    final_state, entering = lax.scan(
        carry_step, jnp.zeros(block_states.shape[1:], jnp.float32), (totals, block_states)
    )
    entering_low = entering.astype(jnp.bfloat16)
    outer = jnp.exp(log_decay)[:, :, None] * jnp.einsum(
        "cin,cnp->cip", c_part, entering_low, preferred_element_type=jnp.float32
    )
    return (inner + outer).reshape(length, -1)


def body(x_in, b_in, c_in, z_in, dt_raw, dt_bias, a_log, d_skip, conv_x, conv_b, conv_c, norm_gain):
    local_rows = x_in.shape[0]
    seq_total = lax.axis_size("seq")
    seq_place = lax.axis_index("seq")
    heads_here = dt_raw.shape[1]
    per_device = heads_here // seq_total
    groups_here = b_in.shape[1] // STATE
    per_group = heads_here // groups_here
    kernel_taps = conv_x.shape[0]

    def widen(groupwise, last_dim):
        row_total = groupwise.shape[0]
        copies = jnp.broadcast_to(
            groupwise.reshape(row_total, groups_here, 1, last_dim),
            (row_total, groups_here, per_group, last_dim),
        )
        return copies.reshape(row_total, seq_total, per_device, last_dim)

    x_send, b_send, c_send = (x_in, b_in, c_in)
    outgoing = (
        x_send.reshape(local_rows, seq_total, per_device, HEAD_DIM),
        widen(b_send, STATE),
        widen(c_send, STATE),
        dt_raw.reshape(local_rows, seq_total, per_device),
    )
    arrived = (
        lax.all_to_all(outgoing[0], "seq", split_axis=1, concat_axis=0, tiled=True),
        lax.all_to_all(outgoing[1], "seq", split_axis=1, concat_axis=0, tiled=True),
        lax.all_to_all(outgoing[2], "seq", split_axis=1, concat_axis=0, tiled=True),
        lax.all_to_all(outgoing[3], "seq", split_axis=1, concat_axis=0, tiled=True),
    )
    length = local_rows * seq_total
    x_heads = arrived[0].reshape(length, per_device, HEAD_DIM)
    b_heads = arrived[1].reshape(length, per_device, STATE)
    c_heads = arrived[2].reshape(length, per_device, STATE)
    raw_rates = arrived[3].reshape(length, per_device)
    kernel_x = lax.dynamic_index_in_dim(
        conv_x.reshape(kernel_taps, seq_total, per_device, HEAD_DIM), seq_place, 1, keepdims=False
    )
    kernel_b = lax.dynamic_index_in_dim(widen(conv_b, STATE), seq_place, 1, keepdims=False)
    kernel_c = lax.dynamic_index_in_dim(widen(conv_c, STATE), seq_place, 1, keepdims=False)
    front = ((kernel_taps - 1, 0), (0, 0), (0, 0))
    x_heads = causal_conv(jnp.pad(x_heads, front), kernel_x, length)
    b_heads = causal_conv(jnp.pad(b_heads, front), kernel_b, length)
    c_heads = causal_conv(jnp.pad(c_heads, front), kernel_c, length)
    first_head = seq_place * per_device
    bias_here = lax.dynamic_slice_in_dim(dt_bias, first_head, per_device)
    alog_here = lax.dynamic_slice_in_dim(a_log, first_head, per_device)
    skip_here = lax.dynamic_slice_in_dim(d_skip, first_head, per_device)
    rates = jax.nn.softplus(raw_rates.astype(jnp.float32) + bias_here[None, :])
    decays = rates * (-jnp.exp(alog_here))[None, :]
    scanned = jax.vmap(blockwise_scan, in_axes=1, out_axes=1)(
        x_heads, b_heads, c_heads, rates, decays
    )
    heads_out = (scanned + skip_here[None, :, None] * x_heads.astype(jnp.float32)).astype(
        jnp.bfloat16
    )
    returned = lax.all_to_all(
        heads_out.reshape(length, 1, per_device, HEAD_DIM),
        "seq",
        split_axis=0,
        concat_axis=1,
        tiled=True,
    )
    merged = returned.reshape(local_rows, heads_here * HEAD_DIM).astype(jnp.float32)
    gated = merged * jax.nn.silu(z_in.astype(jnp.float32))
    grouped = gated.reshape(local_rows, groups_here, -1)
    mean_square = jnp.mean(grouped * grouped, axis=-1, keepdims=True)
    normed = (grouped * lax.rsqrt(mean_square + 1e-05)).reshape(local_rows, -1)
    return (normed * norm_gain[None, :]).astype(jnp.bfloat16)


def solution(mesh):
    placed = (
        P(("rep", "seq"), "head"),
        P(("rep", "seq"), "head"),
        P(("rep", "seq"), "head"),
        P(("rep", "seq"), "head"),
        P(("rep", "seq"), "head"),
        P("head"),
        P("head"),
        P("head"),
        P(None, "head"),
        P(None, "head"),
        P(None, "head"),
        P("head"),
    )
    return jax.shard_map(
        body, mesh=mesh, in_specs=placed, out_specs=P(("rep", "seq"), "head"), check_vma=False
    )
```

profile of v0, /device:TPU:0, one launch (start us, length us, event | category | flops | bytes accessed | tf_op | source)
XLA Modules:
  0.0 69.4 jit_solution(514059991303077825)
XLA Ops:
  0.0 1.3 %copy.99 = bf16[64,8,1]{0,2,1:T(2,128)(2,1)} copy(bf16[64,8,1]{0,1,2:T(8,128)(2,1)} %bitcast.160) | data formatting | bytes 2048 | tf_op jit(solution)/shard_map/reshape | solution.py:81
  1.3 7.3 %all-to-all-start.2 = ((bf16[64,8,1]{0,2,1:T(2,128)(2,1)}), bf16[64,8,1]{0,2,1:T(2,128)(2,1)S(1)}, u32[]{:S(2)}, u32[]{:S(2)}) async-start(bf16[64,8,1]{0,2,1:T(2,128)(2,1)} %copy.99), calls=%async_computation.2 | async-start | bytes 8192 | tf_op jit(solution)/shard_map/all_to_all | solution.py:87
  8.6 0.6 copy-done.4
  9.4 0.7 copy-done.6
  10.2 0.6 copy-done.8
  10.8 0.6 dynamic_slice.30
  11.5 0.6 dynamic_slice.31
  12.8 0.8 %copy-done.3 = bf16[64,512]{1,0:T(8,128)(2,1)S(1)} copy-done((bf16[64,512]{1,0:T(8,128)(2,1)S(1)}, bf16[64,512]{1,0:T(8,128)(2,1)}, u32[]{:S(2)}) %copy-start.3) | copy-done | bytes 65560
  13.8 0.8 %reshape.665 = bf16[8,2,2048]{2,1,0:T(2,128)(2,1)} reshape(bf16[8,1,64,64]{3,2,1,0:T(8,128)(2,1)S(1)} %bitcast.145) | data formatting | bytes 131072
  14.7 0.6 copy-done.10
  15.3 0.6 dynamic_slice.33
  15.9 6.0 %all-to-all-start.3 = ((bf16[8,2,2048]{2,1,0:T(2,128)(2,1)}), bf16[8,2,2048]{2,1,0:T(2,128)(2,1)S(1)}, u32[]{:S(2)}, u32[]{:S(2)}) async-start(bf16[8,2,2048]{2,1,0:T(2,128)(2,1)} %reshape.665), calls=%async_computation.3 | async-start | bytes 131072 | tf_op jit(solution)/shard_map/all_to_all | solution.py:84
  21.9 0.6 convert_add_fusion
  22.6 0.6 reduce-window.6
  24.0 4.8 %all-to-all-done.3 = bf16[8,2,2048]{2,1,0:T(2,128)(2,1)S(1)} async-done(((bf16[8,2,2048]{2,1,0:T(2,128)(2,1)}), bf16[8,2,2048]{2,1,0:T(2,128)(2,1)S(1)}, u32[]{:S(2)}, u32[]{:S(2)}) %all-to-all-start.3) | async-done | bytes 65568 | tf_op jit(solution)/shard_map/all_to_all | solution.py:84
  28.8 0.7 %broadcast_in_dim.82 = bf16[64,4,2,256]{3,0,2,1:T(8,128)(2,1)} broadcast(bf16[64,4,256]{2,0,1:T(8,128)(2,1)S(1)} %bitcast.144), dimensions={0,1,3} | broadcast | bytes 393216 | tf_op jit(solution)/shard_map/broadcast_in_dim | solution.py:70
  29.5 3.4 %all-to-all-start.1 = ((bf16[64,8,1,256]{3,0,2,1:T(8,128)(2,1)}), bf16[64,8,1,256]{3,0,2,1:T(8,128)(2,1)S(1)}, u32[]{:S(2)}, u32[]{:S(2)}) async-start(bf16[64,8,1,256]{3,0,2,1:T(8,128)(2,1)} %bitcast.12), calls=%async_computation.1 | async-start | bytes 524288 | tf_op jit(solution)/shard_map/all_to_all | solution.py:85
  33.7 7.5 %all-to-all-done.1 = bf16[64,8,1,256]{3,0,2,1:T(8,128)(2,1)S(1)} async-done(((bf16[64,8,1,256]{3,0,2,1:T(8,128)(2,1)}), bf16[64,8,1,256]{3,0,2,1:T(8,128)(2,1)S(1)}, u32[]{:S(2)}, u32[]{:S(2)}) %all-to-all-start.1) | async-done | bytes 262176 | tf_op jit(solution)/shard_map/all_to_all | solution.py:85
  41.1 0.7 %broadcast_in_dim.41 = bf16[64,4,2,256]{3,0,2,1:T(8,128)(2,1)} broadcast(bf16[64,4,256]{2,0,1:T(8,128)(2,1)S(1)} %bitcast.143), dimensions={0,1,3} | broadcast | bytes 393216 | tf_op jit(solution)/shard_map/broadcast_in_dim | solution.py:70
  41.8 3.4 %all-to-all-start = ((bf16[64,8,1,256]{3,0,2,1:T(8,128)(2,1)}), bf16[64,8,1,256]{3,0,2,1:T(8,128)(2,1)S(1)}, u32[]{:S(2)}, u32[]{:S(2)}) async-start(bf16[64,8,1,256]{3,0,2,1:T(8,128)(2,1)} %bitcast.1), calls=%async_computation | async-start | bytes 524288 | tf_op jit(solution)/shard_map/all_to_all | solution.py:86
  45.9 2.9 %while.13 = (s32[]{:T(128)}, f32[1,256,64]{2,1,0:T(8,128)S(1)}, bf16[2,1,256,64]{3,2,1,0:T(8,128)(2,1)S(1)}, f32[2,1]{0,1:T(1,128)S(1)}, f32[2,1,256,64]{2,3,0,1:T(8,128)S(1)}, /*index=5*/s32[]{:T(128)}, s32[]{:T(128)}) while((s32[]{:T(128)}, f32[1,256,64]{2,1,0:T(8,128)S(1)}, bf16[2,1,256,64]{3,2,1,0:T(8,128)(2,1)S(1)}, ...), condition=%wide.region_3.4_spmd.clone, body=%wide.region_2.3_spmd.clone.sunk | while | flops 65539 | bytes 655472 | solution.py:48
  46.1 0.6 fusion.52
  46.6 0.7 bitcast_add_fusion.4
  47.5 0.6 fusion.52
  48.1 0.7 bitcast_add_fusion.4
  48.8 4.6 %all-to-all-done = bf16[64,8,1,256]{3,0,2,1:T(8,128)(2,1)S(1)} async-done(((bf16[64,8,1,256]{3,0,2,1:T(8,128)(2,1)}), bf16[64,8,1,256]{3,0,2,1:T(8,128)(2,1)S(1)}, u32[]{:S(2)}, u32[]{:S(2)}) %all-to-all-start) | async-done | bytes 262176 | tf_op jit(solution)/shard_map/all_to_all | solution.py:86
  54.6 0.8 %fusion.22 = bf16[512,1,1,64]{0,3,2,1:T(8,128)(2,1)S(1)} fusion(f32[512,1,64]{0,2,1:T(8,128)S(1)} %reshape.647, f32[]{:T(128)} %bitcast.43, bf16[512,1,64]{0,2,1:T(8,128)(2,1)S(1)} %reshape.642, f32[64]{0:T(128)S(1)} %get-tuple-element.105, f32[64]{0:T(128)S(1)} %get-tuple-element.103, f32[64]{0:T(128)S(1)} %get-tuple-element.104, f32[64]{0:T(128)S(1)} %get-tuple-element.102), kind=kLoop, calls=%fused_computation.45 | loop fusion | flops 655360 | bytes 263172 | tf_op jit(solution)/shard_map/reshape | solution.py:116
  55.9 0.7 reduce.2
  56.9 9.6 %all_to_all.63 = bf16[8,2,2048]{2,1,0:T(2,128)(2,1)S(1)} all-to-all(bf16[8,2,2048]{2,1,0:T(2,128)(2,1)S(1)} %reshape.667), channel_id=1, replica_groups=mesh['rep'=2,'seq'=8,'head'=2] {'seq'}, dimensions={0} | all-to-all | bytes 131072 | tf_op jit(solution)/shard_map/all_to_all | solution.py:115
  67.1 0.7 %copy-done = bf16[64,512]{1,0:T(8,128)(2,1)S(1)} copy-done((bf16[64,512]{1,0:T(8,128)(2,1)S(1)}, bf16[64,512]{1,0:T(8,128)(2,1)}, u32[]{:S(2)}) %copy-start) | copy-done | bytes 65560
  68.2 0.5 copy-done.7
  68.8 0.7 fusion.19
  (76 shorter events, 5.9 us)
Async XLA Ops:
  1.3 14.6 %all-to-all-start.2 = ((bf16[64,8,1]{0,2,1:T(2,128)(2,1)}), bf16[64,8,1]{0,2,1:T(2,128)(2,1)S(1)}, u32[]{:S(2)}, u32[]{:S(2)}) async-start(bf16[64,8,1]{0,2,1:T(2,128)(2,1)} %copy.99), calls=%async_computation.2 | async-start | bytes 8192 | tf_op jit(solution)/shard_map/all_to_all | solution.py:87
  8.6 0.7 %copy-start.4 = (bf16[4,1024]{1,0:T(4,128)(2,1)S(1)}, bf16[4,1024]{1,0:T(4,128)(2,1)}, u32[]{:S(2)}) copy-start(bf16[4,1024]{1,0:T(4,128)(2,1)} %param.24) | copy-start | bytes 24580
  8.6 0.7 %copy-start.5 = (bf16[4,1024]{1,0:T(4,128)(2,1)S(1)}, bf16[4,1024]{1,0:T(4,128)(2,1)}, u32[]{:S(2)}) copy-start(bf16[4,1024]{1,0:T(4,128)(2,1)} %param.23) | copy-start | bytes 24580
  8.6 4.2 %copy-start.1 = (bf16[64,1024]{1,0:T(8,128)(2,1)S(1)}, bf16[64,1024]{1,0:T(8,128)(2,1)}, u32[]{:S(2)}) copy-start(bf16[64,1024]{1,0:T(8,128)(2,1)} %param.15) | copy-start | bytes 393220
  9.3 0.7 copy-start.6
  10.2 0.7 copy-start.8
  10.8 0.7 copy-start.9
  12.8 0.8 %copy-start.3 = (bf16[64,512]{1,0:T(8,128)(2,1)S(1)}, bf16[64,512]{1,0:T(8,128)(2,1)}, u32[]{:S(2)}) copy-start(bf16[64,512]{1,0:T(8,128)(2,1)} %param.14) | copy-start | bytes 196612
  13.8 0.9 %copy-start.2 = (bf16[64,1024]{1,0:T(8,128)(2,1)S(1)}, bf16[64,1024]{1,0:T(8,128)(2,1)}, u32[]{:S(2)}) copy-start(bf16[64,1024]{1,0:T(8,128)(2,1)} %param.16) | copy-start | bytes 393220
  14.7 0.7 copy-start.10
  15.9 12.9 %all-to-all-start.3 = ((bf16[8,2,2048]{2,1,0:T(2,128)(2,1)}), bf16[8,2,2048]{2,1,0:T(2,128)(2,1)S(1)}, u32[]{:S(2)}, u32[]{:S(2)}) async-start(bf16[8,2,2048]{2,1,0:T(2,128)(2,1)} %reshape.665), calls=%async_computation.3 | async-start | bytes 131072 | tf_op jit(solution)/shard_map/all_to_all | solution.py:84
  29.5 11.6 %all-to-all-start.1 = ((bf16[64,8,1,256]{3,0,2,1:T(8,128)(2,1)}), bf16[64,8,1,256]{3,0,2,1:T(8,128)(2,1)S(1)}, u32[]{:S(2)}, u32[]{:S(2)}) async-start(bf16[64,8,1,256]{3,0,2,1:T(8,128)(2,1)} %bitcast.12), calls=%async_computation.1 | async-start | bytes 524288 | tf_op jit(solution)/shard_map/all_to_all | solution.py:85
  41.8 11.6 %all-to-all-start = ((bf16[64,8,1,256]{3,0,2,1:T(8,128)(2,1)}), bf16[64,8,1,256]{3,0,2,1:T(8,128)(2,1)S(1)}, u32[]{:S(2)}, u32[]{:S(2)}) async-start(bf16[64,8,1,256]{3,0,2,1:T(8,128)(2,1)} %bitcast.1), calls=%async_computation | async-start | bytes 524288 | tf_op jit(solution)/shard_map/all_to_all | solution.py:86
  67.0 0.8 %copy-start = (bf16[64,512]{1,0:T(8,128)(2,1)S(1)}, bf16[64,512]{1,0:T(8,128)(2,1)}, u32[]{:S(2)}) copy-start(bf16[64,512]{1,0:T(8,128)(2,1)} %param.17) | copy-start | bytes 196612
  68.1 0.7 copy-start.7
where the time goes:
time: 70.2 us; the launch traced here: 69.4 us
  starting transfers between devices  20.1 us (29%)
  waiting for transfers between devices  16.9 us (24%)
  local copies, waits for them, and re-layouts  14.7 us (21%)
  blocking collectives  9.55 us (14%)
  other arithmetic  6.17 us (9%)
  between operations  1.08 us (2%)
  matrix products  0.91 us (1%)
    all_to_all x1, blocking collectives, body(): lax.all_to_all(heads_out.reshape(length, 1, per_device, HEAD_DIM), 'seq',...  9.55 us
    all_to_all x1, waiting for transfers between devices, body(): lax.all_to_all(outgoing[1], 'seq', split_axis=1, concat_axis=0, tiled=True)  7.46 us
    all_to_all x1, starting transfers between devices, body(): lax.all_to_all(outgoing[3], 'seq', split_axis=1, concat_axis=0, tiled=True)  7.28 us
    unnamed x28, local copies, waits for them, and re-layouts  6.26 us
    all_to_all x1, starting transfers between devices, body(): lax.all_to_all(outgoing[0], 'seq', split_axis=1, concat_axis=0, tiled=True)  6 us
    all_to_all x1, waiting for transfers between devices, body(): lax.all_to_all(outgoing[0], 'seq', split_axis=1, concat_axis=0, tiled=True)  4.77 us
    all_to_all x1, waiting for transfers between devices, body(): lax.all_to_all(outgoing[2], 'seq', split_axis=1, concat_axis=0, tiled=True)  4.64 us
    all_to_all x1, starting transfers between devices, body(): lax.all_to_all(outgoing[1], 'seq', split_axis=1, concat_axis=0, tiled=True)  3.41 us
  transfers between devices with their start and end apart: 4, of which 3 were waited for; matrix products, arithmetic and copies ran while one was open for 13% of the time, Pallas kernels for 0%

commit v1 on v0

v1 whole, which is shorter than its diff:
```python
import functools

import jax
import jax.numpy as jnp
from jax import lax
from jax.experimental import pallas as pl
from jax.experimental.pallas import tpu as pltpu
from jax.sharding import PartitionSpec as P

HEAD_DIM = 64
STATE = 256
BLOCK = 256
LANES = 128
HALO = 8
EDGE = 16
F32 = jnp.float32
BF16 = jnp.bfloat16
VMEM = pl.BlockSpec(memory_space=pltpu.VMEM)
SMEM = pl.BlockSpec(memory_space=pltpu.SMEM)
NT = (((1,), (1,)), ((), ()))
TN = (((0,), (0,)), ((), ()))
NN = (((1,), (0,)), ((), ()))


def dot(a, b, dims):
    return lax.dot_general(a, b, dims, preferred_element_type=F32)


class Sizes:
    def __init__(self, x_in, b_in, dt_raw, seq_total, taps):
        self.rows = x_in.shape[0]
        self.heads = dt_raw.shape[1]
        self.groups = b_in.shape[1] // STATE
        self.per_group = self.heads // self.groups
        self.places = BLOCK // self.rows
        self.blocks = seq_total // self.places
        self.taps = taps
        self.x_blocks = self.per_group * HEAD_DIM // LANES
        self.s_blocks = STATE // LANES
        self.cols = self.x_blocks + 2 * self.s_blocks
        self.message = self.rows * self.cols + self.heads
        self.pad_heads = max(8, self.per_group)
        if self.places != self.groups or self.rows * 2 != LANES or self.places != 4:
            raise ValueError("unsupported shapes")


def lane(start):
    return pl.ds(pl.multiple_of(start, LANES), LANES)


def place_of(sz):
    return lax.rem(lax.axis_index("seq"), sz.places)


def silu_half(half):
    return half + half * jnp.tanh(half)


def column_block(sz, group, t):
    if t < sz.x_blocks:
        return 0, (group * sz.x_blocks + t) * LANES
    t -= sz.x_blocks
    which, t = (1, t) if t < sz.s_blocks else (2, t - sz.s_blocks)
    return which, (group * sz.s_blocks + t) * LANES


def pack_kernel(sz, x, b, c, dt, m1, m2, m3, dt_own):
    place = place_of(sz)
    rows = sz.rows
    line = lax.broadcasted_iota(jnp.int32, (rows, LANES), 0)
    spot = lax.broadcasted_iota(jnp.int32, (rows, LANES), 1)
    turned = jnp.where(spot == line + rows * lax.rem(place, 2), 1.0, 0.0).astype(BF16)
    dt_rows = dot(dt[...], turned, TN).astype(BF16)
    dt_own[...] = dt_rows
    for k, m in ((3, m3), (2, m2), (1, m1)):
        group = lax.bitwise_xor(place, k)
        for t in range(sz.cols):
            which, start = column_block(sz, group, t)
            m[t * rows : (t + 1) * rows, :] = (x, b, c)[which][:, lane(start)]
        m[rows * sz.cols :, :] = dt_rows


def conv_block(buffer, at, count, taps, t):
    n = len(taps)
    first = HALO - (n - 1) + at
    cols = slice(t * LANES, (t + 1) * LANES)
    total = taps[0] * buffer[first : first + count, cols]
    for i in range(1, n):
        total = total + taps[i] * buffer[first + i : first + i + count, cols]
    return total


def halved_taps(ref, start, n):
    return [0.5 * ref[i : i + 1, lane(start)].astype(F32) for i in range(n)]


def gather(sz, buffer, place, base, count, own, messages):
    for k in range(sz.places):
        source = lax.bitwise_xor(place, k)
        at = pl.ds(pl.multiple_of(HALO + source * sz.rows, 8), sz.rows)
        for t in range(count):
            if k == 0:
                _, start = column_block(sz, place, base + t)
                part = own[:, lane(start)]
            else:
                row = (base + t) * sz.rows
                part = messages[k - 1][row : row + sz.rows, :]
            buffer[at, t * LANES : (t + 1) * LANES] = part.astype(F32)


def state_kernel(sz, bias, alog, x, b, c, dt_own, m1, m2, m3, conv_x, conv_b, halo,
                 msg, xc, bc, stats, first, xs, bs, dts, ends):
    chain = sz.blocks > 2
    place = place_of(sz)
    rows, messages = sz.rows, (m1, m2, m3)
    near = dt_own[...].astype(F32) + m1[rows * sz.cols :, :].astype(F32)
    far = m2[rows * sz.cols :, :].astype(F32) + m3[rows * sz.cols :, :].astype(F32)
    side = lax.div(place, 2)
    dts[:, lane(side * LANES)] = near
    dts[:, lane((1 - side) * LANES)] = far
    head0 = place * sz.per_group
    raw = pltpu.roll(dts[...], lax.rem(sz.heads - head0, sz.heads), 0)[0 : sz.pad_heads]
    shape = (sz.pad_heads, BLOCK)
    which = lax.broadcasted_iota(jnp.int32, shape, 0)
    shift = jnp.zeros(shape, F32)
    rate_log = jnp.zeros(shape, F32)
    for h in range(sz.per_group):
        shift = jnp.where(which == h, bias[head0 + h], shift)
        rate_log = jnp.where(which == h, alog[head0 + h], rate_log)
    raw = raw + shift
    rates = jnp.maximum(raw, 0.0) + jnp.log1p(jnp.exp(-jnp.abs(raw)))
    decays = -jnp.exp(rate_log) * rates
    high = decays.astype(BF16).astype(F32)
    middle = (decays - high).astype(BF16).astype(F32)
    low = decays - high - middle
    parts = jnp.concatenate([high, middle, low], axis=0).astype(BF16)
    line = lax.broadcasted_iota(jnp.int32, (BLOCK, BLOCK), 0)
    spot = lax.broadcasted_iota(jnp.int32, (BLOCK, BLOCK), 1)
    upto = jnp.where(line <= spot, 1.0, 0.0).astype(BF16)
    sums = dot(parts, upto, NN)
    n = sz.pad_heads
    log_decay = sums[0:n] + sums[n : 2 * n] + sums[2 * n : 3 * n]
    weight = jnp.exp(log_decay[:, BLOCK - 1 : BLOCK] - log_decay) * rates
    g = sz.per_group
    stats[0:g, :] = log_decay[0:g]
    stats[g : 2 * g, :] = rates[0:g]
    stats[2 * g : 3 * g, :] = jnp.exp(log_decay)[0:g]
    stats[3 * g : 4 * g, :] = weight[0:g]
    gather(sz, xs, place, 0, sz.x_blocks, x, messages)
    gather(sz, bs, place, sz.x_blocks, sz.s_blocks, b, messages)
    for t in range(sz.x_blocks + sz.s_blocks):
        buffer, u = (xs, t) if t < sz.x_blocks else (bs, t - sz.x_blocks)
        cols = slice(u * LANES, (u + 1) * LANES)
        if chain:
            buffer[0:HALO, cols] = halo[t * HALO : (t + 1) * HALO, :]
        else:
            buffer[0:HALO, cols] = jnp.zeros((HALO, LANES), F32)
    for t in range(sz.s_blocks):
        _, start = column_block(sz, place, sz.x_blocks + t)
        taps = halved_taps(conv_b, start, sz.taps)
        cols = slice(t * LANES, (t + 1) * LANES)
        bc[:, cols] = silu_half(conv_block(bs, 0, BLOCK, taps, t)).astype(BF16)
    states = []
    for t in range(sz.x_blocks):
        _, start = column_block(sz, place, t)
        taps = halved_taps(conv_x, start, sz.taps)
        cols = slice(t * LANES, (t + 1) * LANES)
        value = silu_half(conv_block(xs, 0, BLOCK, taps, t)).astype(BF16)
        xc[:, cols] = value
        turned = jnp.transpose(value.astype(F32))
        up = turned[0:HEAD_DIM] * weight[2 * t : 2 * t + 1]
        down = turned[HEAD_DIM:LANES] * weight[2 * t + 1 : 2 * t + 2]
        weighted = jnp.concatenate([up, down], axis=0).astype(BF16)
        states.append(dot(weighted, bc[...], NN))
    for t in range(sz.x_blocks):
        for s in range(sz.s_blocks):
            row = (t * sz.s_blocks + s) * LANES
            part = states[t][:, s * LANES : (s + 1) * LANES]
            msg[row : row + LANES, :] = part.astype(msg.dtype)
    base = sz.x_blocks * STATE
    for t in range(sz.cols):
        if t < sz.x_blocks + sz.s_blocks:
            buffer, u = (xs, t) if t < sz.x_blocks else (bs, t - sz.x_blocks)
            cols = slice(u * LANES, (u + 1) * LANES)
            head, tail = buffer[HALO : 2 * HALO, cols], buffer[BLOCK : BLOCK + HALO, cols]
        else:
            _, start = column_block(sz, place, t)
            own = c[:, lane(start)].astype(F32)
            for k in range(sz.places):
                source = lax.bitwise_xor(place, k)
                row = t * rows
                part = own if k == 0 else messages[k - 1][row : row + rows, :].astype(F32)
                at = pl.multiple_of(source * 2 * HALO, 8)
                ends[pl.ds(at, HALO), :] = part[0:HALO]
                ends[pl.ds(at + HALO, HALO), :] = part[rows - HALO :]
            head = ends[0:HALO, :]
            tail = ends[sz.places * 2 * HALO - HALO :, :]
        first[t * HALO : (t + 1) * HALO, :] = head
        msg[base + t * HALO : base + (t + 1) * HALO, :] = tail.astype(msg.dtype)


def inner_kernel(sz, c, m1, m2, m3, conv_c, xc, bc, stats, halo, inner, cc, columns, cs):
    chain = sz.blocks > 2
    place = place_of(sz)
    base = sz.x_blocks + sz.s_blocks
    g = sz.per_group
    columns[...] = jnp.transpose(stats[...])
    gather(sz, cs, place, base, sz.s_blocks, c, (m1, m2, m3))
    for t in range(sz.s_blocks):
        cols = slice(t * LANES, (t + 1) * LANES)
        if chain:
            cs[0:HALO, cols] = halo[(base + t) * HALO : (base + t + 1) * HALO, :]
        else:
            cs[0:HALO, cols] = jnp.zeros((HALO, LANES), F32)
        _, start = column_block(sz, place, base + t)
        taps = halved_taps(conv_c, start, sz.taps)
        cc[:, cols] = silu_half(conv_block(cs, 0, BLOCK, taps, t)).astype(BF16)
    half = BLOCK // 2
    skip = 0 if chain else EDGE
    for r in range(2):
        width = half * (r + 1)
        at = slice(r * half, (r + 1) * half)
        scores = dot(cc[at, :], bc[0:width, :], NT)
        line = lax.broadcasted_iota(jnp.int32, (half, width), 0) + r * half
        spot = lax.broadcasted_iota(jnp.int32, (half, width), 1)
        keep = (spot <= line) & (spot >= skip)
        low_lanes = lax.broadcasted_iota(jnp.int32, (half, LANES), 1) < HEAD_DIM
        for t in range(sz.x_blocks):
            cols = slice(t * LANES, (t + 1) * LANES)
            sums = []
            for h in (2 * t, 2 * t + 1):
                spread = columns[at, h : h + 1] - stats[h : h + 1, 0:width]
                rate = stats[g + h : g + h + 1, 0:width]
                mixing = scores * jnp.exp(jnp.where(keep, spread, -1e30)) * rate
                sums.append(dot(mixing.astype(BF16), xc[0:width, cols], NN))
            inner[at, cols] = jnp.where(low_lanes, sums[0], sums[1])


def outer_kernel(sz, skip, conv_x, conv_b, conv_c, xc, bc, cc, stats, columns, first, inner, arrived,
                 o0, o1, o2, o3, edge, x_all, c_all, total):
    chain = sz.blocks > 2
    place = place_of(sz)
    later = lax.axis_index("seq") >= sz.places
    g, rows = sz.per_group, sz.rows
    head0 = place * g
    low_lanes = lax.broadcasted_iota(jnp.int32, (BLOCK, LANES), 1) < HEAD_DIM
    if chain:
        x_all[...] = xc[...]
        c_all[...] = cc[...]
    else:
        base = sz.x_blocks * STATE
        renewed = []
        for t in range(sz.cols):
            ahead = arrived[base + t * HALO : base + (t + 1) * HALO, :].astype(F32)
            edge[0:HALO, :] = jnp.where(later, ahead, 0.0)
            edge[HALO : 2 * HALO, :] = first[t * HALO : (t + 1) * HALO, :]
            which, start = column_block(sz, place, t)
            taps = halved_taps((conv_x, conv_b, conv_c)[which], start, sz.taps)
            fresh = silu_half(conv_block(edge, 0, HALO, taps, 0))
            u = t - (0, sz.x_blocks, sz.x_blocks + sz.s_blocks)[which]
            old = (xc, bc, cc)[which][0:EDGE, u * LANES : (u + 1) * LANES].astype(F32)
            renewed.append(jnp.concatenate([fresh, old[HALO:EDGE]], axis=0).astype(BF16))
        for t in range(sz.x_blocks):
            cols = slice(t * LANES, (t + 1) * LANES)
            x_all[EDGE:, cols] = xc[EDGE:, cols]
            x_all[0:EDGE, cols] = renewed[t]
        for t in range(sz.s_blocks):
            cols = slice(t * LANES, (t + 1) * LANES)
            c_all[EDGE:, cols] = cc[EDGE:, cols]
            c_all[0:EDGE, cols] = renewed[sz.x_blocks + sz.s_blocks + t]
        b_edge = jnp.concatenate(renewed[sz.x_blocks : sz.x_blocks + sz.s_blocks], axis=1)
        edge_scores = dot(b_edge, c_all[...], NT)
        line = lax.broadcasted_iota(jnp.int32, (EDGE, BLOCK), 0)
        spot = lax.broadcasted_iota(jnp.int32, (EDGE, BLOCK), 1)
        keep = spot >= line
    for t in range(sz.x_blocks):
        cols = slice(t * LANES, (t + 1) * LANES)
        state = jnp.concatenate(
            [arrived[(t * sz.s_blocks + s) * LANES : (t * sz.s_blocks + s + 1) * LANES, :] for s in range(sz.s_blocks)],
            axis=1,
        )
        state = jnp.where(later, state.astype(F32), 0.0).astype(BF16)
        outer = dot(c_all[...], state, NT)
        growth = jnp.where(
            low_lanes,
            columns[:, 2 * g + 2 * t : 2 * g + 2 * t + 1],
            columns[:, 2 * g + 2 * t + 1 : 2 * g + 2 * t + 2],
        )
        gain = jnp.where(low_lanes, skip[head0 + 2 * t], skip[head0 + 2 * t + 1])
        out = inner[:, cols] + outer * growth + gain * x_all[:, cols].astype(F32)
        if not chain:
            mixed, values = [], []
            edge_low = lax.broadcasted_iota(jnp.int32, (EDGE, LANES), 1) < HEAD_DIM
            x_edge = renewed[t].astype(F32)
            for h in (2 * t, 2 * t + 1):
                spread = stats[h : h + 1, :] - columns[0:EDGE, h : h + 1]
                rate = columns[0:EDGE, g + h : g + h + 1]
                mixed.append(edge_scores * jnp.exp(jnp.where(keep, spread, -1e30)) * rate)
                mine = edge_low if h == 2 * t else jnp.logical_not(edge_low)
                values.append(jnp.where(mine, x_edge, 0.0))
            mixed = jnp.concatenate(mixed, axis=0).astype(BF16)
            values = jnp.concatenate(values, axis=0).astype(BF16)
            out = out + dot(mixed, values, TN)
        total[:, cols] = out
    for k, o in enumerate((o0, o1, o2, o3)):
        target = lax.bitwise_xor(place, k)
        o[...] = total[pl.ds(pl.multiple_of(target * rows, 8), rows), :].astype(BF16)


def norm_kernel(sz, o0, r1, r2, r3, z, gain, out):
    place = place_of(sz)
    width = sz.x_blocks * LANES
    for k, part in enumerate((o0, r1, r2, r3)):
        group = lax.bitwise_xor(place, k)
        at = pl.ds(pl.multiple_of(group * width, LANES), width)
        gate = 0.5 * z[:, at].astype(F32)
        value = part[...].astype(F32) * silu_half(gate)
        mean = jnp.sum(value * value, axis=-1, keepdims=True) * (1.0 / width)
        out[:, at] = (value * lax.rsqrt(mean + 1e-05) * gain[0:1, at]).astype(BF16)


def call(kernel, sz, outs, scratch, specs, name, flops=0, touched=0):
    return pl.pallas_call(
        functools.partial(kernel, sz),
        out_shape=[jax.ShapeDtypeStruct(s, d) for s, d in outs],
        in_specs=specs,
        out_specs=[VMEM] * len(outs),
        scratch_shapes=[pltpu.VMEM(s, d) for s, d in scratch],
        compiler_params=pltpu.CompilerParams(vmem_limit_bytes=24 << 20),
        cost_estimate=pl.CostEstimate(flops=flops, bytes_accessed=touched, transcendentals=0),
        name=name,
    )


def body(x_in, b_in, c_in, z_in, dt_raw, dt_bias, a_log, d_skip, conv_x, conv_b, conv_c, norm_gain):
    seq_total = lax.axis_size("seq")
    sz = Sizes(x_in, b_in, dt_raw, seq_total, conv_x.shape[0])
    n, rows = sz.places, sz.rows
    chain = sz.blocks > 2

    def swap(k):
        return [(i, i - i % n + ((i % n) ^ k)) for i in range(seq_total)]

    def onward(k, wrap):
        pairs = [(i, i + n * k) for i in range(seq_total)]
        return [(i, j % seq_total) for i, j in pairs if wrap or j < seq_total]

    message = ((sz.message, LANES), BF16)
    sent = call(pack_kernel, sz, [message] * 3 + [((sz.heads, LANES), BF16)], [], [VMEM] * 4, "pack")(
        x_in, b_in, c_in, dt_raw
    )
    dt_own = sent[3]
    came = [None] * 3
    for k in (3, 2, 1):
        came[k - 1] = lax.ppermute(sent[k - 1], "seq", swap(k))

    width = sz.x_blocks * LANES
    padded = BLOCK + HALO
    edge_rows = sz.cols * HALO
    if chain:
        own = []
        place = lax.rem(lax.axis_index("seq"), n)
        for t in range(sz.cols):
            which, start = column_block(sz, place, t)
            own.append(lax.dynamic_slice_in_dim((x_in, b_in, c_in)[which], start, LANES, 1)[rows - HALO :])
        tails = [jnp.concatenate(own, axis=0)]
        for k in range(1, n):
            tails.append(
                came[k - 1][: sz.cols * rows].reshape(sz.cols, rows, LANES)[:, rows - HALO :].reshape(-1, LANES)
            )
        tail = lax.dynamic_index_in_dim(
            jnp.stack(tails), lax.bitwise_xor(place, n - 1), 0, keepdims=False
        )
        halo = lax.ppermute(tail, "seq", onward(1, False)).astype(F32)
    else:
        halo = jnp.zeros((8, LANES), F32)

    stat_rows = 4 * sz.per_group
    msg, xc, bc, stats, first = call(
        state_kernel,
        sz,
        [
            ((sz.x_blocks * STATE + edge_rows, LANES), F32 if chain else BF16),
            ((BLOCK, width), BF16),
            ((BLOCK, STATE), BF16),
            ((stat_rows, BLOCK), F32),
            ((edge_rows, LANES), F32),
        ],
        [
            ((padded, width), F32),
            ((padded, STATE), F32),
            ((sz.heads, BLOCK), F32),
            ((n * 2 * HALO, LANES), F32),
        ],
        [SMEM] * 2 + [VMEM] * 10,
        "state",
    )(dt_bias, a_log, x_in, b_in, c_in, dt_own, *came, conv_x, conv_b, halo)

    if chain:
        cut = sz.x_blocks * STATE
        grown = msg[:cut].reshape(sz.x_blocks, sz.s_blocks, 2, HEAD_DIM, LANES)
        fade = jnp.exp(stats[: sz.per_group, BLOCK - 1]).reshape(sz.x_blocks, 1, 2, 1, 1)
        k = 1
        while k < sz.blocks:
            grown = grown + fade * lax.ppermute(grown, "seq", onward(k, False))
            fade = fade * lax.ppermute(fade, "seq", onward(k, False))
            k *= 2
        msg = jnp.concatenate([grown.reshape(cut, LANES), msg[cut:]], axis=0).astype(BF16)
    arrived = lax.ppermute(msg, "seq", onward(1, True))

    inner, cc, columns = call(
        inner_kernel,
        sz,
        [((BLOCK, width), F32), ((BLOCK, STATE), BF16), ((BLOCK, stat_rows), F32)],
        [((padded, STATE), F32)],
        [VMEM] * 9,
        "inner",
        flops=1 << 30,
        touched=1 << 22,
    )(c_in, *came, conv_c, xc, bc, stats, halo)

    piece = ((rows, width), BF16)
    back = call(
        outer_kernel,
        sz,
        [piece] * 4,
        [
            ((2 * HALO, LANES), F32),
            ((BLOCK, width), BF16),
            ((BLOCK, STATE), BF16),
            ((BLOCK, width), F32),
        ],
        [SMEM] + [VMEM] * 11,
        "outer",
    )(d_skip, conv_x, conv_b, conv_c, xc, bc, cc, stats, columns, first, inner, arrived)
    home = [None] * 3
    for k in (3, 2, 1):
        home[k - 1] = lax.ppermute(back[k], "seq", swap(k))

    out = call(norm_kernel, sz, [(x_in.shape, BF16)], [], [VMEM] * 6, "norm")(
        back[0], *home, z_in, norm_gain.reshape(1, -1)
    )
    return out[0]


def solution(mesh):
    rows, wide = P(("rep", "seq"), "head"), P(None, "head")
    placed = (rows,) * 5 + (P("head"),) * 3 + (wide,) * 3 + (P("head"),)
    return jax.shard_map(body, mesh=mesh, in_specs=placed, out_specs=rows, check_vma=False)
```

time: 70.2 us -> 29.4 us (0.42)
  local copies, waits for them, and re-layouts: 14.7 us -> 4.11 us
  blocking collectives: 9.55 us -> 0 us
  starting transfers between devices: 20.1 us -> 10.8 us
  waiting for transfers between devices: 16.9 us -> 10.5 us
  other arithmetic: 6.17 us -> 0 us
  Pallas kernels: 0 us -> 3.7 us
  between operations: 1.08 us -> 0.07 us
  matrix products: 0.91 us -> 0 us
    all_to_all x4 -> x0, starting transfers between devices: 20.1 us -> none  [the longest x1 7.28 us: body(): lax.all_to_all(outgoing[3], 'seq', split_axis=1, concat_axis=0, tiled=True)]
    all_to_all x4 -> x0, waiting for transfers between devices: 16.9 us -> none  [the longest x1 7.46 us: body(): lax.all_to_all(outgoing[1], 'seq', split_axis=1, concat_axis=0, tiled=True)]
    ppermute x0 -> x7, starting transfers between devices: none -> 10.8 us  [the longest x3 4.55 us: body(): came[k - 1] = lax.ppermute(sent[k - 1], 'seq', swap(k))]
    ppermute x0 -> x7, waiting for transfers between devices: none -> 10.5 us  [the longest x3 5.36 us: body(): came[k - 1] = lax.ppermute(sent[k - 1], 'seq', swap(k))]
    all_to_all x1 -> x0, blocking collectives: 9.55 us -> none  [body(): lax.all_to_all(heads_out.reshape(length, 1, per_device, HEAD_DIM), 'seq',...]
    pallas_call x0 -> x5, Pallas kernels: none -> 3.7 us  [the longest x1 1.14 us: body(): call(state_kernel, sz, [((sz.x_blocks * STATE + edge_rows, LANES), F32 if...]
    reshape x7 -> x0, local copies, waits for them, and re-layouts: 2.15 us -> none  [the longest x1 1.28 us: body(): dt_raw.reshape(local_rows, seq_total, per_device)]
    unnamed x28 -> x25, local copies, waits for them, and re-layouts: 6.26 us -> 4.11 us
  transfers between devices with their start and end apart: 4 -> 7, of which waited for: 3 -> 7; matrix products, arithmetic and copies ran while one was open for 13% -> 0% of each run, Pallas kernels for 0% -> 2%
where the time goes in v1:
time: 29.4 us; the launch traced here: 29.2 us
  starting transfers between devices  10.8 us (37%)
  waiting for transfers between devices  10.5 us (36%)
  local copies, waits for them, and re-layouts  4.11 us (14%)
  Pallas kernels  3.7 us (13%)
    ppermute x3, waiting for transfers between devices, body(): came[k - 1] = lax.ppermute(sent[k - 1], 'seq', swap(k))  5.36 us
    ppermute x3, starting transfers between devices, body(): came[k - 1] = lax.ppermute(sent[k - 1], 'seq', swap(k))  4.55 us
    unnamed x25, local copies, waits for them, and re-layouts  4.11 us
    ppermute x3, starting transfers between devices, body(): home[k - 1] = lax.ppermute(back[k], 'seq', swap(k))  3.55 us
    ppermute x1, waiting for transfers between devices, body(): arrived = lax.ppermute(msg, 'seq', onward(1, True))  2.86 us
    ppermute x1, starting transfers between devices, body(): arrived = lax.ppermute(msg, 'seq', onward(1, True))  2.66 us
    ppermute x3, waiting for transfers between devices, body(): home[k - 1] = lax.ppermute(back[k], 'seq', swap(k))  2.29 us
    pallas_call x1, Pallas kernels, body(): call(state_kernel, sz, [((sz.x_blocks * STATE + edge_rows, LANES), F32 if...  1.14 us
  transfers between devices with their start and end apart: 7, of which 7 were waited for; matrix products, arithmetic and copies ran while one was open for 0% of the time, Pallas kernels for 2%

profile of v1, /device:TPU:0, one launch (start us, length us, event | category | flops | bytes accessed | tf_op | source)
XLA Modules:
  0.0 29.2 jit_solution(12341586161140513019)
XLA Ops:
  0.0 0.8 %copy.13.dt = bf16[64,8]{1,0:T(8,128)(2,1)S(1)} copy(bf16[64,8]{0,1:T(8,128)(2,1)} %param.16) | data formatting | bytes 2048 | tf_op args[4]
  0.8 0.9 %copy-done = bf16[64,1024]{1,0:T(8,128)(2,1)S(1)} copy-done((bf16[64,1024]{1,0:T(8,128)(2,1)S(1)}, bf16[64,1024]{1,0:T(8,128)(2,1)}, u32[]{:S(2)}) %copy-start) | copy-done | bytes 131096
  1.7 0.9 %copy-done.1 = bf16[64,1024]{1,0:T(8,128)(2,1)S(1)} copy-done((bf16[64,1024]{1,0:T(8,128)(2,1)S(1)}, bf16[64,1024]{1,0:T(8,128)(2,1)}, u32[]{:S(2)}) %copy-start.1) | copy-done | bytes 131096
  2.6 0.8 %copy-done.3 = bf16[64,512]{1,0:T(8,128)(2,1)S(1)} copy-done((bf16[64,512]{1,0:T(8,128)(2,1)S(1)}, bf16[64,512]{1,0:T(8,128)(2,1)}, u32[]{:S(2)}) %copy-start.3) | copy-done | bytes 65560
  3.4 0.2 pack.1
  3.6 3.0 %collective-permute-start = (bf16[328,128]{1,0:T(8,128)(2,1)S(1)}, bf16[328,128]{1,0:T(8,128)(2,1)S(1)}, u32[]{:S(2)}, u32[]{:S(2)}) collective-permute-start(bf16[328,128]{1,0:T(8,128)(2,1)S(1)} %get-tuple-element.22), channel_id=1, source_target_pairs={{0,2},{2,0},{4,6},{6,4},{8,10},{10,8},{12,14},{14,12},{1,3},{3,1},... | collective-permute-start | bytes 251912 | tf_op jit(solution)/shard_map/ppermute | solution.py:355
  6.6 1.6 %collective-permute-start.1 = (bf16[328,128]{1,0:T(8,128)(2,1)S(1)}, bf16[328,128]{1,0:T(8,128)(2,1)S(1)}, u32[]{:S(2)}, u32[]{:S(2)}) collective-permute-start(bf16[328,128]{1,0:T(8,128)(2,1)S(1)} %get-tuple-element.23), channel_id=1, source_target_pairs={{0,4},{2,6},{4,0},{6,2},{8,12},{10,14},{12,8},{14,10},{1,5},{3,7},... | collective-permute-start | bytes 251912 | tf_op jit(solution)/shard_map/ppermute | solution.py:355
  8.2 0.0 collective-permute-start.2
  8.2 0.9 %collective-permute-done.m1 = bf16[328,128]{1,0:T(8,128)(2,1)S(1)} collective-permute-done((bf16[328,128]{1,0:T(8,128)(2,1)S(1)}, bf16[328,128]{1,0:T(8,128)(2,1)S(1)}, u32[]{:S(2)}, u32[]{:S(2)}) %collective-permute-start) | collective-permute-done | bytes 84000 | tf_op jit(solution)/shard_map/ppermute | solution.py:355
  9.1 2.7 %collective-permute-done.1.m2 = bf16[328,128]{1,0:T(8,128)(2,1)S(1)} collective-permute-done((bf16[328,128]{1,0:T(8,128)(2,1)S(1)}, bf16[328,128]{1,0:T(8,128)(2,1)S(1)}, u32[]{:S(2)}, u32[]{:S(2)}) %collective-permute-start.1) | collective-permute-done | bytes 84000 | tf_op jit(solution)/shard_map/ppermute | solution.py:355
  11.8 1.7 %collective-permute-done.2.m3 = bf16[328,128]{1,0:T(8,128)(2,1)S(1)} collective-permute-done((bf16[328,128]{1,0:T(8,128)(2,1)S(1)}, bf16[328,128]{1,0:T(8,128)(2,1)S(1)}, u32[]{:S(2)}, u32[]{:S(2)}) %collective-permute-start.2) | collective-permute-done | bytes 84000 | tf_op jit(solution)/shard_map/ppermute | solution.py:355
  13.5 0.0 copy-done.9
  13.5 0.0 copy-done.10
  13.5 0.0 copy-done.5
  13.5 0.0 copy-done.6
  13.5 0.0 copy-start.2
  13.5 0.0 copy-start.7
  13.6 1.1 %state.1 = (bf16[296,128]{1,0:T(8,128)(2,1)S(1)}, bf16[256,128]{1,0:T(8,128)(2,1)S(1)}, bf16[256,256]{1,0:T(8,128)(2,1)S(1)}, f32[8,256]{1,0:T(8,128)S(1)}, f32[40,128]{1,0:T(8,128)S(1)}) custom-call(f32[8]{0:T(128)S(1)} %copy-done.9, f32[8]{0:T(128)S(1)} %copy-done.10, bf16[64,512]{1,0:T(8,128)(2,1)S(1)} %copy-done.3, bf16[64,1024]{1,0:T(8,128)(2,1)S(1)} %copy-done, ...), custom_call_target="tpu_custom_call" | custom-call | tf_op jit(solution)/shard_map/state/pallas_call | solution.py:379
  14.7 2.7 %collective-permute-start.3 = (bf16[296,128]{1,0:T(8,128)(2,1)S(1)}, bf16[296,128]{1,0:T(8,128)(2,1)S(1)}, u32[]{:S(2)}, u32[]{:S(2)}) collective-permute-start(bf16[296,128]{1,0:T(8,128)(2,1)S(1)} %get-tuple-element.32), channel_id=1, source_target_pairs={{0,8},{2,10},{4,12},{6,14},{8,0},{10,2},{12,4},{14,6},{1,9},{3,11}... | collective-permute-start | bytes 227336 | tf_op jit(solution)/shard_map/ppermute | solution.py:409
  17.4 0.0 copy-done.2
  17.4 0.0 copy-done.7
  17.4 0.6 %inner.1 = (f32[256,128]{1,0:T(8,128)S(1)}, bf16[256,256]{1,0:T(8,128)(2,1)S(1)}, f32[256,8]{1,0:T(8,128)S(1)}) custom-call(bf16[64,1024]{1,0:T(8,128)(2,1)S(1)} %copy-done.2, bf16[328,128]{1,0:T(8,128)(2,1)S(1)} %collective-permute-done.m1, bf16[328,128]{1,0:T(8,128)(2,1)S(1)} %collective-permute-done.1.m2, bf16[328,128]{1,0:T(8,128)(2,1)S(1)} %collective-permute-done.2.m3, ...), custom_call_target="tpu_custom_call" | custom-call | flops 1073741824 | bytes 4194304 | tf_op jit(solution)/shard_map/inner/pallas_call | solution.py:411
  18.0 2.9 %collective-permute-done.3.arrived = bf16[296,128]{1,0:T(8,128)(2,1)S(1)} collective-permute-done((bf16[296,128]{1,0:T(8,128)(2,1)S(1)}, bf16[296,128]{1,0:T(8,128)(2,1)S(1)}, u32[]{:S(2)}, u32[]{:S(2)}) %collective-permute-start.3) | collective-permute-done | bytes 75808 | tf_op jit(solution)/shard_map/ppermute | solution.py:409
  20.9 0.7 %copy-done.11 = f32[8]{0:T(128)S(1)} copy-done((f32[8]{0:T(128)S(1)}, f32[8]{0:T(128)}, u32[]{:S(2)}) %copy-start.11) | copy-done | bytes 56
  21.5 1.0 %outer.1 = (bf16[64,128]{1,0:T(8,128)(2,1)S(1)}, bf16[64,128]{1,0:T(8,128)(2,1)S(1)}, bf16[64,128]{1,0:T(8,128)(2,1)S(1)}, bf16[64,128]{1,0:T(8,128)(2,1)S(1)}) custom-call(f32[8]{0:T(128)S(1)} %copy-done.11, bf16[4,512]{1,0:T(4,128)(2,1)S(1)} %copy-done.6, bf16[4,1024]{1,0:T(4,128)(2,1)S(1)} %copy-done.5, bf16[4,1024]{1,0:T(4,128)(2,1)S(1)} %copy-done.7, ...), custom_call_target="tpu_custom_call" | custom-call | tf_op jit(solution)/shard_map/outer/pallas_call | solution.py:423
  22.5 0.7 %collective-permute-start.4 = (bf16[64,128]{1,0:T(8,128)(2,1)S(1)}, bf16[64,128]{1,0:T(8,128)(2,1)S(1)}, u32[]{:S(2)}, u32[]{:S(2)}) collective-permute-start(bf16[64,128]{1,0:T(8,128)(2,1)S(1)} %get-tuple-element.34), channel_id=1, source_target_pairs={{0,2},{2,0},{4,6},{6,4},{8,10},{10,8},{12,14},{14,12},{1,3},{3,1},... | collective-permute-start | bytes 49160 | tf_op jit(solution)/shard_map/ppermute | solution.py:438
  23.2 0.5 %collective-permute-start.5 = (bf16[64,128]{1,0:T(8,128)(2,1)S(1)}, bf16[64,128]{1,0:T(8,128)(2,1)S(1)}, u32[]{:S(2)}, u32[]{:S(2)}) collective-permute-start(bf16[64,128]{1,0:T(8,128)(2,1)S(1)} %get-tuple-element.35), channel_id=1, source_target_pairs={{0,4},{2,6},{4,0},{6,2},{8,12},{10,14},{12,8},{14,10},{1,5},{3,7},... | collective-permute-start | bytes 49160 | tf_op jit(solution)/shard_map/ppermute | solution.py:438
  23.7 2.3 %collective-permute-start.6 = (bf16[64,128]{1,0:T(8,128)(2,1)S(1)}, bf16[64,128]{1,0:T(8,128)(2,1)S(1)}, u32[]{:S(2)}, u32[]{:S(2)}) collective-permute-start(bf16[64,128]{1,0:T(8,128)(2,1)S(1)} %get-tuple-element.36), channel_id=1, source_target_pairs={{0,6},{2,4},{4,2},{6,0},{8,14},{10,12},{12,10},{14,8},{1,7},{3,5},... | collective-permute-start | bytes 49160 | tf_op jit(solution)/shard_map/ppermute | solution.py:438
  26.1 0.2 collective-permute-done.4.r1
  26.3 0.6 %collective-permute-done.5.r2 = bf16[64,128]{1,0:T(8,128)(2,1)S(1)} collective-permute-done((bf16[64,128]{1,0:T(8,128)(2,1)S(1)}, bf16[64,128]{1,0:T(8,128)(2,1)S(1)}, u32[]{:S(2)}, u32[]{:S(2)}) %collective-permute-start.5) | collective-permute-done | bytes 16416 | tf_op jit(solution)/shard_map/ppermute | solution.py:438
  27.0 1.4 %collective-permute-done.6.r3 = bf16[64,128]{1,0:T(8,128)(2,1)S(1)} collective-permute-done((bf16[64,128]{1,0:T(8,128)(2,1)S(1)}, bf16[64,128]{1,0:T(8,128)(2,1)S(1)}, u32[]{:S(2)}, u32[]{:S(2)}) %collective-permute-start.6) | collective-permute-done | bytes 16416 | tf_op jit(solution)/shard_map/ppermute | solution.py:438
  28.4 0.8 %norm.1 = bf16[64,512]{1,0:T(8,128)(2,1)} custom-call(bf16[64,128]{1,0:T(8,128)(2,1)S(1)} %get-tuple-element.33.o0, bf16[64,128]{1,0:T(8,128)(2,1)S(1)} %collective-permute-done.4.r1, bf16[64,128]{1,0:T(8,128)(2,1)S(1)} %collective-permute-done.5.r2, bf16[64,128]{1,0:T(8,128)(2,1)S(1)} %collective-permute-done.6.r3, bf16[64,512]{1,0:T(8,128)(2,1)S(1)} %copy-done.4, ...), custom_call_target="tpu_custom_call" | custom-call | tf_op jit(solution)/shard_map/norm/pallas_call | solution.py:440
  (13 shorter events, 0.0 us)
Async XLA Ops:
  0.8 0.9 %copy-start = (bf16[64,1024]{1,0:T(8,128)(2,1)S(1)}, bf16[64,1024]{1,0:T(8,128)(2,1)}, u32[]{:S(2)}) copy-start(bf16[64,1024]{1,0:T(8,128)(2,1)} %b.3) | copy-start | bytes 393220
  1.7 0.9 %copy-start.1 = (bf16[64,1024]{1,0:T(8,128)(2,1)S(1)}, bf16[64,1024]{1,0:T(8,128)(2,1)}, u32[]{:S(2)}) copy-start(bf16[64,1024]{1,0:T(8,128)(2,1)} %c.5) | copy-start | bytes 393220
  2.6 0.8 %copy-start.3 = (bf16[64,512]{1,0:T(8,128)(2,1)S(1)}, bf16[64,512]{1,0:T(8,128)(2,1)}, u32[]{:S(2)}) copy-start(bf16[64,512]{1,0:T(8,128)(2,1)} %x.3) | copy-start | bytes 196612
  3.4 10.1 %copy-start.9 = (f32[8]{0:T(128)S(1)}, f32[8]{0:T(128)}, u32[]{:S(2)}) copy-start(f32[8]{0:T(128)} %bias.1) | copy-start | bytes 100
  3.4 10.1 %copy-start.10 = (f32[8]{0:T(128)S(1)}, f32[8]{0:T(128)}, u32[]{:S(2)}) copy-start(f32[8]{0:T(128)} %alog.1) | copy-start | bytes 100
  3.6 9.9 %copy-start.5 = (bf16[4,1024]{1,0:T(4,128)(2,1)S(1)}, bf16[4,1024]{1,0:T(4,128)(2,1)}, u32[]{:S(2)}) copy-start(bf16[4,1024]{1,0:T(4,128)(2,1)} %conv_b.3) | copy-start | bytes 24580
  3.6 5.5 %collective-permute-start = (bf16[328,128]{1,0:T(8,128)(2,1)S(1)}, bf16[328,128]{1,0:T(8,128)(2,1)S(1)}, u32[]{:S(2)}, u32[]{:S(2)}) collective-permute-start(bf16[328,128]{1,0:T(8,128)(2,1)S(1)} %get-tuple-element.22), channel_id=1, source_target_pairs={{0,2},{2,0},{4,6},{6,4},{8,10},{10,8},{12,14},{14,12},{1,3},{3,1},... | collective-permute-start | bytes 251912 | tf_op jit(solution)/shard_map/ppermute | solution.py:355
  6.6 7.0 %copy-start.6 = (bf16[4,512]{1,0:T(4,128)(2,1)S(1)}, bf16[4,512]{1,0:T(4,128)(2,1)}, u32[]{:S(2)}) copy-start(bf16[4,512]{1,0:T(4,128)(2,1)} %conv_x.3) | copy-start | bytes 12292
  6.6 5.2 %collective-permute-start.1 = (bf16[328,128]{1,0:T(8,128)(2,1)S(1)}, bf16[328,128]{1,0:T(8,128)(2,1)S(1)}, u32[]{:S(2)}, u32[]{:S(2)}) collective-permute-start(bf16[328,128]{1,0:T(8,128)(2,1)S(1)} %get-tuple-element.23), channel_id=1, source_target_pairs={{0,4},{2,6},{4,0},{6,2},{8,12},{10,14},{12,8},{14,10},{1,5},{3,7},... | collective-permute-start | bytes 251912 | tf_op jit(solution)/shard_map/ppermute | solution.py:355
  8.2 5.4 %collective-permute-start.2 = (bf16[328,128]{1,0:T(8,128)(2,1)S(1)}, bf16[328,128]{1,0:T(8,128)(2,1)S(1)}, u32[]{:S(2)}, u32[]{:S(2)}) collective-permute-start(bf16[328,128]{1,0:T(8,128)(2,1)S(1)} %get-tuple-element.24), channel_id=1, source_target_pairs={{0,6},{2,4},{4,2},{6,0},{8,14},{10,12},{12,10},{14,8},{1,7},{3,5},... | collective-permute-start | bytes 251912 | tf_op jit(solution)/shard_map/ppermute | solution.py:355
  13.5 3.8 %copy-start.2 = (bf16[64,1024]{1,0:T(8,128)(2,1)S(1)}, bf16[64,1024]{1,0:T(8,128)(2,1)}, u32[]{:S(2)}) copy-start(bf16[64,1024]{1,0:T(8,128)(2,1)} %c.5) | copy-start | bytes 393220
  13.5 3.8 %copy-start.7 = (bf16[4,1024]{1,0:T(4,128)(2,1)S(1)}, bf16[4,1024]{1,0:T(4,128)(2,1)}, u32[]{:S(2)}) copy-start(bf16[4,1024]{1,0:T(4,128)(2,1)} %conv_c.3) | copy-start | bytes 24580
  14.7 6.1 %collective-permute-start.3 = (bf16[296,128]{1,0:T(8,128)(2,1)S(1)}, bf16[296,128]{1,0:T(8,128)(2,1)S(1)}, u32[]{:S(2)}, u32[]{:S(2)}) collective-permute-start(bf16[296,128]{1,0:T(8,128)(2,1)S(1)} %get-tuple-element.32), channel_id=1, source_target_pairs={{0,8},{2,10},{4,12},{6,14},{8,0},{10,2},{12,4},{14,6},{1,9},{3,11}... | collective-permute-start | bytes 227336 | tf_op jit(solution)/shard_map/ppermute | solution.py:409
  20.8 0.7 %copy-start.11 = (f32[8]{0:T(128)S(1)}, f32[8]{0:T(128)}, u32[]{:S(2)}) copy-start(f32[8]{0:T(128)} %skip.1) | copy-start | bytes 100
  21.5 6.9 %copy-start.4 = (bf16[64,512]{1,0:T(8,128)(2,1)S(1)}, bf16[64,512]{1,0:T(8,128)(2,1)}, u32[]{:S(2)}) copy-start(bf16[64,512]{1,0:T(8,128)(2,1)} %z.1) | copy-start | bytes 196612
  22.5 3.8 %collective-permute-start.4 = (bf16[64,128]{1,0:T(8,128)(2,1)S(1)}, bf16[64,128]{1,0:T(8,128)(2,1)S(1)}, u32[]{:S(2)}, u32[]{:S(2)}) collective-permute-start(bf16[64,128]{1,0:T(8,128)(2,1)S(1)} %get-tuple-element.34), channel_id=1, source_target_pairs={{0,2},{2,0},{4,6},{6,4},{8,10},{10,8},{12,14},{14,12},{1,3},{3,1},... | collective-permute-start | bytes 49160 | tf_op jit(solution)/shard_map/ppermute | solution.py:438
  23.2 3.7 %collective-permute-start.5 = (bf16[64,128]{1,0:T(8,128)(2,1)S(1)}, bf16[64,128]{1,0:T(8,128)(2,1)S(1)}, u32[]{:S(2)}, u32[]{:S(2)}) collective-permute-start(bf16[64,128]{1,0:T(8,128)(2,1)S(1)} %get-tuple-element.35), channel_id=1, source_target_pairs={{0,4},{2,6},{4,0},{6,2},{8,12},{10,14},{12,8},{14,10},{1,5},{3,7},... | collective-permute-start | bytes 49160 | tf_op jit(solution)/shard_map/ppermute | solution.py:438
  23.7 4.6 %copy-start.8 = (f32[512]{0:T(512)S(1)}, f32[512]{0:T(512)}, u32[]{:S(2)}) copy-start(f32[512]{0:T(512)} %param.23) | copy-start | bytes 6148
  23.7 4.6 %collective-permute-start.6 = (bf16[64,128]{1,0:T(8,128)(2,1)S(1)}, bf16[64,128]{1,0:T(8,128)(2,1)S(1)}, u32[]{:S(2)}, u32[]{:S(2)}) collective-permute-start(bf16[64,128]{1,0:T(8,128)(2,1)S(1)} %get-tuple-element.36), channel_id=1, source_target_pairs={{0,6},{2,4},{4,2},{6,0},{8,14},{10,12},{12,10},{14,8},{1,7},{3,5},... | collective-permute-start | bytes 49160 | tf_op jit(solution)/shard_map/ppermute | solution.py:438

commit v2 on v1

v2 whole, which is shorter than its diff:
```python
import functools

import jax
import jax.numpy as jnp
from jax import lax
from jax.experimental import pallas as pl
from jax.experimental.pallas import tpu as pltpu
from jax.sharding import PartitionSpec as P

HEAD_DIM = 64
STATE = 256
BLOCK = 256
LANES = 128
HALO = 8
EDGE = 16
F32 = jnp.float32
BF16 = jnp.bfloat16
VMEM = pl.BlockSpec(memory_space=pltpu.VMEM)
HBM = pl.BlockSpec(memory_space=pltpu.HBM)
NT = (((1,), (1,)), ((), ()))
TN = (((0,), (0,)), ((), ()))
NN = (((1,), (0,)), ((), ()))


def dot(a, b, dims):
    return lax.dot_general(a, b, dims, preferred_element_type=F32)


class Sizes:
    def __init__(self, x_in, b_in, dt_raw, seq_total, taps):
        self.rows = x_in.shape[0]
        self.heads = dt_raw.shape[1]
        self.groups = b_in.shape[1] // STATE
        self.per_group = self.heads // self.groups
        self.places = BLOCK // self.rows
        self.blocks = seq_total // self.places
        self.taps = taps
        self.x_blocks = self.per_group * HEAD_DIM // LANES
        self.s_blocks = STATE // LANES
        self.base = self.x_blocks + self.s_blocks
        self.cols = self.base + self.s_blocks
        self.tail_at = self.rows * self.base
        self.dt_at = self.tail_at + self.s_blocks * HALO
        self.message = self.dt_at + self.heads
        self.message_c = self.rows * self.s_blocks
        self.pad_heads = max(8, self.per_group)
        self.stat_rows = 4 * self.per_group
        if self.places != self.groups or self.rows * 2 != LANES or self.places != 4:
            raise ValueError("unsupported shapes")


def lane(start):
    return pl.ds(pl.multiple_of(start, LANES), LANES)


def place_of(sz):
    return lax.rem(lax.axis_index("seq"), sz.places)


def silu_half(half):
    return half + half * jnp.tanh(half)


def column_block(sz, group, t):
    if t < sz.x_blocks:
        return 0, (group * sz.x_blocks + t) * LANES
    t -= sz.x_blocks
    which, t = (1, t) if t < sz.s_blocks else (2, t - sz.s_blocks)
    return which, (group * sz.s_blocks + t) * LANES


def pack_kernel(sz, x, b, c, dt, m0, m1, m2, m3, c0, c1, c2, c3, dt_here, sem):
    place = place_of(sz)
    rows = sz.rows
    copies = []

    def fetch(source, target):
        copies.append(pltpu.make_async_copy(source, target, sem.at[len(copies)]))
        copies[-1].start()

    fetch(dt, dt_here)
    for k, m, mc in ((3, m3, c3), (2, m2, c2), (1, m1, c1), (0, m0, c0)):
        group = lax.bitwise_xor(place, k)
        for t in range(sz.cols):
            which, start = column_block(sz, group, t)
            source = (x, b, c)[which].at[:, lane(start)]
            if t < sz.base:
                fetch(source, m.at[t * rows : (t + 1) * rows, :])
            else:
                u = t - sz.base
                fetch(source, mc.at[u * rows : (u + 1) * rows, :])
                at = sz.tail_at + u * HALO
                fetch(c.at[rows - HALO :, lane(start)], m.at[at : at + HALO, :])
    copies[0].wait()
    here = dt_here[...].astype(F32)
    twice = jnp.concatenate([here, here], axis=1)
    spot = lax.broadcasted_iota(jnp.int32, twice.shape, 1)
    mine = lax.div(spot, rows) == lax.rem(place, 2)
    dt_rows = jnp.where(mine, twice, 0.0).astype(BF16)
    for m in (m0, m1, m2, m3):
        m[sz.dt_at :, :] = dt_rows
    for copy in copies[1:]:
        copy.wait()


def conv_block(buffer, count, taps, t):
    n = len(taps)
    first = HALO - (n - 1)
    cols = slice(t * LANES, (t + 1) * LANES)
    total = taps[0] * buffer[first : first + count, cols]
    for i in range(1, n):
        total = total + taps[i] * buffer[first + i : first + i + count, cols]
    return total


def halved_taps(ref, start, n):
    return [0.5 * ref[i : i + 1, lane(start)].astype(F32) for i in range(n)]


def gather(sz, buffer, place, base, count, messages):
    for k, m in enumerate(messages):
        source = lax.bitwise_xor(place, k)
        at = pl.ds(pl.multiple_of(HALO + source * sz.rows, 8), sz.rows)
        for t in range(count):
            row = (base + t) * sz.rows
            buffer[at, t * LANES : (t + 1) * LANES] = m[row : row + sz.rows, :].astype(F32)


def of_heads(sz, ref, head0):
    shape = (sz.pad_heads, sz.heads)
    line = lax.broadcasted_iota(jnp.int32, shape, 0)
    spot = lax.broadcasted_iota(jnp.int32, shape, 1)
    row = jnp.broadcast_to(ref[...], shape)
    return jnp.sum(jnp.where(spot == line + head0, row, 0.0), axis=1, keepdims=True)


def state_kernel(sz, bias, alog, m0, m1, m2, m3, conv_x, conv_b, halo,
                 msg, xc, bc, stats, first, xs, bs, dts, tails):
    chain = sz.blocks > 2
    place = place_of(sz)
    messages = (m0, m1, m2, m3)
    near, far = (
        p[sz.dt_at :, :].astype(F32) + q[sz.dt_at :, :].astype(F32) for p, q in ((m0, m1), (m2, m3))
    )
    side = lax.div(place, 2)
    dts[:, lane(side * LANES)] = near
    dts[:, lane((1 - side) * LANES)] = far
    head0 = place * sz.per_group
    raw = pltpu.roll(dts[...], lax.rem(sz.heads - head0, sz.heads), 0)[0 : sz.pad_heads]
    raw = raw + of_heads(sz, bias, head0)
    rates = jnp.maximum(raw, 0.0) + jnp.log1p(jnp.exp(-jnp.abs(raw)))
    decays = -jnp.exp(of_heads(sz, alog, head0)) * rates
    high = decays.astype(BF16).astype(F32)
    middle = (decays - high).astype(BF16).astype(F32)
    low = decays - high - middle
    parts = jnp.concatenate([high, middle, low], axis=0).astype(BF16)
    line = lax.broadcasted_iota(jnp.int32, (BLOCK, BLOCK), 0)
    spot = lax.broadcasted_iota(jnp.int32, (BLOCK, BLOCK), 1)
    upto = jnp.where(line <= spot, 1.0, 0.0).astype(BF16)
    sums = dot(parts, upto, NN)
    n = sz.pad_heads
    log_decay = sums[0:n] + sums[n : 2 * n] + sums[2 * n : 3 * n]
    weight = jnp.exp(log_decay[:, BLOCK - 1 : BLOCK] - log_decay) * rates
    g = sz.per_group
    stats[0:g, :] = log_decay[0:g]
    stats[g : 2 * g, :] = rates[0:g]
    stats[2 * g : 3 * g, :] = jnp.exp(log_decay)[0:g]
    stats[3 * g : 4 * g, :] = weight[0:g]
    gather(sz, xs, place, 0, sz.x_blocks, messages)
    gather(sz, bs, place, sz.x_blocks, sz.s_blocks, messages)
    for t in range(sz.base):
        buffer, u = (xs, t) if t < sz.x_blocks else (bs, t - sz.x_blocks)
        cols = slice(u * LANES, (u + 1) * LANES)
        if chain:
            buffer[0:HALO, cols] = halo[t * HALO : (t + 1) * HALO, :]
        else:
            buffer[0:HALO, cols] = jnp.zeros((HALO, LANES), F32)
    for t in range(sz.s_blocks):
        _, start = column_block(sz, place, sz.x_blocks + t)
        taps = halved_taps(conv_b, start, sz.taps)
        cols = slice(t * LANES, (t + 1) * LANES)
        bc[:, cols] = silu_half(conv_block(bs, BLOCK, taps, t)).astype(BF16)
    states = []
    for t in range(sz.x_blocks):
        _, start = column_block(sz, place, t)
        taps = halved_taps(conv_x, start, sz.taps)
        cols = slice(t * LANES, (t + 1) * LANES)
        value = silu_half(conv_block(xs, BLOCK, taps, t)).astype(BF16)
        xc[:, cols] = value
        turned = jnp.transpose(value.astype(F32))
        up = turned[0:HEAD_DIM] * weight[2 * t : 2 * t + 1]
        down = turned[HEAD_DIM:LANES] * weight[2 * t + 1 : 2 * t + 2]
        weighted = jnp.concatenate([up, down], axis=0).astype(BF16)
        states.append(dot(weighted, bc[...], NN))
    for t in range(sz.x_blocks):
        for s in range(sz.s_blocks):
            row = (t * sz.s_blocks + s) * LANES
            part = states[t][:, s * LANES : (s + 1) * LANES]
            msg[row : row + LANES, :] = part.astype(msg.dtype)
    base = sz.x_blocks * STATE
    for t in range(sz.base):
        buffer, u = (xs, t) if t < sz.x_blocks else (bs, t - sz.x_blocks)
        cols = slice(u * LANES, (u + 1) * LANES)
        first[t * HALO : (t + 1) * HALO, :] = buffer[HALO : 2 * HALO, cols]
        msg[base + t * HALO : base + (t + 1) * HALO, :] = buffer[BLOCK : BLOCK + HALO, cols].astype(msg.dtype)
    size = sz.s_blocks * HALO
    for k, m in enumerate(messages):
        source = lax.bitwise_xor(place, k)
        at = pl.ds(pl.multiple_of(source * size, 8), size)
        tails[at, :] = m[sz.tail_at : sz.tail_at + size, :].astype(F32)
    last = tails[(sz.places - 1) * size :, :]
    msg[base + sz.base * HALO :, :] = last.astype(msg.dtype)


def inner_kernel(sz, skip, c0, c1, c2, c3, conv_c, xc, bc, stats, halo,
                 out, growth, gains, cc, columns, first_c, cs, turned):
    chain = sz.blocks > 2
    place = place_of(sz)
    g = sz.per_group
    turned[...] = jnp.transpose(stats[...])
    columns[...] = turned[0:EDGE, :]
    skips = of_heads(sz, skip, place * g)
    gather(sz, cs, place, 0, sz.s_blocks, (c0, c1, c2, c3))
    for t in range(sz.s_blocks):
        cols = slice(t * LANES, (t + 1) * LANES)
        if chain:
            cs[0:HALO, cols] = halo[(sz.base + t) * HALO : (sz.base + t + 1) * HALO, :]
        else:
            cs[0:HALO, cols] = jnp.zeros((HALO, LANES), F32)
        first_c[t * HALO : (t + 1) * HALO, :] = cs[HALO : 2 * HALO, cols]
        _, start = column_block(sz, place, sz.base + t)
        taps = halved_taps(conv_c, start, sz.taps)
        cc[:, cols] = silu_half(conv_block(cs, BLOCK, taps, t)).astype(BF16)
    half = BLOCK // 2
    skip_keys = 0 if chain else EDGE
    low_lanes = lax.broadcasted_iota(jnp.int32, (half, LANES), 1) < HEAD_DIM
    for t in range(sz.x_blocks):
        cols = slice(t * LANES, (t + 1) * LANES)
        gains[:, cols] = jnp.where(low_lanes[0:8], skips[2 * t : 2 * t + 1], skips[2 * t + 1 : 2 * t + 2])
    for r in range(2):
        width = half * (r + 1)
        at = slice(r * half, (r + 1) * half)
        scores = dot(cc[at, :], bc[0:width, :], NT)
        line = lax.broadcasted_iota(jnp.int32, (half, width), 0) + r * half
        spot = lax.broadcasted_iota(jnp.int32, (half, width), 1)
        keep = (spot <= line) & (spot >= skip_keys)
        for t in range(sz.x_blocks):
            cols = slice(t * LANES, (t + 1) * LANES)
            sums = []
            for h in (2 * t, 2 * t + 1):
                spread = turned[at, h : h + 1] - stats[h : h + 1, 0:width]
                rate = stats[g + h : g + h + 1, 0:width]
                mixing = scores * jnp.exp(jnp.where(keep, spread, -1e30)) * rate
                sums.append(dot(mixing.astype(BF16), xc[0:width, cols], NN))
            both = jnp.where(low_lanes, sums[0], sums[1])
            out[at, cols] = both + gains[0:1, cols] * xc[at, cols].astype(F32)
            rise = 2 * g + 2 * t
            growth[at, cols] = jnp.where(low_lanes, turned[at, rise : rise + 1], turned[at, rise + 1 : rise + 2])


def outer_kernel(sz, conv_x, conv_b, conv_c, xc, bc, cc, stats, columns, first, first_c, growth, gains,
                 inner, arrived, o0, o1, o2, o3, edge, c_all, total):
    chain = sz.blocks > 2
    place = place_of(sz)
    later = lax.axis_index("seq") >= sz.places
    g, rows = sz.per_group, sz.rows
    if chain:
        c_all[...] = cc[...]
    else:
        base = sz.x_blocks * STATE
        renewed = []
        for t in range(sz.cols):
            cols = slice(t * LANES, (t + 1) * LANES)
            ahead = arrived[base + t * HALO : base + (t + 1) * HALO, :].astype(F32)
            edge[0:HALO, cols] = jnp.where(later, ahead, 0.0)
            u = t - sz.base
            edge[HALO : 2 * HALO, cols] = (
                first[t * HALO : (t + 1) * HALO, :] if u < 0 else first_c[u * HALO : (u + 1) * HALO, :]
            )
        for t in range(sz.cols):
            which, start = column_block(sz, place, t)
            taps = halved_taps((conv_x, conv_b, conv_c)[which], start, sz.taps)
            fresh = silu_half(conv_block(edge, HALO, taps, t))
            u = t - (0, sz.x_blocks, sz.base)[which]
            old = (xc, bc, cc)[which][0:EDGE, u * LANES : (u + 1) * LANES].astype(F32)
            renewed.append(jnp.concatenate([fresh, old[HALO:EDGE]], axis=0).astype(BF16))
        for t in range(sz.s_blocks):
            cols = slice(t * LANES, (t + 1) * LANES)
            c_all[EDGE:, cols] = cc[EDGE:, cols]
            c_all[0:EDGE, cols] = renewed[sz.base + t]
        b_edge = jnp.concatenate(renewed[sz.x_blocks : sz.base], axis=1)
        edge_scores = dot(b_edge, c_all[...], NT)
        line = lax.broadcasted_iota(jnp.int32, (EDGE, BLOCK), 0)
        spot = lax.broadcasted_iota(jnp.int32, (EDGE, BLOCK), 1)
        keep = spot >= line
    for t in range(sz.x_blocks):
        cols = slice(t * LANES, (t + 1) * LANES)
        pieces = [
            arrived[(t * sz.s_blocks + s) * LANES : (t * sz.s_blocks + s + 1) * LANES, :]
            for s in range(sz.s_blocks)
        ]
        state = jnp.where(later, jnp.concatenate(pieces, axis=1).astype(F32), 0.0).astype(BF16)
        out = inner[:, cols] + dot(c_all[...], state, NT) * growth[:, cols]
        if not chain:
            mixed, values = [], []
            edge_low = lax.broadcasted_iota(jnp.int32, (EDGE, LANES), 1) < HEAD_DIM
            x_edge = renewed[t].astype(F32)
            for h in (2 * t, 2 * t + 1):
                spread = stats[h : h + 1, :] - columns[:, h : h + 1]
                rate = columns[:, g + h : g + h + 1]
                mixed.append(edge_scores * jnp.exp(jnp.where(keep, spread, -1e30)) * rate)
                mine = edge_low if h == 2 * t else jnp.logical_not(edge_low)
                values.append(jnp.where(mine, x_edge, 0.0))
            mixed = jnp.concatenate(mixed, axis=0).astype(BF16)
            values = jnp.concatenate(values, axis=0).astype(BF16)
            out = out + dot(mixed, values, TN)
            change = gains[0:1, cols] * (x_edge - xc[0:EDGE, cols].astype(F32))
            total[:, cols] = out
            total[0:EDGE, cols] = out[0:EDGE] + change
        else:
            total[:, cols] = out
    for k, o in enumerate((o0, o1, o2, o3)):
        target = lax.bitwise_xor(place, k)
        o[...] = total[pl.ds(pl.multiple_of(target * rows, 8), rows), :].astype(BF16)


def norm_kernel(sz, o0, r1, r2, r3, z, gain, out):
    place = place_of(sz)
    width = sz.x_blocks * LANES
    for k, part in enumerate((o0, r1, r2, r3)):
        group = lax.bitwise_xor(place, k)
        at = pl.ds(pl.multiple_of(group * width, LANES), width)
        gate = 0.5 * z[:, at].astype(F32)
        value = part[...].astype(F32) * silu_half(gate)
        mean = jnp.sum(value * value, axis=-1, keepdims=True) * (1.0 / width)
        out[:, at] = (value * lax.rsqrt(mean + 1e-05) * gain[0:1, at]).astype(BF16)


def call(kernel, sz, outs, scratch, specs, name, flops=0, touched=0):
    return pl.pallas_call(
        functools.partial(kernel, sz),
        out_shape=[jax.ShapeDtypeStruct(s, d) for s, d in outs],
        in_specs=specs,
        out_specs=[VMEM] * len(outs),
        scratch_shapes=[s if not isinstance(s, tuple) else pltpu.VMEM(*s) for s in scratch],
        compiler_params=pltpu.CompilerParams(vmem_limit_bytes=24 << 20),
        cost_estimate=pl.CostEstimate(flops=flops, bytes_accessed=touched, transcendentals=0),
        name=name,
    )


def body(x_in, b_in, c_in, z_in, dt_raw, dt_bias, a_log, d_skip, conv_x, conv_b, conv_c, norm_gain):
    seq_total = lax.axis_size("seq")
    sz = Sizes(x_in, b_in, dt_raw, seq_total, conv_x.shape[0])
    n, rows = sz.places, sz.rows
    chain = sz.blocks > 2

    def swap(k):
        return [(i, i - i % n + ((i % n) ^ k)) for i in range(seq_total)]

    def onward(k, wrap):
        pairs = [(i, i + n * k) for i in range(seq_total)]
        return [(i, j % seq_total) for i, j in pairs if wrap or j < seq_total]

    copies = 1 + n * (sz.cols + sz.s_blocks)
    sent = call(
        pack_kernel,
        sz,
        [((sz.message, LANES), BF16)] * n + [((sz.message_c, LANES), BF16)] * n,
        [((sz.heads, rows), BF16), pltpu.SemaphoreType.DMA((copies,))],
        [HBM] * 4,
        "pack",
    )(*(pltpu.with_memory_space_constraint(a, pltpu.HBM) for a in (x_in, b_in, c_in, dt_raw.T)))
    came, came_c = [sent[0]], [sent[n]]
    for k in range(1, n):
        came.append(lax.ppermute(sent[k], "seq", swap(k)))
    for k in range(1, n):
        came_c.append(lax.ppermute(sent[n + k], "seq", swap(k)))

    width = sz.x_blocks * LANES
    padded = BLOCK + HALO
    edge_rows = sz.cols * HALO
    if chain:
        place = lax.rem(lax.axis_index("seq"), n)
        ends = []
        for m in came:
            body_rows = m[: sz.tail_at].reshape(sz.base, rows, LANES)[:, rows - HALO :]
            ends.append(jnp.concatenate([body_rows.reshape(-1, LANES), m[sz.tail_at : sz.dt_at]], axis=0))
        tail = lax.dynamic_index_in_dim(jnp.stack(ends), lax.bitwise_xor(place, n - 1), 0, keepdims=False)
        halo = lax.ppermute(tail, "seq", onward(1, False)).astype(F32)
    else:
        halo = jnp.zeros((8, LANES), F32)

    msg, xc, bc, stats, first = call(
        state_kernel,
        sz,
        [
            ((sz.x_blocks * STATE + edge_rows, LANES), F32 if chain else BF16),
            ((BLOCK, width), BF16),
            ((BLOCK, STATE), BF16),
            ((sz.stat_rows, BLOCK), F32),
            ((sz.base * HALO, LANES), F32),
        ],
        [
            ((padded, width), F32),
            ((padded, STATE), F32),
            ((sz.heads, BLOCK), F32),
            ((n * sz.s_blocks * HALO, LANES), F32),
        ],
        [VMEM] * 9,
        "state",
    )(dt_bias.reshape(1, -1), a_log.reshape(1, -1), *came, conv_x, conv_b, halo)

    if chain:
        cut = sz.x_blocks * STATE
        grown = msg[:cut].reshape(sz.x_blocks, sz.s_blocks, 2, HEAD_DIM, LANES)
        fade = jnp.exp(stats[: sz.per_group, BLOCK - 1]).reshape(sz.x_blocks, 1, 2, 1, 1)
        k = 1
        while k < sz.blocks:
            grown = grown + fade * lax.ppermute(grown, "seq", onward(k, False))
            fade = fade * lax.ppermute(fade, "seq", onward(k, False))
            k *= 2
        msg = jnp.concatenate([grown.reshape(cut, LANES), msg[cut:]], axis=0).astype(BF16)
    arrived = lax.ppermute(msg, "seq", onward(1, True))

    inner, growth, gains, cc, columns, first_c = call(
        inner_kernel,
        sz,
        [
            ((BLOCK, width), F32),
            ((BLOCK, width), F32),
            ((8, width), F32),
            ((BLOCK, STATE), BF16),
            ((EDGE, sz.stat_rows), F32),
            ((sz.s_blocks * HALO, LANES), F32),
        ],
        [((padded, STATE), F32), ((BLOCK, sz.stat_rows), F32)],
        [VMEM] * 10,
        "inner",
        flops=1 << 30,
        touched=1 << 22,
    )(d_skip.reshape(1, -1), *came_c, conv_c, xc, bc, stats, halo)

    back = call(
        outer_kernel,
        sz,
        [((rows, width), BF16)] * 4,
        [
            ((2 * HALO, sz.cols * LANES), F32),
            ((BLOCK, STATE), BF16),
            ((BLOCK, width), F32),
        ],
        [VMEM] * 14,
        "outer",
    )(conv_x, conv_b, conv_c, xc, bc, cc, stats, columns, first, first_c, growth, gains, inner, arrived)
    home = [lax.ppermute(back[k], "seq", swap(k)) for k in range(1, n)]

    out = call(norm_kernel, sz, [(x_in.shape, BF16)], [], [VMEM] * 6, "norm")(
        back[0], *home, z_in, norm_gain.reshape(1, -1)
    )
    return out[0]


def solution(mesh):
    rows, wide = P(("rep", "seq"), "head"), P(None, "head")
    placed = (rows,) * 5 + (P("head"),) * 3 + (wide,) * 3 + (P("head"),)
    return jax.shard_map(body, mesh=mesh, in_specs=placed, out_specs=rows, check_vma=False)
```

time: 29.4 us -> 25.7 us (0.87)
  waiting for transfers between devices: 10.5 us -> 6.04 us
  starting transfers between devices: 10.8 us -> 14.4 us
  local copies, waits for them, and re-layouts: 4.11 us -> 1.33 us
    ppermute x6 -> x9, waiting for transfers between devices: 7.65 us -> 3.8 us  [the longest x3 2.33 us: body(): home = [lax.ppermute(back[k], 'seq', swap(k)) for k in range(1, n)]]
    ppermute x6 -> x9, starting transfers between devices: 8.1 us -> 11.7 us  [the longest x3 4.61 us: body(): came.append(lax.ppermute(sent[k], 'seq', swap(k)))]
    unnamed x25 -> x16, local copies, waits for them, and re-layouts: 4.11 us -> 1.33 us
    ppermute x1, waiting for transfers between devices: 2.86 us -> 2.24 us  [body(): arrived = lax.ppermute(msg, 'seq', onward(1, True))]
    pallas_call x1, Pallas kernels: 1.14 us -> 0.64 us  [body(): call(state_kernel, sz, [((sz.x_blocks * STATE + edge_rows, LANES), F32 if...]
    pallas_call x3, Pallas kernels: 1.79 us -> 2.25 us  [the longest x1 1.22 us: body(): call(pack_kernel, sz, [((sz.message, LANES), BF16)] * n + [((sz.message_c...]
  transfers between devices with their start and end apart: 7 -> 10, of which waited for: 7 -> 5; matrix products, arithmetic and copies ran while one was open for 0% -> 0% of each run, Pallas kernels for 2% -> 5%
where the time goes in v2:
time: 25.7 us; the launch traced here: 25.5 us
  starting transfers between devices  14.4 us (56%)
  waiting for transfers between devices  6.04 us (24%)
  Pallas kernels  3.66 us (14%)
  local copies, waits for them, and re-layouts  1.33 us (5%)
    ppermute x3, starting transfers between devices, body(): came.append(lax.ppermute(sent[k], 'seq', swap(k)))  4.61 us
    ppermute x3, starting transfers between devices, body(): came_c.append(lax.ppermute(sent[n + k], 'seq', swap(k)))  3.58 us
    ppermute x3, starting transfers between devices, body(): home = [lax.ppermute(back[k], 'seq', swap(k)) for k in range(1, n)]  3.55 us
    ppermute x1, starting transfers between devices, body(): arrived = lax.ppermute(msg, 'seq', onward(1, True))  2.66 us
    ppermute x3, waiting for transfers between devices, body(): home = [lax.ppermute(back[k], 'seq', swap(k)) for k in range(1, n)]  2.33 us
    ppermute x1, waiting for transfers between devices, body(): arrived = lax.ppermute(msg, 'seq', onward(1, True))  2.24 us
    ppermute x3, waiting for transfers between devices, body(): came.append(lax.ppermute(sent[k], 'seq', swap(k)))  1.47 us
    unnamed x16, local copies, waits for them, and re-layouts  1.33 us
  transfers between devices with their start and end apart: 10, of which 5 were waited for; matrix products, arithmetic and copies ran while one was open for 0% of the time, Pallas kernels for 5%

profile of v2, /device:TPU:0, one launch (start us, length us, event | category | flops | bytes accessed | tf_op | source)
XLA Modules:
  0.0 25.5 jit_solution(17985208214037952933)
XLA Ops:
  0.0 1.2 %pack.1 = (bf16[216,128]{1,0:T(8,128)(2,1)S(1)}, bf16[216,128]{1,0:T(8,128)(2,1)S(1)}, bf16[216,128]{1,0:T(8,128)(2,1)S(1)}, bf16[216,128]{1,0:T(8,128)(2,1)S(1)...) custom-call(bf16[64,512]{1,0:T(8,128)(2,1)} %x.1, ...), custom_call_target="tpu_custom_call" | custom-call | tf_op jit(solution)/shard_map/pack/pallas_call | solution.py:366
  1.2 3.0 %collective-permute-start = (bf16[216,128]{1,0:T(8,128)(2,1)S(1)}, bf16[216,128]{1,0:T(8,128)(2,1)S(1)}, u32[]{:S(2)}, u32[]{:S(2)}) collective-permute-start(bf16[216,128]{1,0:T(8,128)(2,1)S(1)} %get-tuple-element.29), channel_id=1, source_target_pairs={{0,2},{2,0},{4,6},{6,4},{8,10},{10,8},{12,14},{14,12},{1,3},{3,1},... | collective-permute-start | bytes 165896 | tf_op jit(solution)/shard_map/ppermute | solution.py:376
  4.3 1.6 %collective-permute-start.1 = (bf16[216,128]{1,0:T(8,128)(2,1)S(1)}, bf16[216,128]{1,0:T(8,128)(2,1)S(1)}, u32[]{:S(2)}, u32[]{:S(2)}) collective-permute-start(bf16[216,128]{1,0:T(8,128)(2,1)S(1)} %get-tuple-element.30), channel_id=1, source_target_pairs={{0,4},{2,6},{4,0},{6,2},{8,12},{10,14},{12,8},{14,10},{1,5},{3,7},... | collective-permute-start | bytes 165896 | tf_op jit(solution)/shard_map/ppermute | solution.py:376
  5.8 0.0 collective-permute-start.2
  5.8 1.9 %collective-permute-start.3 = (bf16[128,128]{1,0:T(8,128)(2,1)S(1)}, bf16[128,128]{1,0:T(8,128)(2,1)S(1)}, u32[]{:S(2)}, u32[]{:S(2)}) collective-permute-start(bf16[128,128]{1,0:T(8,128)(2,1)S(1)} %get-tuple-element.35), channel_id=1, source_target_pairs={{0,2},{2,0},{4,6},{6,4},{8,10},{10,8},{12,14},{14,12},{1,3},{3,1},... | collective-permute-start | bytes 98312 | tf_op jit(solution)/shard_map/ppermute | solution.py:378
  7.7 1.6 %collective-permute-start.4 = (bf16[128,128]{1,0:T(8,128)(2,1)S(1)}, bf16[128,128]{1,0:T(8,128)(2,1)S(1)}, u32[]{:S(2)}, u32[]{:S(2)}) collective-permute-start(bf16[128,128]{1,0:T(8,128)(2,1)S(1)} %get-tuple-element.36), channel_id=1, source_target_pairs={{0,4},{2,6},{4,0},{6,2},{8,12},{10,14},{12,8},{14,10},{1,5},{3,7},... | collective-permute-start | bytes 98312 | tf_op jit(solution)/shard_map/ppermute | solution.py:378
  9.3 0.0 collective-permute-done.m1
  9.3 0.1 collective-permute-start.5
  9.4 0.0 collective-permute-done.1.m2
  9.4 1.5 %collective-permute-done.2.m3 = bf16[216,128]{1,0:T(8,128)(2,1)S(1)} collective-permute-done((bf16[216,128]{1,0:T(8,128)(2,1)S(1)}, bf16[216,128]{1,0:T(8,128)(2,1)S(1)}, u32[]{:S(2)}, u32[]{:S(2)}) %collective-permute-start.2) | collective-permute-done | bytes 55328 | tf_op jit(solution)/shard_map/ppermute | solution.py:376
  10.9 0.0 copy-done.1
  10.9 0.7 %copy-done.2 = bf16[4,512]{1,0:T(4,128)(2,1)S(1)} copy-done((bf16[4,512]{1,0:T(4,128)(2,1)S(1)}, bf16[4,512]{1,0:T(4,128)(2,1)}, u32[]{:S(2)}) %copy-start.2) | copy-done | bytes 4120
  11.6 0.0 copy-done.6
  11.6 0.6 %state.1 = (bf16[296,128]{1,0:T(8,128)(2,1)S(1)}, bf16[256,128]{1,0:T(8,128)(2,1)S(1)}, bf16[256,256]{1,0:T(8,128)(2,1)S(1)}, f32[8,256]{1,0:T(8,128)S(1)}, f32[24,128]{1,0:T(8,128)S(1)}) custom-call(f32[1,8]{1,0:T(1,128)S(1)} %bitcast.6, f32[1,8]{1,0:T(1,128)S(1)} %bitcast.7, bf16[216,128]{1,0:T(8,128)(2,1)S(1)} %get-tuple-element.28.m0, ...), custom_call_target="tpu_custom_call" | custom-call | tf_op jit(solution)/shard_map/state/pallas_call | solution.py:394
  12.2 0.0 copy-start.3
  12.2 2.7 %collective-permute-start.6 = (bf16[296,128]{1,0:T(8,128)(2,1)S(1)}, bf16[296,128]{1,0:T(8,128)(2,1)S(1)}, u32[]{:S(2)}, u32[]{:S(2)}) collective-permute-start(bf16[296,128]{1,0:T(8,128)(2,1)S(1)} %get-tuple-element.46), channel_id=1, source_target_pairs={{0,8},{2,10},{4,12},{6,14},{8,0},{10,2},{12,4},{14,6},{1,9},{3,11}... | collective-permute-start | bytes 227336 | tf_op jit(solution)/shard_map/ppermute | solution.py:424
  14.9 0.0 collective-permute-done.3.c1
  14.9 0.0 collective-permute-done.4.c2
  14.9 0.0 collective-permute-done.5.c3
  14.9 0.0 copy-start.7
  14.9 0.0 copy-done.3
  14.9 0.6 %copy-done.7 = f32[8]{0:T(128)S(1)} copy-done((f32[8]{0:T(128)S(1)}, f32[8]{0:T(128)}, u32[]{:S(2)}) %copy-start.7) | copy-done | bytes 56
  15.6 0.6 %inner.1 = (f32[256,128]{1,0:T(8,128)S(1)}, f32[256,128]{1,0:T(8,128)S(1)}, f32[8,128]{1,0:T(8,128)S(1)}, bf16[256,256]{1,0:T(8,128)(2,1)S(1)}, f32[16,8]{1,0:T(8,128)S(1)}, /*index=5*/f32[16,128]{1,0:T(8,128)S(1)}) custom-call(f32[1,8]{1,0:T(1,128)S(1)} %bitcast.8, bf16[128,128]{1,0:T(8,128)(2,1)S(1)} %get-tuple-element.34.c0, ...), custom_call_target="tpu_custom_call" | custom-call | flops 1073741824 | bytes 4194304 | tf_op jit(solution)/shard_map/inner/pallas_call | solution.py:426
  16.2 2.2 %collective-permute-done.6.arrived = bf16[296,128]{1,0:T(8,128)(2,1)S(1)} collective-permute-done((bf16[296,128]{1,0:T(8,128)(2,1)S(1)}, bf16[296,128]{1,0:T(8,128)(2,1)S(1)}, u32[]{:S(2)}, u32[]{:S(2)}) %collective-permute-start.6) | collective-permute-done | bytes 75808 | tf_op jit(solution)/shard_map/ppermute | solution.py:424
  18.4 0.4 %outer.1 = (bf16[64,128]{1,0:T(8,128)(2,1)S(1)}, bf16[64,128]{1,0:T(8,128)(2,1)S(1)}, bf16[64,128]{1,0:T(8,128)(2,1)S(1)}, bf16[64,128]{1,0:T(8,128)(2,1)S(1)}) custom-call(bf16[4,512]{1,0:T(4,128)(2,1)S(1)} %copy-done.2, bf16[4,1024]{1,0:T(4,128)(2,1)S(1)} %copy-done.1, bf16[4,1024]{1,0:T(4,128)(2,1)S(1)} %copy-done.3, ...), custom_call_target="tpu_custom_call" | custom-call | tf_op jit(solution)/shard_map/outer/pallas_call | solution.py:444
  18.9 0.1 collective-permute-start.7
  18.9 1.2 %collective-permute-start.8 = (bf16[64,128]{1,0:T(8,128)(2,1)S(1)}, bf16[64,128]{1,0:T(8,128)(2,1)S(1)}, u32[]{:S(2)}, u32[]{:S(2)}) collective-permute-start(bf16[64,128]{1,0:T(8,128)(2,1)S(1)} %get-tuple-element.49), channel_id=1, source_target_pairs={{0,4},{2,6},{4,0},{6,2},{8,12},{10,14},{12,8},{14,10},{1,5},{3,7},... | collective-permute-start | bytes 49160 | tf_op jit(solution)/shard_map/ppermute | solution.py:456
  20.1 2.3 %collective-permute-start.9 = (bf16[64,128]{1,0:T(8,128)(2,1)S(1)}, bf16[64,128]{1,0:T(8,128)(2,1)S(1)}, u32[]{:S(2)}, u32[]{:S(2)}) collective-permute-start(bf16[64,128]{1,0:T(8,128)(2,1)S(1)} %get-tuple-element.50), channel_id=1, source_target_pairs={{0,6},{2,4},{4,2},{6,0},{8,14},{10,12},{12,10},{14,8},{1,7},{3,5},... | collective-permute-start | bytes 49160 | tf_op jit(solution)/shard_map/ppermute | solution.py:456
  22.4 0.2 collective-permute-done.7.r1
  22.7 0.1 collective-permute-done.8.r2
  22.7 2.0 %collective-permute-done.9.r3 = bf16[64,128]{1,0:T(8,128)(2,1)S(1)} collective-permute-done((bf16[64,128]{1,0:T(8,128)(2,1)S(1)}, bf16[64,128]{1,0:T(8,128)(2,1)S(1)}, u32[]{:S(2)}, u32[]{:S(2)}) %collective-permute-start.9) | collective-permute-done | bytes 16416 | tf_op jit(solution)/shard_map/ppermute | solution.py:456
  24.8 0.8 %norm.1 = bf16[64,512]{1,0:T(8,128)(2,1)} custom-call(bf16[64,128]{1,0:T(8,128)(2,1)S(1)} %get-tuple-element.47.o0, bf16[64,128]{1,0:T(8,128)(2,1)S(1)} %collective-permute-done.7.r1, bf16[64,128]{1,0:T(8,128)(2,1)S(1)} %collective-permute-done.8.r2, bf16[64,128]{1,0:T(8,128)(2,1)S(1)} %collective-permute-done.9.r3, bf16[64,512]{1,0:T(8,128)(2,1)S(1)} %copy-done, ...), custom_call_target="tpu_custom_call" | custom-call | tf_op jit(solution)/shard_map/norm/pallas_call | solution.py:458
  (10 shorter events, 0.0 us)
Async XLA Ops:
  1.2 8.1 %collective-permute-start = (bf16[216,128]{1,0:T(8,128)(2,1)S(1)}, bf16[216,128]{1,0:T(8,128)(2,1)S(1)}, u32[]{:S(2)}, u32[]{:S(2)}) collective-permute-start(bf16[216,128]{1,0:T(8,128)(2,1)S(1)} %get-tuple-element.29), channel_id=1, source_target_pairs={{0,2},{2,0},{4,6},{6,4},{8,10},{10,8},{12,14},{14,12},{1,3},{3,1},... | collective-permute-start | bytes 165896 | tf_op jit(solution)/shard_map/ppermute | solution.py:376
  4.3 5.2 %collective-permute-start.1 = (bf16[216,128]{1,0:T(8,128)(2,1)S(1)}, bf16[216,128]{1,0:T(8,128)(2,1)S(1)}, u32[]{:S(2)}, u32[]{:S(2)}) collective-permute-start(bf16[216,128]{1,0:T(8,128)(2,1)S(1)} %get-tuple-element.30), channel_id=1, source_target_pairs={{0,4},{2,6},{4,0},{6,2},{8,12},{10,14},{12,8},{14,10},{1,5},{3,7},... | collective-permute-start | bytes 165896 | tf_op jit(solution)/shard_map/ppermute | solution.py:376
  5.8 5.1 %copy-start.1 = (bf16[4,1024]{1,0:T(4,128)(2,1)S(1)}, bf16[4,1024]{1,0:T(4,128)(2,1)}, u32[]{:S(2)}) copy-start(bf16[4,1024]{1,0:T(4,128)(2,1)} %conv_b.3) | copy-start | bytes 24580
  5.8 5.1 %collective-permute-start.2 = (bf16[216,128]{1,0:T(8,128)(2,1)S(1)}, bf16[216,128]{1,0:T(8,128)(2,1)S(1)}, u32[]{:S(2)}, u32[]{:S(2)}) collective-permute-start(bf16[216,128]{1,0:T(8,128)(2,1)S(1)} %get-tuple-element.31), channel_id=1, source_target_pairs={{0,6},{2,4},{4,2},{6,0},{8,14},{10,12},{12,10},{14,8},{1,7},{3,5},... | collective-permute-start | bytes 165896 | tf_op jit(solution)/shard_map/ppermute | solution.py:376
  5.8 9.1 %collective-permute-start.3 = (bf16[128,128]{1,0:T(8,128)(2,1)S(1)}, bf16[128,128]{1,0:T(8,128)(2,1)S(1)}, u32[]{:S(2)}, u32[]{:S(2)}) collective-permute-start(bf16[128,128]{1,0:T(8,128)(2,1)S(1)} %get-tuple-element.35), channel_id=1, source_target_pairs={{0,2},{2,0},{4,6},{6,4},{8,10},{10,8},{12,14},{14,12},{1,3},{3,1},... | collective-permute-start | bytes 98312 | tf_op jit(solution)/shard_map/ppermute | solution.py:378
  7.7 7.2 %collective-permute-start.4 = (bf16[128,128]{1,0:T(8,128)(2,1)S(1)}, bf16[128,128]{1,0:T(8,128)(2,1)S(1)}, u32[]{:S(2)}, u32[]{:S(2)}) collective-permute-start(bf16[128,128]{1,0:T(8,128)(2,1)S(1)} %get-tuple-element.36), channel_id=1, source_target_pairs={{0,4},{2,6},{4,0},{6,2},{8,12},{10,14},{12,8},{14,10},{1,5},{3,7},... | collective-permute-start | bytes 98312 | tf_op jit(solution)/shard_map/ppermute | solution.py:378
  9.3 5.6 %collective-permute-start.5 = (bf16[128,128]{1,0:T(8,128)(2,1)S(1)}, bf16[128,128]{1,0:T(8,128)(2,1)S(1)}, u32[]{:S(2)}, u32[]{:S(2)}) collective-permute-start(bf16[128,128]{1,0:T(8,128)(2,1)S(1)} %get-tuple-element.37), channel_id=1, source_target_pairs={{0,6},{2,4},{4,2},{6,0},{8,14},{10,12},{12,10},{14,8},{1,7},{3,5},... | collective-permute-start | bytes 98312 | tf_op jit(solution)/shard_map/ppermute | solution.py:378
  10.9 0.7 %copy-start.2 = (bf16[4,512]{1,0:T(4,128)(2,1)S(1)}, bf16[4,512]{1,0:T(4,128)(2,1)}, u32[]{:S(2)}) copy-start(bf16[4,512]{1,0:T(4,128)(2,1)} %conv_x.3) | copy-start | bytes 12292
  10.9 0.7 %copy-start.5 = (f32[8]{0:T(128)S(1)}, f32[8]{0:T(128)}, u32[]{:S(2)}) copy-start(f32[8]{0:T(128)} %param.17) | copy-start | bytes 100
  10.9 0.7 %copy-start.6 = (f32[8]{0:T(128)S(1)}, f32[8]{0:T(128)}, u32[]{:S(2)}) copy-start(f32[8]{0:T(128)} %param.18) | copy-start | bytes 100
  12.2 2.7 %copy-start.3 = (bf16[4,1024]{1,0:T(4,128)(2,1)S(1)}, bf16[4,1024]{1,0:T(4,128)(2,1)}, u32[]{:S(2)}) copy-start(bf16[4,1024]{1,0:T(4,128)(2,1)} %conv_c.3) | copy-start | bytes 24580
  12.2 6.2 %collective-permute-start.6 = (bf16[296,128]{1,0:T(8,128)(2,1)S(1)}, bf16[296,128]{1,0:T(8,128)(2,1)S(1)}, u32[]{:S(2)}, u32[]{:S(2)}) collective-permute-start(bf16[296,128]{1,0:T(8,128)(2,1)S(1)} %get-tuple-element.46), channel_id=1, source_target_pairs={{0,8},{2,10},{4,12},{6,14},{8,0},{10,2},{12,4},{14,6},{1,9},{3,11}... | collective-permute-start | bytes 227336 | tf_op jit(solution)/shard_map/ppermute | solution.py:424
  14.9 0.7 %copy-start.7 = (f32[8]{0:T(128)S(1)}, f32[8]{0:T(128)}, u32[]{:S(2)}) copy-start(f32[8]{0:T(128)} %param.19) | copy-start | bytes 100
  18.4 6.3 %copy-start = (bf16[64,512]{1,0:T(8,128)(2,1)S(1)}, bf16[64,512]{1,0:T(8,128)(2,1)}, u32[]{:S(2)}) copy-start(bf16[64,512]{1,0:T(8,128)(2,1)} %z.1) | copy-start | bytes 196612
  18.9 3.8 %collective-permute-start.7 = (bf16[64,128]{1,0:T(8,128)(2,1)S(1)}, bf16[64,128]{1,0:T(8,128)(2,1)S(1)}, u32[]{:S(2)}, u32[]{:S(2)}) collective-permute-start(bf16[64,128]{1,0:T(8,128)(2,1)S(1)} %get-tuple-element.48), channel_id=1, source_target_pairs={{0,2},{2,0},{4,6},{6,4},{8,10},{10,8},{12,14},{14,12},{1,3},{3,1},... | collective-permute-start | bytes 49160 | tf_op jit(solution)/shard_map/ppermute | solution.py:456
  18.9 3.8 %collective-permute-start.8 = (bf16[64,128]{1,0:T(8,128)(2,1)S(1)}, bf16[64,128]{1,0:T(8,128)(2,1)S(1)}, u32[]{:S(2)}, u32[]{:S(2)}) collective-permute-start(bf16[64,128]{1,0:T(8,128)(2,1)S(1)} %get-tuple-element.49), channel_id=1, source_target_pairs={{0,4},{2,6},{4,0},{6,2},{8,12},{10,14},{12,8},{14,10},{1,5},{3,7},... | collective-permute-start | bytes 49160 | tf_op jit(solution)/shard_map/ppermute | solution.py:456
  20.1 4.6 %copy-start.4 = (f32[512]{0:T(512)S(1)}, f32[512]{0:T(512)}, u32[]{:S(2)}) copy-start(f32[512]{0:T(512)} %param.23) | copy-start | bytes 6148
  20.1 4.6 %collective-permute-start.9 = (bf16[64,128]{1,0:T(8,128)(2,1)S(1)}, bf16[64,128]{1,0:T(8,128)(2,1)S(1)}, u32[]{:S(2)}, u32[]{:S(2)}) collective-permute-start(bf16[64,128]{1,0:T(8,128)(2,1)S(1)} %get-tuple-element.50), channel_id=1, source_target_pairs={{0,6},{2,4},{4,2},{6,0},{8,14},{10,12},{12,10},{14,8},{1,7},{3,5},... | collective-permute-start | bytes 49160 | tf_op jit(solution)/shard_map/ppermute | solution.py:456

commit v3 on v2

--- a/solution.py
+++ b/solution.py
@@ -39,10 +39,9 @@
         self.s_blocks = STATE // LANES
         self.base = self.x_blocks + self.s_blocks
         self.cols = self.base + self.s_blocks
-        self.tail_at = self.rows * self.base
-        self.dt_at = self.tail_at + self.s_blocks * HALO
-        self.message = self.dt_at + self.heads
-        self.message_c = self.rows * self.s_blocks
+        self.message = (self.rows + max(HALO, self.heads), self.base * LANES)
+        self.dt_lanes = slice((self.base - 1) * LANES, self.base * LANES)
+        self.halo_rows = -(-self.cols * (taps - 1) // 16) * 16
         self.pad_heads = max(8, self.per_group)
         self.stat_rows = 4 * self.per_group
         if self.places != self.groups or self.rows * 2 != LANES or self.places != 4:
@@ -61,45 +60,61 @@
     return half + half * jnp.tanh(half)
 
 
-def column_block(sz, group, t):
-    if t < sz.x_blocks:
-        return 0, (group * sz.x_blocks + t) * LANES
-    t -= sz.x_blocks
-    which, t = (1, t) if t < sz.s_blocks else (2, t - sz.s_blocks)
-    return which, (group * sz.s_blocks + t) * LANES
-
-
-def pack_kernel(sz, x, b, c, dt, m0, m1, m2, m3, c0, c1, c2, c3, dt_here, sem):
-    place = place_of(sz)
-    rows = sz.rows
-    copies = []
-
-    def fetch(source, target):
-        copies.append(pltpu.make_async_copy(source, target, sem.at[len(copies)]))
-        copies[-1].start()
-
-    fetch(dt, dt_here)
-    for k, m, mc in ((3, m3, c3), (2, m2, c2), (1, m1, c1), (0, m0, c0)):
-        group = lax.bitwise_xor(place, k)
-        for t in range(sz.cols):
-            which, start = column_block(sz, group, t)
-            source = (x, b, c)[which].at[:, lane(start)]
-            if t < sz.base:
-                fetch(source, m.at[t * rows : (t + 1) * rows, :])
-            else:
-                u = t - sz.base
-                fetch(source, mc.at[u * rows : (u + 1) * rows, :])
-                at = sz.tail_at + u * HALO
-                fetch(c.at[rows - HALO :, lane(start)], m.at[at : at + HALO, :])
+def lanes_of(array, group, width):
+    return array.at[:, pl.ds(pl.multiple_of(group * width, LANES), width)]
+
+
+def fetch_all(pairs, sem):
+    copies = [pltpu.make_async_copy(source, target, sem.at[i]) for i, (source, target) in enumerate(pairs)]
+    for copy in copies:
+        copy.start()
+    return copies
+
+
+def message_parts(sz, group, x, b, c, m, mc):
+    rows, wide = sz.rows, sz.x_blocks * LANES
+    tail = lanes_of(c, group, STATE).at[rows - HALO :, :]
+    return [
+        (lanes_of(x, group, wide), m.at[0:rows, 0:wide]),
+        (lanes_of(b, group, STATE), m.at[0:rows, wide:]),
+        (tail, m.at[rows : rows + HALO, 0:STATE]),
+        (lanes_of(c, group, STATE), mc),
+    ]
+
+
+def pack_kernel(sz, x, b, c, dt, m1, m2, m3, c1, c2, c3, dt_rows, dt_here, sem):
+    place = place_of(sz)
+    pairs = [(dt, dt_here)]
+    for k, m, mc in ((3, m3, c3), (2, m2, c2), (1, m1, c1)):
+        pairs += message_parts(sz, lax.bitwise_xor(place, k), x, b, c, m, mc)
+    copies = fetch_all(pairs, sem)
     copies[0].wait()
     here = dt_here[...].astype(F32)
     twice = jnp.concatenate([here, here], axis=1)
     spot = lax.broadcasted_iota(jnp.int32, twice.shape, 1)
-    mine = lax.div(spot, rows) == lax.rem(place, 2)
-    dt_rows = jnp.where(mine, twice, 0.0).astype(BF16)
-    for m in (m0, m1, m2, m3):
-        m[sz.dt_at :, :] = dt_rows
+    mine = lax.div(spot, sz.rows) == lax.rem(place, 2)
+    spread = jnp.where(mine, twice, 0.0).astype(BF16)
+    dt_rows[...] = spread
+    for m in (m1, m2, m3):
+        m[sz.rows : sz.rows + sz.heads, sz.dt_lanes] = spread
     for copy in copies[1:]:
+        copy.wait()
+
+
+def own_kernel(sz, x, b, c, conv_x, conv_b, conv_c, bias, alog, skip, dt_rows,
+               m0, c0, taps_x, taps_b, taps_c, bias_here, alog_here, skip_here, sem):
+    place = place_of(sz)
+    pairs = message_parts(sz, place, x, b, c, m0, c0) + [
+        (lanes_of(conv_x, place, sz.x_blocks * LANES), taps_x),
+        (lanes_of(conv_b, place, STATE), taps_b),
+        (lanes_of(conv_c, place, STATE), taps_c),
+        (bias, bias_here),
+        (alog, alog_here),
+        (skip, skip_here),
+    ]
+    copies = fetch_all(pairs, sem)
+    m0[sz.rows : sz.rows + sz.heads, sz.dt_lanes] = dt_rows[...]
+    for copy in copies:
         copy.wait()
 
 
@@ -113,8 +128,8 @@
     return total
 
 
-def halved_taps(ref, start, n):
-    return [0.5 * ref[i : i + 1, lane(start)].astype(F32) for i in range(n)]
+def halved_taps(ref, t, n):
+    return [0.5 * ref[i : i + 1, t * LANES : (t + 1) * LANES].astype(F32) for i in range(n)]
 
 
 def gather(sz, buffer, place, base, count, messages):
@@ -122,8 +137,8 @@
         source = lax.bitwise_xor(place, k)
         at = pl.ds(pl.multiple_of(HALO + source * sz.rows, 8), sz.rows)
         for t in range(count):
-            row = (base + t) * sz.rows
-            buffer[at, t * LANES : (t + 1) * LANES] = m[row : row + sz.rows, :].astype(F32)
+            cols = slice((base + t) * LANES, (base + t + 1) * LANES)
+            buffer[at, t * LANES : (t + 1) * LANES] = m[0 : sz.rows, cols].astype(F32)
 
 
 def of_heads(sz, ref, head0):
@@ -134,13 +149,15 @@
     return jnp.sum(jnp.where(spot == line + head0, row, 0.0), axis=1, keepdims=True)
 
 
-def state_kernel(sz, bias, alog, m0, m1, m2, m3, conv_x, conv_b, halo,
-                 msg, xc, bc, stats, first, xs, bs, dts, tails):
+def state_kernel(sz, bias, alog, m0, m1, m2, m3, taps_x, taps_b, halo,
+                 msg, xc, bc, stats, first, xs, bs, dts, tails, packed):
     chain = sz.blocks > 2
     place = place_of(sz)
     messages = (m0, m1, m2, m3)
+    dt_at = slice(sz.rows, sz.rows + sz.heads)
     near, far = (
-        p[sz.dt_at :, :].astype(F32) + q[sz.dt_at :, :].astype(F32) for p, q in ((m0, m1), (m2, m3))
+        p[dt_at, sz.dt_lanes].astype(F32) + q[dt_at, sz.dt_lanes].astype(F32)
+        for p, q in ((m0, m1), (m2, m3))
     )
     side = lax.div(place, 2)
     dts[:, lane(side * LANES)] = near
@@ -176,14 +193,12 @@
         else:
             buffer[0:HALO, cols] = jnp.zeros((HALO, LANES), F32)
     for t in range(sz.s_blocks):
-        _, start = column_block(sz, place, sz.x_blocks + t)
-        taps = halved_taps(conv_b, start, sz.taps)
+        taps = halved_taps(taps_b, t, sz.taps)
         cols = slice(t * LANES, (t + 1) * LANES)
         bc[:, cols] = silu_half(conv_block(bs, BLOCK, taps, t)).astype(BF16)
     states = []
     for t in range(sz.x_blocks):
-        _, start = column_block(sz, place, t)
-        taps = halved_taps(conv_x, start, sz.taps)
+        taps = halved_taps(taps_x, t, sz.taps)
         cols = slice(t * LANES, (t + 1) * LANES)
         value = silu_half(conv_block(xs, BLOCK, taps, t)).astype(BF16)
         xc[:, cols] = value
@@ -197,22 +212,26 @@
             row = (t * sz.s_blocks + s) * LANES
             part = states[t][:, s * LANES : (s + 1) * LANES]
             msg[row : row + LANES, :] = part.astype(msg.dtype)
-    base = sz.x_blocks * STATE
-    for t in range(sz.base):
-        buffer, u = (xs, t) if t < sz.x_blocks else (bs, t - sz.x_blocks)
-        cols = slice(u * LANES, (u + 1) * LANES)
-        first[t * HALO : (t + 1) * HALO, :] = buffer[HALO : 2 * HALO, cols]
-        msg[base + t * HALO : base + (t + 1) * HALO, :] = buffer[BLOCK : BLOCK + HALO, cols].astype(msg.dtype)
-    size = sz.s_blocks * HALO
+    base, over = sz.x_blocks * STATE, sz.taps - 1
     for k, m in enumerate(messages):
         source = lax.bitwise_xor(place, k)
-        at = pl.ds(pl.multiple_of(source * size, 8), size)
-        tails[at, :] = m[sz.tail_at : sz.tail_at + size, :].astype(F32)
-    last = tails[(sz.places - 1) * size :, :]
-    msg[base + sz.base * HALO :, :] = last.astype(msg.dtype)
-
-
-def inner_kernel(sz, skip, c0, c1, c2, c3, conv_c, xc, bc, stats, halo,
+        at = pl.ds(pl.multiple_of(source * HALO, 8), HALO)
+        tails[at, :] = m[sz.rows : sz.rows + HALO, 0:STATE].astype(F32)
+    packed[...] = jnp.zeros(packed.shape, F32)
+    for t in range(sz.cols):
+        if t < sz.base:
+            buffer, u = (xs, t) if t < sz.x_blocks else (bs, t - sz.x_blocks)
+            cols = slice(u * LANES, (u + 1) * LANES)
+            first[t * HALO : (t + 1) * HALO, :] = buffer[HALO : 2 * HALO, cols]
+            last = buffer[BLOCK : BLOCK + HALO, cols]
+        else:
+            cols = slice((t - sz.base) * LANES, (t - sz.base + 1) * LANES)
+            last = tails[(sz.places - 1) * HALO :, cols]
+        packed[t * over : (t + 1) * over, :] = last[HALO - over :]
+    msg[base:, :] = packed[...].astype(msg.dtype)
+
+
+def inner_kernel(sz, skip, c0, c1, c2, c3, taps_c, xc, bc, stats, halo,
                  out, growth, gains, cc, columns, first_c, cs, turned):
     chain = sz.blocks > 2
     place = place_of(sz)
@@ -228,8 +247,7 @@
         else:
             cs[0:HALO, cols] = jnp.zeros((HALO, LANES), F32)
         first_c[t * HALO : (t + 1) * HALO, :] = cs[HALO : 2 * HALO, cols]
-        _, start = column_block(sz, place, sz.base + t)
-        taps = halved_taps(conv_c, start, sz.taps)
+        taps = halved_taps(taps_c, t, sz.taps)
         cc[:, cols] = silu_half(conv_block(cs, BLOCK, taps, t)).astype(BF16)
     half = BLOCK // 2
     skip_keys = 0 if chain else EDGE
@@ -258,8 +276,8 @@
             growth[at, cols] = jnp.where(low_lanes, turned[at, rise : rise + 1], turned[at, rise + 1 : rise + 2])
 
 
-def outer_kernel(sz, conv_x, conv_b, conv_c, xc, bc, cc, stats, columns, first, first_c, growth, gains,
-                 inner, arrived, o0, o1, o2, o3, edge, c_all, total):
+def outer_kernel(sz, taps_x, taps_b, taps_c, xc, bc, cc, stats, columns, first, first_c, growth, gains,
+                 inner, arrived, o0, o1, o2, o3, edge, ahead, c_all, total):
     chain = sz.blocks > 2
     place = place_of(sz)
     later = lax.axis_index("seq") >= sz.places
@@ -268,20 +286,20 @@
         c_all[...] = cc[...]
     else:
         base = sz.x_blocks * STATE
-        renewed = []
+        renewed, over = [], sz.taps - 1
+        ahead[...] = jnp.where(later, arrived[base:, :].astype(F32), 0.0)
         for t in range(sz.cols):
             cols = slice(t * LANES, (t + 1) * LANES)
-            ahead = arrived[base + t * HALO : base + (t + 1) * HALO, :].astype(F32)
-            edge[0:HALO, cols] = jnp.where(later, ahead, 0.0)
+            edge[HALO - over : HALO, cols] = ahead[t * over : (t + 1) * over, :]
             u = t - sz.base
             edge[HALO : 2 * HALO, cols] = (
                 first[t * HALO : (t + 1) * HALO, :] if u < 0 else first_c[u * HALO : (u + 1) * HALO, :]
             )
         for t in range(sz.cols):
-            which, start = column_block(sz, place, t)
-            taps = halved_taps((conv_x, conv_b, conv_c)[which], start, sz.taps)
+            which = (t >= sz.x_blocks) + (t >= sz.base)
+            u = t - (0, sz.x_blocks, sz.base)[which]
+            taps = halved_taps((taps_x, taps_b, taps_c)[which], u, sz.taps)
             fresh = silu_half(conv_block(edge, HALO, taps, t))
-            u = t - (0, sz.x_blocks, sz.base)[which]
             old = (xc, bc, cc)[which][0:EDGE, u * LANES : (u + 1) * LANES].astype(F32)
             renewed.append(jnp.concatenate([fresh, old[HALO:EDGE]], axis=0).astype(BF16))
         for t in range(sz.s_blocks):
@@ -362,30 +380,41 @@
         pairs = [(i, i + n * k) for i in range(seq_total)]
         return [(i, j % seq_total) for i, j in pairs if wrap or j < seq_total]
 
-    copies = 1 + n * (sz.cols + sz.s_blocks)
-    sent = call(
+    def stay(*arrays):
+        return [pltpu.with_memory_space_constraint(a, pltpu.HBM) for a in arrays]
+
+    width = sz.x_blocks * LANES
+    to_c = ((rows, STATE), BF16)
+    *sent, dt_rows = call(
         pack_kernel,
         sz,
-        [((sz.message, LANES), BF16)] * n + [((sz.message_c, LANES), BF16)] * n,
-        [((sz.heads, rows), BF16), pltpu.SemaphoreType.DMA((copies,))],
+        [(sz.message, BF16)] * (n - 1) + [to_c] * (n - 1) + [((sz.heads, LANES), BF16)],
+        [((sz.heads, rows), BF16), pltpu.SemaphoreType.DMA((1 + 4 * (n - 1),))],
         [HBM] * 4,
         "pack",
-    )(*(pltpu.with_memory_space_constraint(a, pltpu.HBM) for a in (x_in, b_in, c_in, dt_raw.T)))
-    came, came_c = [sent[0]], [sent[n]]
-    for k in range(1, n):
-        came.append(lax.ppermute(sent[k], "seq", swap(k)))
-    for k in range(1, n):
-        came_c.append(lax.ppermute(sent[n + k], "seq", swap(k)))
-
-    width = sz.x_blocks * LANES
+    )(*stay(x_in, b_in, c_in, dt_raw.T))
+    arrivals = [lax.ppermute(sent[k], "seq", swap(k % (n - 1) + 1)) for k in range(2 * (n - 1))]
+    vectors = [v.reshape(1, -1) for v in (dt_bias, a_log, d_skip)]
+    m0, c0, taps_x, taps_b, taps_c, bias, alog, skip = call(
+        own_kernel,
+        sz,
+        [(sz.message, BF16), to_c, ((sz.taps, width), BF16)]
+        + [((sz.taps, STATE), BF16)] * 2
+        + [((1, sz.heads), F32)] * 3,
+        [pltpu.SemaphoreType.DMA((10,))],
+        [HBM] * 9 + [VMEM],
+        "own",
+    )(*stay(x_in, b_in, c_in, conv_x, conv_b, conv_c, *vectors), dt_rows)
+    came, came_c = [m0, *arrivals[: n - 1]], [c0, *arrivals[n - 1 :]]
+
     padded = BLOCK + HALO
-    edge_rows = sz.cols * HALO
+    edge_rows = sz.halo_rows
     if chain:
         place = lax.rem(lax.axis_index("seq"), n)
         ends = []
         for m in came:
-            body_rows = m[: sz.tail_at].reshape(sz.base, rows, LANES)[:, rows - HALO :]
-            ends.append(jnp.concatenate([body_rows.reshape(-1, LANES), m[sz.tail_at : sz.dt_at]], axis=0))
+            both = jnp.concatenate([m[rows - HALO : rows], m[rows : rows + HALO, :STATE]], axis=1)
+            ends.append(both.reshape(HALO, sz.cols, LANES).swapaxes(0, 1).reshape(-1, LANES))
         tail = lax.dynamic_index_in_dim(jnp.stack(ends), lax.bitwise_xor(place, n - 1), 0, keepdims=False)
         halo = lax.ppermute(tail, "seq", onward(1, False)).astype(F32)
     else:
@@ -405,11 +434,12 @@
             ((padded, width), F32),
             ((padded, STATE), F32),
             ((sz.heads, BLOCK), F32),
-            ((n * sz.s_blocks * HALO, LANES), F32),
+            ((n * HALO, STATE), F32),
+            ((edge_rows, LANES), F32),
         ],
         [VMEM] * 9,
         "state",
-    )(dt_bias.reshape(1, -1), a_log.reshape(1, -1), *came, conv_x, conv_b, halo)
+    )(bias, alog, *came, taps_x, taps_b, halo)
 
     if chain:
         cut = sz.x_blocks * STATE
@@ -439,7 +469,7 @@
         "inner",
         flops=1 << 30,
         touched=1 << 22,
-    )(d_skip.reshape(1, -1), *came_c, conv_c, xc, bc, stats, halo)
+    )(skip, *came_c, taps_c, xc, bc, stats, halo)
 
     back = call(
         outer_kernel,
@@ -447,12 +477,13 @@
         [((rows, width), BF16)] * 4,
         [
             ((2 * HALO, sz.cols * LANES), F32),
+            ((edge_rows, LANES), F32),
             ((BLOCK, STATE), BF16),
             ((BLOCK, width), F32),
         ],
         [VMEM] * 14,
         "outer",
-    )(conv_x, conv_b, conv_c, xc, bc, cc, stats, columns, first, first_c, growth, gains, inner, arrived)
+    )(taps_x, taps_b, taps_c, xc, bc, cc, stats, columns, first, first_c, growth, gains, inner, arrived)
     home = [lax.ppermute(back[k], "seq", swap(k)) for k in range(1, n)]
 
     out = call(norm_kernel, sz, [(x_in.shape, BF16)], [], [VMEM] * 6, "norm")(

time: 25.7 us -> 25.8 us (level)
  local copies, waits for them, and re-layouts: 1.33 us -> 0.01 us
  Pallas kernels: 3.66 us -> 4.42 us
  waiting for transfers between devices: 6.04 us -> 6.6 us
    ppermute x3, waiting for transfers between devices: 2.33 us -> 4.05 us  [body(): home = [lax.ppermute(back[k], 'seq', swap(k)) for k in range(1, n)]]
    unnamed x16 -> x4, local copies, waits for them, and re-layouts: 1.33 us -> 0.01 us
    ppermute x1, waiting for transfers between devices: 2.24 us -> 1.35 us  [body(): arrived = lax.ppermute(msg, 'seq', onward(1, True))]
    pallas_call x1 -> x2, Pallas kernels: 1.22 us -> 1.97 us  [the longest x1 1.04 us: body(): call(pack_kernel, sz, [(sz.message, BF16)] * (n - 1) + [to_c] * (n - 1) +...]
    ppermute x6, waiting for transfers between devices: 1.47 us -> 1.2 us  [body(): lax.ppermute(sent[k], 'seq', swap(k % (n - 1) + 1))]
  transfers between devices with their start and end apart: 10 -> 10, of which waited for: 5 -> 6; matrix products, arithmetic and copies ran while one was open for 0% -> 0% of each run, Pallas kernels for 5% -> 8%
where the time goes in v3:
time: 25.8 us; the launch traced here: 25.5 us
  starting transfers between devices  14.4 us (56%)
  waiting for transfers between devices  6.6 us (26%)
  Pallas kernels  4.42 us (17%)
    ppermute x6, starting transfers between devices, body(): lax.ppermute(sent[k], 'seq', swap(k % (n - 1) + 1))  8.2 us
    ppermute x3, waiting for transfers between devices, body(): home = [lax.ppermute(back[k], 'seq', swap(k)) for k in range(1, n)]  4.05 us
    ppermute x3, starting transfers between devices, body(): home = [lax.ppermute(back[k], 'seq', swap(k)) for k in range(1, n)]  3.55 us
    ppermute x1, starting transfers between devices, body(): arrived = lax.ppermute(msg, 'seq', onward(1, True))  2.66 us
    ppermute x1, waiting for transfers between devices, body(): arrived = lax.ppermute(msg, 'seq', onward(1, True))  1.35 us
    ppermute x6, waiting for transfers between devices, body(): lax.ppermute(sent[k], 'seq', swap(k % (n - 1) + 1))  1.2 us
    pallas_call x1, Pallas kernels, body(): call(pack_kernel, sz, [(sz.message, BF16)] * (n - 1) + [to_c] * (n - 1) +...  1.04 us
    pallas_call x1, Pallas kernels, body(): call(own_kernel, sz, [(sz.message, BF16), to_c, ((sz.taps, width), BF16)]...  0.93 us
  transfers between devices with their start and end apart: 10, of which 6 were waited for; matrix products, arithmetic and copies ran while one was open for 0% of the time, Pallas kernels for 8%

profile of v3, /device:TPU:0, one launch (start us, length us, event | category | flops | bytes accessed | tf_op | source)
XLA Modules:
  0.0 25.5 jit_solution(16540602375910238003)
XLA Ops:
  0.0 1.0 %pack.1 = (bf16[72,384]{1,0:T(8,128)(2,1)S(1)}, bf16[72,384]{1,0:T(8,128)(2,1)S(1)}, bf16[72,384]{1,0:T(8,128)(2,1)S(1)}, bf16[64,256]{1,0:T(8,128)(2,1)S(1)}, b...) custom-call(bf16[64,512]{1,0:T(8,128)(2,1)} %x.3, bf16[64,1024]{1,0:T(8,128)(2,1)} %b.3, ...), custom_call_target="tpu_custom_call" | custom-call | tf_op jit(solution)/shard_map/pack/pallas_call | solution.py:388
  1.1 3.0 %collective-permute-start = (bf16[72,384]{1,0:T(8,128)(2,1)S(1)}, bf16[72,384]{1,0:T(8,128)(2,1)S(1)}, u32[]{:S(2)}, u32[]{:S(2)}) collective-permute-start(bf16[72,384]{1,0:T(8,128)(2,1)S(1)} %get-tuple-element.42), channel_id=1, source_target_pairs={{0,2},{2,0},{4,6},{6,4},{8,10},{10,8},{12,14},{14,12},{1,3},{3,1},... | collective-permute-start | bytes 165896 | tf_op jit(solution)/shard_map/ppermute | solution.py:396
  4.1 1.6 %collective-permute-start.1 = (bf16[72,384]{1,0:T(8,128)(2,1)S(1)}, bf16[72,384]{1,0:T(8,128)(2,1)S(1)}, u32[]{:S(2)}, u32[]{:S(2)}) collective-permute-start(bf16[72,384]{1,0:T(8,128)(2,1)S(1)} %get-tuple-element.43), channel_id=1, source_target_pairs={{0,4},{2,6},{4,0},{6,2},{8,12},{10,14},{12,8},{14,10},{1,5},{3,7},... | collective-permute-start | bytes 165896 | tf_op jit(solution)/shard_map/ppermute | solution.py:396
  5.7 0.0 collective-permute-start.2
  5.7 1.9 %collective-permute-start.3 = (bf16[64,256]{1,0:T(8,128)(2,1)S(1)}, bf16[64,256]{1,0:T(8,128)(2,1)S(1)}, u32[]{:S(2)}, u32[]{:S(2)}) collective-permute-start(bf16[64,256]{1,0:T(8,128)(2,1)S(1)} %get-tuple-element.49), channel_id=1, source_target_pairs={{0,2},{2,0},{4,6},{6,4},{8,10},{10,8},{12,14},{14,12},{1,3},{3,1},... | collective-permute-start | bytes 98312 | tf_op jit(solution)/shard_map/ppermute | solution.py:396
  7.6 1.6 %collective-permute-start.4 = (bf16[64,256]{1,0:T(8,128)(2,1)S(1)}, bf16[64,256]{1,0:T(8,128)(2,1)S(1)}, u32[]{:S(2)}, u32[]{:S(2)}) collective-permute-start(bf16[64,256]{1,0:T(8,128)(2,1)S(1)} %get-tuple-element.50), channel_id=1, source_target_pairs={{0,4},{2,6},{4,0},{6,2},{8,12},{10,14},{12,8},{14,10},{1,5},{3,7},... | collective-permute-start | bytes 98312 | tf_op jit(solution)/shard_map/ppermute | solution.py:396
  9.1 0.0 collective-permute-done.m1
  9.2 0.1 collective-permute-start.5
  9.3 0.9 %own.1 = (bf16[72,384]{1,0:T(8,128)(2,1)S(1)}, bf16[64,256]{1,0:T(8,128)(2,1)S(1)}, bf16[4,128]{1,0:T(4,128)(2,1)S(1)}, bf16[4,256]{1,0:T(4,128)(2,1)S(1)}, bf16...) custom-call(bf16[64,512]{1,0:T(8,128)(2,1)} %x.3, bf16[64,1024]{1,0:T(8,128)(2,1)} %b.3, ...), custom_call_target="tpu_custom_call" | custom-call | tf_op jit(solution)/shard_map/own/pallas_call | solution.py:398
  10.2 0.0 collective-permute-done.1.m2
  10.2 0.5 %collective-permute-done.2.m3 = bf16[72,384]{1,0:T(8,128)(2,1)S(1)} collective-permute-done((bf16[72,384]{1,0:T(8,128)(2,1)S(1)}, bf16[72,384]{1,0:T(8,128)(2,1)S(1)}, u32[]{:S(2)}, u32[]{:S(2)}) %collective-permute-start.2) | collective-permute-done | bytes 55328 | tf_op jit(solution)/shard_map/ppermute | solution.py:396
  10.7 0.6 %state.1 = (bf16[272,128]{1,0:T(8,128)(2,1)S(1)}, bf16[256,128]{1,0:T(8,128)(2,1)S(1)}, bf16[256,256]{1,0:T(8,128)(2,1)S(1)}, f32[8,256]{1,0:T(8,128)S(1)}, f32[24,128]{1,0:T(8,128)S(1)}) custom-call(f32[1,8]{1,0:T(1,128)S(1)} %get-tuple-element.39.bias, f32[1,8]{1,0:T(1,128)S(1)} %get-tuple-element.40.alog, bf16[72,384]{1,0:T(8,128)(2,1)S(1)} %get-tuple-element.41.m0, ...), custom_call_target="tpu_custom_call" | custom-call | tf_op jit(solution)/shard_map/state/pallas_call | solution.py:423
  11.4 2.7 %collective-permute-start.6 = (bf16[272,128]{1,0:T(8,128)(2,1)S(1)}, bf16[272,128]{1,0:T(8,128)(2,1)S(1)}, u32[]{:S(2)}, u32[]{:S(2)}) collective-permute-start(bf16[272,128]{1,0:T(8,128)(2,1)S(1)} %get-tuple-element.60), channel_id=1, source_target_pairs={{0,8},{2,10},{4,12},{6,14},{8,0},{10,2},{12,4},{14,6},{1,9},{3,11}... | collective-permute-start | bytes 208904 | tf_op jit(solution)/shard_map/ppermute | solution.py:454
  14.0 0.0 collective-permute-done.3.c1
  14.0 0.0 collective-permute-done.4.c2
  14.0 0.7 %collective-permute-done.5.c3 = bf16[64,256]{1,0:T(8,128)(2,1)S(1)} collective-permute-done((bf16[64,256]{1,0:T(8,128)(2,1)S(1)}, bf16[64,256]{1,0:T(8,128)(2,1)S(1)}, u32[]{:S(2)}, u32[]{:S(2)}) %collective-permute-start.5) | collective-permute-done | bytes 32800 | tf_op jit(solution)/shard_map/ppermute | solution.py:396
  14.7 0.6 %inner.1 = (f32[256,128]{1,0:T(8,128)S(1)}, f32[256,128]{1,0:T(8,128)S(1)}, f32[8,128]{1,0:T(8,128)S(1)}, bf16[256,256]{1,0:T(8,128)(2,1)S(1)}, f32[16,8]{1,0:T(8,128)S(1)}, /*index=5*/f32[16,128]{1,0:T(8,128)S(1)}) custom-call(f32[1,8]{1,0:T(1,128)S(1)} %get-tuple-element.47.skip, bf16[64,256]{1,0:T(8,128)(2,1)S(1)} %get-tuple-element.48.c0, ...), custom_call_target="tpu_custom_call" | custom-call | flops 1073741824 | bytes 4194304 | tf_op jit(solution)/shard_map/inner/pallas_call | solution.py:456
  15.3 1.3 %collective-permute-done.6.arrived = bf16[272,128]{1,0:T(8,128)(2,1)S(1)} collective-permute-done((bf16[272,128]{1,0:T(8,128)(2,1)S(1)}, bf16[272,128]{1,0:T(8,128)(2,1)S(1)}, u32[]{:S(2)}, u32[]{:S(2)}) %collective-permute-start.6) | collective-permute-done | bytes 69664 | tf_op jit(solution)/shard_map/ppermute | solution.py:454
  16.6 0.0 copy-start
  16.6 0.5 %outer.1 = (bf16[64,128]{1,0:T(8,128)(2,1)S(1)}, bf16[64,128]{1,0:T(8,128)(2,1)S(1)}, bf16[64,128]{1,0:T(8,128)(2,1)S(1)}, bf16[64,128]{1,0:T(8,128)(2,1)S(1)}) custom-call(bf16[4,128]{1,0:T(4,128)(2,1)S(1)} %get-tuple-element.36.taps_x, bf16[4,256]{1,0:T(4,128)(2,1)S(1)} %get-tuple-element.37.taps_b, bf16[4,256]{1,0:T(4,128)(2,1)S(1)} %get-tuple-element.38.taps_c, ...), custom_call_target="tpu_custom_call" | custom-call | tf_op jit(solution)/shard_map/outer/pallas_call | solution.py:474
  17.1 1.4 %collective-permute-start.7 = (bf16[64,128]{1,0:T(8,128)(2,1)S(1)}, bf16[64,128]{1,0:T(8,128)(2,1)S(1)}, u32[]{:S(2)}, u32[]{:S(2)}) collective-permute-start(bf16[64,128]{1,0:T(8,128)(2,1)S(1)} %get-tuple-element.62), channel_id=1, source_target_pairs={{0,2},{2,0},{4,6},{6,4},{8,10},{10,8},{12,14},{14,12},{1,3},{3,1},... | collective-permute-start | bytes 49160 | tf_op jit(solution)/shard_map/ppermute | solution.py:487
  18.5 1.6 %collective-permute-start.8 = (bf16[64,128]{1,0:T(8,128)(2,1)S(1)}, bf16[64,128]{1,0:T(8,128)(2,1)S(1)}, u32[]{:S(2)}, u32[]{:S(2)}) collective-permute-start(bf16[64,128]{1,0:T(8,128)(2,1)S(1)} %get-tuple-element.63), channel_id=1, source_target_pairs={{0,4},{2,6},{4,0},{6,2},{8,12},{10,14},{12,8},{14,10},{1,5},{3,7},... | collective-permute-start | bytes 49160 | tf_op jit(solution)/shard_map/ppermute | solution.py:487
  20.1 0.0 copy-start.1
  20.1 0.6 %collective-permute-start.9 = (bf16[64,128]{1,0:T(8,128)(2,1)S(1)}, bf16[64,128]{1,0:T(8,128)(2,1)S(1)}, u32[]{:S(2)}, u32[]{:S(2)}) collective-permute-start(bf16[64,128]{1,0:T(8,128)(2,1)S(1)} %get-tuple-element.64), channel_id=1, source_target_pairs={{0,6},{2,4},{4,2},{6,0},{8,14},{10,12},{12,10},{14,8},{1,7},{3,5},... | collective-permute-start | bytes 49160 | tf_op jit(solution)/shard_map/ppermute | solution.py:487
  20.7 0.2 collective-permute-done.7.r1
  20.9 1.3 %collective-permute-done.8.r2 = bf16[64,128]{1,0:T(8,128)(2,1)S(1)} collective-permute-done((bf16[64,128]{1,0:T(8,128)(2,1)S(1)}, bf16[64,128]{1,0:T(8,128)(2,1)S(1)}, u32[]{:S(2)}, u32[]{:S(2)}) %collective-permute-start.8) | collective-permute-done | bytes 16416 | tf_op jit(solution)/shard_map/ppermute | solution.py:487
  22.2 2.5 %collective-permute-done.9.r3 = bf16[64,128]{1,0:T(8,128)(2,1)S(1)} collective-permute-done((bf16[64,128]{1,0:T(8,128)(2,1)S(1)}, bf16[64,128]{1,0:T(8,128)(2,1)S(1)}, u32[]{:S(2)}, u32[]{:S(2)}) %collective-permute-start.9) | collective-permute-done | bytes 16416 | tf_op jit(solution)/shard_map/ppermute | solution.py:487
  24.7 0.0 copy-done
  24.7 0.0 copy-done.1
  24.7 0.8 %norm.1 = bf16[64,512]{1,0:T(8,128)(2,1)} custom-call(bf16[64,128]{1,0:T(8,128)(2,1)S(1)} %get-tuple-element.61.o0, bf16[64,128]{1,0:T(8,128)(2,1)S(1)} %collective-permute-done.7.r1, bf16[64,128]{1,0:T(8,128)(2,1)S(1)} %collective-permute-done.8.r2, bf16[64,128]{1,0:T(8,128)(2,1)S(1)} %collective-permute-done.9.r3, bf16[64,512]{1,0:T(8,128)(2,1)S(1)} %copy-done, ...), custom_call_target="tpu_custom_call" | custom-call | tf_op jit(solution)/shard_map/norm/pallas_call | solution.py:489
  (1 shorter events, 0.0 us)
Async XLA Ops:
  1.1 8.1 %collective-permute-start = (bf16[72,384]{1,0:T(8,128)(2,1)S(1)}, bf16[72,384]{1,0:T(8,128)(2,1)S(1)}, u32[]{:S(2)}, u32[]{:S(2)}) collective-permute-start(bf16[72,384]{1,0:T(8,128)(2,1)S(1)} %get-tuple-element.42), channel_id=1, source_target_pairs={{0,2},{2,0},{4,6},{6,4},{8,10},{10,8},{12,14},{14,12},{1,3},{3,1},... | collective-permute-start | bytes 165896 | tf_op jit(solution)/shard_map/ppermute | solution.py:396
  4.1 6.1 %collective-permute-start.1 = (bf16[72,384]{1,0:T(8,128)(2,1)S(1)}, bf16[72,384]{1,0:T(8,128)(2,1)S(1)}, u32[]{:S(2)}, u32[]{:S(2)}) collective-permute-start(bf16[72,384]{1,0:T(8,128)(2,1)S(1)} %get-tuple-element.43), channel_id=1, source_target_pairs={{0,4},{2,6},{4,0},{6,2},{8,12},{10,14},{12,8},{14,10},{1,5},{3,7},... | collective-permute-start | bytes 165896 | tf_op jit(solution)/shard_map/ppermute | solution.py:396
  5.7 5.1 %collective-permute-start.2 = (bf16[72,384]{1,0:T(8,128)(2,1)S(1)}, bf16[72,384]{1,0:T(8,128)(2,1)S(1)}, u32[]{:S(2)}, u32[]{:S(2)}) collective-permute-start(bf16[72,384]{1,0:T(8,128)(2,1)S(1)} %get-tuple-element.44), channel_id=1, source_target_pairs={{0,6},{2,4},{4,2},{6,0},{8,14},{10,12},{12,10},{14,8},{1,7},{3,5},... | collective-permute-start | bytes 165896 | tf_op jit(solution)/shard_map/ppermute | solution.py:396
  5.7 8.4 %collective-permute-start.3 = (bf16[64,256]{1,0:T(8,128)(2,1)S(1)}, bf16[64,256]{1,0:T(8,128)(2,1)S(1)}, u32[]{:S(2)}, u32[]{:S(2)}) collective-permute-start(bf16[64,256]{1,0:T(8,128)(2,1)S(1)} %get-tuple-element.49), channel_id=1, source_target_pairs={{0,2},{2,0},{4,6},{6,4},{8,10},{10,8},{12,14},{14,12},{1,3},{3,1},... | collective-permute-start | bytes 98312 | tf_op jit(solution)/shard_map/ppermute | solution.py:396
  7.6 6.5 %collective-permute-start.4 = (bf16[64,256]{1,0:T(8,128)(2,1)S(1)}, bf16[64,256]{1,0:T(8,128)(2,1)S(1)}, u32[]{:S(2)}, u32[]{:S(2)}) collective-permute-start(bf16[64,256]{1,0:T(8,128)(2,1)S(1)} %get-tuple-element.50), channel_id=1, source_target_pairs={{0,4},{2,6},{4,0},{6,2},{8,12},{10,14},{12,8},{14,10},{1,5},{3,7},... | collective-permute-start | bytes 98312 | tf_op jit(solution)/shard_map/ppermute | solution.py:396
  9.2 5.6 %collective-permute-start.5 = (bf16[64,256]{1,0:T(8,128)(2,1)S(1)}, bf16[64,256]{1,0:T(8,128)(2,1)S(1)}, u32[]{:S(2)}, u32[]{:S(2)}) collective-permute-start(bf16[64,256]{1,0:T(8,128)(2,1)S(1)} %get-tuple-element.51), channel_id=1, source_target_pairs={{0,6},{2,4},{4,2},{6,0},{8,14},{10,12},{12,10},{14,8},{1,7},{3,5},... | collective-permute-start | bytes 98312 | tf_op jit(solution)/shard_map/ppermute | solution.py:396
  11.4 5.3 %collective-permute-start.6 = (bf16[272,128]{1,0:T(8,128)(2,1)S(1)}, bf16[272,128]{1,0:T(8,128)(2,1)S(1)}, u32[]{:S(2)}, u32[]{:S(2)}) collective-permute-start(bf16[272,128]{1,0:T(8,128)(2,1)S(1)} %get-tuple-element.60), channel_id=1, source_target_pairs={{0,8},{2,10},{4,12},{6,14},{8,0},{10,2},{12,4},{14,6},{1,9},{3,11}... | collective-permute-start | bytes 208904 | tf_op jit(solution)/shard_map/ppermute | solution.py:454
  16.6 8.1 %copy-start = (bf16[64,512]{1,0:T(8,128)(2,1)S(1)}, bf16[64,512]{1,0:T(8,128)(2,1)}, u32[]{:S(2)}) copy-start(bf16[64,512]{1,0:T(8,128)(2,1)} %z.1) | copy-start | bytes 196612
  17.1 3.8 %collective-permute-start.7 = (bf16[64,128]{1,0:T(8,128)(2,1)S(1)}, bf16[64,128]{1,0:T(8,128)(2,1)S(1)}, u32[]{:S(2)}, u32[]{:S(2)}) collective-permute-start(bf16[64,128]{1,0:T(8,128)(2,1)S(1)} %get-tuple-element.62), channel_id=1, source_target_pairs={{0,2},{2,0},{4,6},{6,4},{8,10},{10,8},{12,14},{14,12},{1,3},{3,1},... | collective-permute-start | bytes 49160 | tf_op jit(solution)/shard_map/ppermute | solution.py:487
  18.5 3.7 %collective-permute-start.8 = (bf16[64,128]{1,0:T(8,128)(2,1)S(1)}, bf16[64,128]{1,0:T(8,128)(2,1)S(1)}, u32[]{:S(2)}, u32[]{:S(2)}) collective-permute-start(bf16[64,128]{1,0:T(8,128)(2,1)S(1)} %get-tuple-element.63), channel_id=1, source_target_pairs={{0,4},{2,6},{4,0},{6,2},{8,12},{10,14},{12,8},{14,10},{1,5},{3,7},... | collective-permute-start | bytes 49160 | tf_op jit(solution)/shard_map/ppermute | solution.py:487
  20.1 4.6 %copy-start.1 = (f32[512]{0:T(512)S(1)}, f32[512]{0:T(512)}, u32[]{:S(2)}) copy-start(f32[512]{0:T(512)} %param.23) | copy-start | bytes 6148
  20.1 4.6 %collective-permute-start.9 = (bf16[64,128]{1,0:T(8,128)(2,1)S(1)}, bf16[64,128]{1,0:T(8,128)(2,1)S(1)}, u32[]{:S(2)}, u32[]{:S(2)}) collective-permute-start(bf16[64,128]{1,0:T(8,128)(2,1)S(1)} %get-tuple-element.64), channel_id=1, source_target_pairs={{0,6},{2,4},{4,2},{6,0},{8,14},{10,12},{12,10},{14,8},{1,7},{3,5},... | collective-permute-start | bytes 49160 | tf_op jit(solution)/shard_map/ppermute | solution.py:487

commit v4 on v3

--- a/solution.py
+++ b/solution.py
@@ -13,6 +13,7 @@
 LANES = 128
 HALO = 8
 EDGE = 16
+ORDER = (3, 1, 2)
 F32 = jnp.float32
 BF16 = jnp.bfloat16
 VMEM = pl.BlockSpec(memory_space=pltpu.VMEM)
@@ -82,29 +83,14 @@
     ]
 
 
-def pack_kernel(sz, x, b, c, dt, m1, m2, m3, c1, c2, c3, dt_rows, dt_here, sem):
+def pack_kernel(sz, x, b, c, dt, conv_x, conv_b, conv_c, bias, alog, skip,
+                m0, m1, m2, m3, c0, c1, c2, c3, taps_x, taps_b, taps_c, bias_here, alog_here, skip_here,
+                dt_here, sem):
     place = place_of(sz)
     pairs = [(dt, dt_here)]
-    for k, m, mc in ((3, m3, c3), (2, m2, c2), (1, m1, c1)):
+    for k, m, mc in ((3, m3, c3), (1, m1, c1), (2, m2, c2), (0, m0, c0)):
         pairs += message_parts(sz, lax.bitwise_xor(place, k), x, b, c, m, mc)
-    copies = fetch_all(pairs, sem)
-    copies[0].wait()
-    here = dt_here[...].astype(F32)
-    twice = jnp.concatenate([here, here], axis=1)
-    spot = lax.broadcasted_iota(jnp.int32, twice.shape, 1)
-    mine = lax.div(spot, sz.rows) == lax.rem(place, 2)
-    spread = jnp.where(mine, twice, 0.0).astype(BF16)
-    dt_rows[...] = spread
-    for m in (m1, m2, m3):
-        m[sz.rows : sz.rows + sz.heads, sz.dt_lanes] = spread
-    for copy in copies[1:]:
-        copy.wait()
-
-
-def own_kernel(sz, x, b, c, conv_x, conv_b, conv_c, bias, alog, skip, dt_rows,
-               m0, c0, taps_x, taps_b, taps_c, bias_here, alog_here, skip_here, sem):
-    place = place_of(sz)
-    pairs = message_parts(sz, place, x, b, c, m0, c0) + [
+    pairs += [
         (lanes_of(conv_x, place, sz.x_blocks * LANES), taps_x),
         (lanes_of(conv_b, place, STATE), taps_b),
         (lanes_of(conv_c, place, STATE), taps_c),
@@ -113,8 +99,15 @@
         (skip, skip_here),
     ]
     copies = fetch_all(pairs, sem)
-    m0[sz.rows : sz.rows + sz.heads, sz.dt_lanes] = dt_rows[...]
-    for copy in copies:
+    copies[0].wait()
+    here = dt_here[...].astype(F32)
+    twice = jnp.concatenate([here, here], axis=1)
+    spot = lax.broadcasted_iota(jnp.int32, twice.shape, 1)
+    mine = lax.div(spot, sz.rows) == lax.rem(place, 2)
+    spread = jnp.where(mine, twice, 0.0).astype(BF16)
+    for m in (m0, m1, m2, m3):
+        m[sz.rows : sz.rows + sz.heads, sz.dt_lanes] = spread
+    for copy in copies[1:]:
         copy.wait()
 
 
@@ -149,7 +142,7 @@
     return jnp.sum(jnp.where(spot == line + head0, row, 0.0), axis=1, keepdims=True)
 
 
-def state_kernel(sz, bias, alog, m0, m1, m2, m3, taps_x, taps_b, halo,
+def state_kernel(sz, bias, alog, m0, m3, m1, m2, taps_x, taps_b, halo,
                  msg, xc, bc, stats, first, xs, bs, dts, tails, packed):
     chain = sz.blocks > 2
     place = place_of(sz)
@@ -231,7 +224,7 @@
     msg[base:, :] = packed[...].astype(msg.dtype)
 
 
-def inner_kernel(sz, skip, c0, c1, c2, c3, taps_c, xc, bc, stats, halo,
+def inner_kernel(sz, skip, c0, c3, c1, c2, taps_c, xc, bc, stats, halo,
                  out, growth, gains, cc, columns, first_c, cs, turned):
     chain = sz.blocks > 2
     place = place_of(sz)
@@ -342,7 +335,7 @@
         o[...] = total[pl.ds(pl.multiple_of(target * rows, 8), rows), :].astype(BF16)
 
 
-def norm_kernel(sz, o0, r1, r2, r3, z, gain, out):
+def norm_kernel(sz, o0, r3, r1, r2, z, gain, out):
     place = place_of(sz)
     width = sz.x_blocks * LANES
     for k, part in enumerate((o0, r1, r2, r3)):
@@ -380,32 +373,34 @@
         pairs = [(i, i + n * k) for i in range(seq_total)]
         return [(i, j % seq_total) for i, j in pairs if wrap or j < seq_total]
 
+    def ordered(arrays):
+        return [arrays[0]] + [arrays[k] for k in ORDER]
+
     def stay(*arrays):
         return [pltpu.with_memory_space_constraint(a, pltpu.HBM) for a in arrays]
 
     width = sz.x_blocks * LANES
     to_c = ((rows, STATE), BF16)
-    *sent, dt_rows = call(
+    vectors = [v.reshape(1, -1) for v in (dt_bias, a_log, d_skip)]
+    *sent, taps_x, taps_b, taps_c, bias, alog, skip = call(
         pack_kernel,
         sz,
-        [(sz.message, BF16)] * (n - 1) + [to_c] * (n - 1) + [((sz.heads, LANES), BF16)],
-        [((sz.heads, rows), BF16), pltpu.SemaphoreType.DMA((1 + 4 * (n - 1),))],
-        [HBM] * 4,
-        "pack",
-    )(*stay(x_in, b_in, c_in, dt_raw.T))
-    arrivals = [lax.ppermute(sent[k], "seq", swap(k % (n - 1) + 1)) for k in range(2 * (n - 1))]
-    vectors = [v.reshape(1, -1) for v in (dt_bias, a_log, d_skip)]
-    m0, c0, taps_x, taps_b, taps_c, bias, alog, skip = call(
-        own_kernel,
-        sz,
-        [(sz.message, BF16), to_c, ((sz.taps, width), BF16)]
+        [(sz.message, BF16)] * n
+        + [to_c] * n
+        + [((sz.taps, width), BF16)]
         + [((sz.taps, STATE), BF16)] * 2
         + [((1, sz.heads), F32)] * 3,
-        [pltpu.SemaphoreType.DMA((10,))],
-        [HBM] * 9 + [VMEM],
-        "own",
-    )(*stay(x_in, b_in, c_in, conv_x, conv_b, conv_c, *vectors), dt_rows)
-    came, came_c = [m0, *arrivals[: n - 1]], [c0, *arrivals[n - 1 :]]
+        [((sz.heads, rows), BF16), pltpu.SemaphoreType.DMA((7 + 4 * n,))],
+        [HBM] * 10,
+        "pack",
+    )(*stay(x_in, b_in, c_in, dt_raw.T, conv_x, conv_b, conv_c, *vectors))
+    arrivals = {}
+    for k in ORDER:
+        arrivals[k] = lax.ppermute(sent[k], "seq", swap(k))
+    for k in ORDER:
+        arrivals[n + k] = lax.ppermute(sent[n + k], "seq", swap(k))
+    came = [sent[0]] + [arrivals[k] for k in range(1, n)]
+    came_c = [sent[n]] + [arrivals[n + k] for k in range(1, n)]
 
     padded = BLOCK + HALO
     edge_rows = sz.halo_rows
@@ -439,7 +434,7 @@
         ],
         [VMEM] * 9,
         "state",
-    )(bias, alog, *came, taps_x, taps_b, halo)
+    )(bias, alog, *ordered(came), taps_x, taps_b, halo)
 
     if chain:
         cut = sz.x_blocks * STATE
@@ -469,7 +464,7 @@
         "inner",
         flops=1 << 30,
         touched=1 << 22,
-    )(skip, *came_c, taps_c, xc, bc, stats, halo)
+    )(skip, *ordered(came_c), taps_c, xc, bc, stats, halo)
 
     back = call(
         outer_kernel,
@@ -484,10 +479,12 @@
         [VMEM] * 14,
         "outer",
     )(taps_x, taps_b, taps_c, xc, bc, cc, stats, columns, first, first_c, growth, gains, inner, arrived)
-    home = [lax.ppermute(back[k], "seq", swap(k)) for k in range(1, n)]
+    home = list(back)
+    for k in ORDER:
+        home[k] = lax.ppermute(back[k], "seq", swap(k))
 
     out = call(norm_kernel, sz, [(x_in.shape, BF16)], [], [VMEM] * 6, "norm")(
-        back[0], *home, z_in, norm_gain.reshape(1, -1)
+        *ordered(home), z_in, norm_gain.reshape(1, -1)
     )
     return out[0]
 

time: 25.8 us -> 23.9 us (0.926)
  waiting for transfers between devices: 6.6 us -> 5.34 us
  Pallas kernels: 4.42 us -> 3.63 us
  starting transfers between devices: 14.4 us -> 14.7 us
    ppermute x9, waiting for transfers between devices: 5.26 us -> 3.6 us  [the longest x3 3.09 us: body(): home[k] = lax.ppermute(back[k], 'seq', swap(k))]
    pallas_call x2 -> x1, Pallas kernels: 1.97 us -> 1.18 us  [body(): call(pack_kernel, sz, [(sz.message, BF16)] * n + [to_c] * n + [((sz.taps,...]
    ppermute x1, waiting for transfers between devices: 1.35 us -> 1.74 us  [body(): arrived = lax.ppermute(msg, 'seq', onward(1, True))]
    ppermute x9, starting transfers between devices: 11.7 us -> 12.1 us  [the longest x3 4.69 us: body(): arrivals[k] = lax.ppermute(sent[k], 'seq', swap(k))]
  transfers between devices with their start and end apart: 10 -> 10, of which waited for: 6 -> 6; matrix products, arithmetic and copies ran while one was open for 0% -> 0% of each run, Pallas kernels for 8% -> 5%
where the time goes in v4:
time: 23.9 us; the launch traced here: 23.7 us
  starting transfers between devices  14.7 us (62%)
  waiting for transfers between devices  5.34 us (22%)
  Pallas kernels  3.63 us (15%)
    ppermute x3, starting transfers between devices, body(): arrivals[k] = lax.ppermute(sent[k], 'seq', swap(k))  4.69 us
    ppermute x3, starting transfers between devices, body(): arrivals[n + k] = lax.ppermute(sent[n + k], 'seq', swap(k))  3.83 us
    ppermute x3, starting transfers between devices, body(): home[k] = lax.ppermute(back[k], 'seq', swap(k))  3.55 us
    ppermute x3, waiting for transfers between devices, body(): home[k] = lax.ppermute(back[k], 'seq', swap(k))  3.09 us
    ppermute x1, starting transfers between devices, body(): arrived = lax.ppermute(msg, 'seq', onward(1, True))  2.65 us
    ppermute x1, waiting for transfers between devices, body(): arrived = lax.ppermute(msg, 'seq', onward(1, True))  1.74 us
    pallas_call x1, Pallas kernels, body(): call(pack_kernel, sz, [(sz.message, BF16)] * n + [to_c] * n + [((sz.taps,...  1.18 us
    pallas_call x1, Pallas kernels, body(): call(norm_kernel, sz, [(x_in.shape, BF16)], [], [VMEM] * 6, 'norm')  0.77 us
  transfers between devices with their start and end apart: 10, of which 6 were waited for; matrix products, arithmetic and copies ran while one was open for 0% of the time, Pallas kernels for 5%

profile of v4, /device:TPU:0, one launch (start us, length us, event | category | flops | bytes accessed | tf_op | source)
XLA Modules:
  0.0 23.7 jit_solution(13000781921609539281)
XLA Ops:
  0.0 1.2 %pack.1 = (bf16[72,384]{1,0:T(8,128)(2,1)S(1)}, bf16[72,384]{1,0:T(8,128)(2,1)S(1)}, bf16[72,384]{1,0:T(8,128)(2,1)S(1)}, bf16[72,384]{1,0:T(8,128)(2,1)S(1)}, b...) custom-call(bf16[64,512]{1,0:T(8,128)(2,1)} %x.1, ...), custom_call_target="tpu_custom_call" | custom-call | tf_op jit(solution)/shard_map/pack/pallas_call | solution.py:385
  1.2 4.0 %collective-permute-start = (bf16[72,384]{1,0:T(8,128)(2,1)S(1)}, bf16[72,384]{1,0:T(8,128)(2,1)S(1)}, u32[]{:S(2)}, u32[]{:S(2)}) collective-permute-start(bf16[72,384]{1,0:T(8,128)(2,1)S(1)} %get-tuple-element.40), channel_id=1, source_target_pairs={{0,6},{2,4},{4,2},{6,0},{8,14},{10,12},{12,10},{14,8},{1,7},{3,5},... | collective-permute-start | bytes 165896 | tf_op jit(solution)/shard_map/ppermute | solution.py:399
  5.2 0.5 %collective-permute-start.1 = (bf16[72,384]{1,0:T(8,128)(2,1)S(1)}, bf16[72,384]{1,0:T(8,128)(2,1)S(1)}, u32[]{:S(2)}, u32[]{:S(2)}) collective-permute-start(bf16[72,384]{1,0:T(8,128)(2,1)S(1)} %get-tuple-element.41), channel_id=1, source_target_pairs={{0,2},{2,0},{4,6},{6,4},{8,10},{10,8},{12,14},{14,12},{1,3},{3,1},... | collective-permute-start | bytes 165896 | tf_op jit(solution)/shard_map/ppermute | solution.py:399
  5.8 0.1 collective-permute-start.2
  5.9 2.8 %collective-permute-start.3 = (bf16[64,256]{1,0:T(8,128)(2,1)S(1)}, bf16[64,256]{1,0:T(8,128)(2,1)S(1)}, u32[]{:S(2)}, u32[]{:S(2)}) collective-permute-start(bf16[64,256]{1,0:T(8,128)(2,1)S(1)} %get-tuple-element.47), channel_id=1, source_target_pairs={{0,6},{2,4},{4,2},{6,0},{8,14},{10,12},{12,10},{14,8},{1,7},{3,5},... | collective-permute-start | bytes 98312 | tf_op jit(solution)/shard_map/ppermute | solution.py:401
  8.7 0.5 %collective-permute-start.4 = (bf16[64,256]{1,0:T(8,128)(2,1)S(1)}, bf16[64,256]{1,0:T(8,128)(2,1)S(1)}, u32[]{:S(2)}, u32[]{:S(2)}) collective-permute-start(bf16[64,256]{1,0:T(8,128)(2,1)S(1)} %get-tuple-element.48), channel_id=1, source_target_pairs={{0,2},{2,0},{4,6},{6,4},{8,10},{10,8},{12,14},{14,12},{1,3},{3,1},... | collective-permute-start | bytes 98312 | tf_op jit(solution)/shard_map/ppermute | solution.py:401
  9.3 0.0 collective-permute-done.m3
  9.3 0.4 %collective-permute-start.5 = (bf16[64,256]{1,0:T(8,128)(2,1)S(1)}, bf16[64,256]{1,0:T(8,128)(2,1)S(1)}, u32[]{:S(2)}, u32[]{:S(2)}) collective-permute-start(bf16[64,256]{1,0:T(8,128)(2,1)S(1)} %get-tuple-element.49), channel_id=1, source_target_pairs={{0,4},{2,6},{4,0},{6,2},{8,12},{10,14},{12,8},{14,10},{1,5},{3,7},... | collective-permute-start | bytes 98312 | tf_op jit(solution)/shard_map/ppermute | solution.py:401
  9.7 0.0 collective-permute-done.1.m1
  9.7 0.2 collective-permute-done.2.m2
  9.9 0.6 %state.1 = (bf16[272,128]{1,0:T(8,128)(2,1)S(1)}, bf16[256,128]{1,0:T(8,128)(2,1)S(1)}, bf16[256,256]{1,0:T(8,128)(2,1)S(1)}, f32[8,256]{1,0:T(8,128)S(1)}, f32[24,128]{1,0:T(8,128)S(1)}) custom-call(f32[1,8]{1,0:T(1,128)S(1)} %get-tuple-element.37.bias, f32[1,8]{1,0:T(1,128)S(1)} %get-tuple-element.38.alog, bf16[72,384]{1,0:T(8,128)(2,1)S(1)} %get-tuple-element.39.m0, ...), custom_call_target="tpu_custom_call" | custom-call | tf_op jit(solution)/shard_map/state/pallas_call | solution.py:418
  10.6 2.7 %collective-permute-start.6 = (bf16[272,128]{1,0:T(8,128)(2,1)S(1)}, bf16[272,128]{1,0:T(8,128)(2,1)S(1)}, u32[]{:S(2)}, u32[]{:S(2)}) collective-permute-start(bf16[272,128]{1,0:T(8,128)(2,1)S(1)} %get-tuple-element.58), channel_id=1, source_target_pairs={{0,8},{2,10},{4,12},{6,14},{8,0},{10,2},{12,4},{14,6},{1,9},{3,11}... | collective-permute-start | bytes 208904 | tf_op jit(solution)/shard_map/ppermute | solution.py:449
  13.2 0.0 collective-permute-done.3.c3
  13.2 0.0 collective-permute-done.4.c1
  13.2 0.3 %collective-permute-done.5.c2 = bf16[64,256]{1,0:T(8,128)(2,1)S(1)} collective-permute-done((bf16[64,256]{1,0:T(8,128)(2,1)S(1)}, bf16[64,256]{1,0:T(8,128)(2,1)S(1)}, u32[]{:S(2)}, u32[]{:S(2)}) %collective-permute-start.5) | collective-permute-done | bytes 32800 | tf_op jit(solution)/shard_map/ppermute | solution.py:401
  13.5 0.6 %inner.1 = (f32[256,128]{1,0:T(8,128)S(1)}, f32[256,128]{1,0:T(8,128)S(1)}, f32[8,128]{1,0:T(8,128)S(1)}, bf16[256,256]{1,0:T(8,128)(2,1)S(1)}, f32[16,8]{1,0:T(8,128)S(1)}, /*index=5*/f32[16,128]{1,0:T(8,128)S(1)}) custom-call(f32[1,8]{1,0:T(1,128)S(1)} %get-tuple-element.45.skip, bf16[64,256]{1,0:T(8,128)(2,1)S(1)} %get-tuple-element.46.c0, ...), custom_call_target="tpu_custom_call" | custom-call | flops 1073741824 | bytes 4194304 | tf_op jit(solution)/shard_map/inner/pallas_call | solution.py:451
  14.1 1.7 %collective-permute-done.6.arrived = bf16[272,128]{1,0:T(8,128)(2,1)S(1)} collective-permute-done((bf16[272,128]{1,0:T(8,128)(2,1)S(1)}, bf16[272,128]{1,0:T(8,128)(2,1)S(1)}, u32[]{:S(2)}, u32[]{:S(2)}) %collective-permute-start.6) | collective-permute-done | bytes 69664 | tf_op jit(solution)/shard_map/ppermute | solution.py:449
  15.9 0.0 copy-start
  15.9 0.5 %outer.1 = (bf16[64,128]{1,0:T(8,128)(2,1)S(1)}, bf16[64,128]{1,0:T(8,128)(2,1)S(1)}, bf16[64,128]{1,0:T(8,128)(2,1)S(1)}, bf16[64,128]{1,0:T(8,128)(2,1)S(1)}) custom-call(bf16[4,128]{1,0:T(4,128)(2,1)S(1)} %get-tuple-element.34.taps_x, bf16[4,256]{1,0:T(4,128)(2,1)S(1)} %get-tuple-element.35.taps_b, bf16[4,256]{1,0:T(4,128)(2,1)S(1)} %get-tuple-element.36.taps_c, ...), custom_call_target="tpu_custom_call" | custom-call | tf_op jit(solution)/shard_map/outer/pallas_call | solution.py:469
  16.3 2.4 %collective-permute-start.7 = (bf16[64,128]{1,0:T(8,128)(2,1)S(1)}, bf16[64,128]{1,0:T(8,128)(2,1)S(1)}, u32[]{:S(2)}, u32[]{:S(2)}) collective-permute-start(bf16[64,128]{1,0:T(8,128)(2,1)S(1)} %get-tuple-element.60), channel_id=1, source_target_pairs={{0,6},{2,4},{4,2},{6,0},{8,14},{10,12},{12,10},{14,8},{1,7},{3,5},... | collective-permute-start | bytes 49160 | tf_op jit(solution)/shard_map/ppermute | solution.py:484
  18.7 0.5 %collective-permute-start.8 = (bf16[64,128]{1,0:T(8,128)(2,1)S(1)}, bf16[64,128]{1,0:T(8,128)(2,1)S(1)}, u32[]{:S(2)}, u32[]{:S(2)}) collective-permute-start(bf16[64,128]{1,0:T(8,128)(2,1)S(1)} %get-tuple-element.61), channel_id=1, source_target_pairs={{0,2},{2,0},{4,6},{6,4},{8,10},{10,8},{12,14},{14,12},{1,3},{3,1},... | collective-permute-start | bytes 49160 | tf_op jit(solution)/shard_map/ppermute | solution.py:484
  19.2 0.0 copy-start.1
  19.2 0.7 %collective-permute-start.9 = (bf16[64,128]{1,0:T(8,128)(2,1)S(1)}, bf16[64,128]{1,0:T(8,128)(2,1)S(1)}, u32[]{:S(2)}, u32[]{:S(2)}) collective-permute-start(bf16[64,128]{1,0:T(8,128)(2,1)S(1)} %get-tuple-element.62), channel_id=1, source_target_pairs={{0,4},{2,6},{4,0},{6,2},{8,12},{10,14},{12,8},{14,10},{1,5},{3,7},... | collective-permute-start | bytes 49160 | tf_op jit(solution)/shard_map/ppermute | solution.py:484
  19.9 1.1 %collective-permute-done.7.r3 = bf16[64,128]{1,0:T(8,128)(2,1)S(1)} collective-permute-done((bf16[64,128]{1,0:T(8,128)(2,1)S(1)}, bf16[64,128]{1,0:T(8,128)(2,1)S(1)}, u32[]{:S(2)}, u32[]{:S(2)}) %collective-permute-start.7) | collective-permute-done | bytes 16416 | tf_op jit(solution)/shard_map/ppermute | solution.py:484
  21.0 1.4 %collective-permute-done.8.r1 = bf16[64,128]{1,0:T(8,128)(2,1)S(1)} collective-permute-done((bf16[64,128]{1,0:T(8,128)(2,1)S(1)}, bf16[64,128]{1,0:T(8,128)(2,1)S(1)}, u32[]{:S(2)}, u32[]{:S(2)}) %collective-permute-start.8) | collective-permute-done | bytes 16416 | tf_op jit(solution)/shard_map/ppermute | solution.py:484
  22.4 0.5 %collective-permute-done.9.r2 = bf16[64,128]{1,0:T(8,128)(2,1)S(1)} collective-permute-done((bf16[64,128]{1,0:T(8,128)(2,1)S(1)}, bf16[64,128]{1,0:T(8,128)(2,1)S(1)}, u32[]{:S(2)}, u32[]{:S(2)}) %collective-permute-start.9) | collective-permute-done | bytes 16416 | tf_op jit(solution)/shard_map/ppermute | solution.py:484
  23.0 0.0 copy-done
  23.0 0.0 copy-done.1
  23.0 0.8 %norm.1 = bf16[64,512]{1,0:T(8,128)(2,1)} custom-call(bf16[64,128]{1,0:T(8,128)(2,1)S(1)} %get-tuple-element.59.o0, bf16[64,128]{1,0:T(8,128)(2,1)S(1)} %collective-permute-done.7.r3, bf16[64,128]{1,0:T(8,128)(2,1)S(1)} %collective-permute-done.8.r1, bf16[64,128]{1,0:T(8,128)(2,1)S(1)} %collective-permute-done.9.r2, bf16[64,512]{1,0:T(8,128)(2,1)S(1)} %copy-done, ...), custom_call_target="tpu_custom_call" | custom-call | tf_op jit(solution)/shard_map/norm/pallas_call | solution.py:486
  (1 shorter events, 0.0 us)
Async XLA Ops:
  1.2 8.1 %collective-permute-start = (bf16[72,384]{1,0:T(8,128)(2,1)S(1)}, bf16[72,384]{1,0:T(8,128)(2,1)S(1)}, u32[]{:S(2)}, u32[]{:S(2)}) collective-permute-start(bf16[72,384]{1,0:T(8,128)(2,1)S(1)} %get-tuple-element.40), channel_id=1, source_target_pairs={{0,6},{2,4},{4,2},{6,0},{8,14},{10,12},{12,10},{14,8},{1,7},{3,5},... | collective-permute-start | bytes 165896 | tf_op jit(solution)/shard_map/ppermute | solution.py:399
  5.2 4.5 %collective-permute-start.1 = (bf16[72,384]{1,0:T(8,128)(2,1)S(1)}, bf16[72,384]{1,0:T(8,128)(2,1)S(1)}, u32[]{:S(2)}, u32[]{:S(2)}) collective-permute-start(bf16[72,384]{1,0:T(8,128)(2,1)S(1)} %get-tuple-element.41), channel_id=1, source_target_pairs={{0,2},{2,0},{4,6},{6,4},{8,10},{10,8},{12,14},{14,12},{1,3},{3,1},... | collective-permute-start | bytes 165896 | tf_op jit(solution)/shard_map/ppermute | solution.py:399
  5.8 4.2 %collective-permute-start.2 = (bf16[72,384]{1,0:T(8,128)(2,1)S(1)}, bf16[72,384]{1,0:T(8,128)(2,1)S(1)}, u32[]{:S(2)}, u32[]{:S(2)}) collective-permute-start(bf16[72,384]{1,0:T(8,128)(2,1)S(1)} %get-tuple-element.42), channel_id=1, source_target_pairs={{0,4},{2,6},{4,0},{6,2},{8,12},{10,14},{12,8},{14,10},{1,5},{3,7},... | collective-permute-start | bytes 165896 | tf_op jit(solution)/shard_map/ppermute | solution.py:399
  5.9 7.4 %collective-permute-start.3 = (bf16[64,256]{1,0:T(8,128)(2,1)S(1)}, bf16[64,256]{1,0:T(8,128)(2,1)S(1)}, u32[]{:S(2)}, u32[]{:S(2)}) collective-permute-start(bf16[64,256]{1,0:T(8,128)(2,1)S(1)} %get-tuple-element.47), channel_id=1, source_target_pairs={{0,6},{2,4},{4,2},{6,0},{8,14},{10,12},{12,10},{14,8},{1,7},{3,5},... | collective-permute-start | bytes 98312 | tf_op jit(solution)/shard_map/ppermute | solution.py:401
  8.7 4.5 %collective-permute-start.4 = (bf16[64,256]{1,0:T(8,128)(2,1)S(1)}, bf16[64,256]{1,0:T(8,128)(2,1)S(1)}, u32[]{:S(2)}, u32[]{:S(2)}) collective-permute-start(bf16[64,256]{1,0:T(8,128)(2,1)S(1)} %get-tuple-element.48), channel_id=1, source_target_pairs={{0,2},{2,0},{4,6},{6,4},{8,10},{10,8},{12,14},{14,12},{1,3},{3,1},... | collective-permute-start | bytes 98312 | tf_op jit(solution)/shard_map/ppermute | solution.py:401
  9.3 4.3 %collective-permute-start.5 = (bf16[64,256]{1,0:T(8,128)(2,1)S(1)}, bf16[64,256]{1,0:T(8,128)(2,1)S(1)}, u32[]{:S(2)}, u32[]{:S(2)}) collective-permute-start(bf16[64,256]{1,0:T(8,128)(2,1)S(1)} %get-tuple-element.49), channel_id=1, source_target_pairs={{0,4},{2,6},{4,0},{6,2},{8,12},{10,14},{12,8},{14,10},{1,5},{3,7},... | collective-permute-start | bytes 98312 | tf_op jit(solution)/shard_map/ppermute | solution.py:401
  10.6 5.3 %collective-permute-start.6 = (bf16[272,128]{1,0:T(8,128)(2,1)S(1)}, bf16[272,128]{1,0:T(8,128)(2,1)S(1)}, u32[]{:S(2)}, u32[]{:S(2)}) collective-permute-start(bf16[272,128]{1,0:T(8,128)(2,1)S(1)} %get-tuple-element.58), channel_id=1, source_target_pairs={{0,8},{2,10},{4,12},{6,14},{8,0},{10,2},{12,4},{14,6},{1,9},{3,11}... | collective-permute-start | bytes 208904 | tf_op jit(solution)/shard_map/ppermute | solution.py:449
  15.9 7.1 %copy-start = (bf16[64,512]{1,0:T(8,128)(2,1)S(1)}, bf16[64,512]{1,0:T(8,128)(2,1)}, u32[]{:S(2)}) copy-start(bf16[64,512]{1,0:T(8,128)(2,1)} %z.1) | copy-start | bytes 196612
  16.3 4.7 %collective-permute-start.7 = (bf16[64,128]{1,0:T(8,128)(2,1)S(1)}, bf16[64,128]{1,0:T(8,128)(2,1)S(1)}, u32[]{:S(2)}, u32[]{:S(2)}) collective-permute-start(bf16[64,128]{1,0:T(8,128)(2,1)S(1)} %get-tuple-element.60), channel_id=1, source_target_pairs={{0,6},{2,4},{4,2},{6,0},{8,14},{10,12},{12,10},{14,8},{1,7},{3,5},... | collective-permute-start | bytes 49160 | tf_op jit(solution)/shard_map/ppermute | solution.py:484
  18.7 3.7 %collective-permute-start.8 = (bf16[64,128]{1,0:T(8,128)(2,1)S(1)}, bf16[64,128]{1,0:T(8,128)(2,1)S(1)}, u32[]{:S(2)}, u32[]{:S(2)}) collective-permute-start(bf16[64,128]{1,0:T(8,128)(2,1)S(1)} %get-tuple-element.61), channel_id=1, source_target_pairs={{0,2},{2,0},{4,6},{6,4},{8,10},{10,8},{12,14},{14,12},{1,3},{3,1},... | collective-permute-start | bytes 49160 | tf_op jit(solution)/shard_map/ppermute | solution.py:484
  19.2 3.7 %copy-start.1 = (f32[512]{0:T(512)S(1)}, f32[512]{0:T(512)}, u32[]{:S(2)}) copy-start(f32[512]{0:T(512)} %param.23) | copy-start | bytes 6148
  19.2 3.7 %collective-permute-start.9 = (bf16[64,128]{1,0:T(8,128)(2,1)S(1)}, bf16[64,128]{1,0:T(8,128)(2,1)S(1)}, u32[]{:S(2)}, u32[]{:S(2)}) collective-permute-start(bf16[64,128]{1,0:T(8,128)(2,1)S(1)} %get-tuple-element.62), channel_id=1, source_target_pairs={{0,4},{2,6},{4,0},{6,2},{8,12},{10,14},{12,8},{14,10},{1,5},{3,7},... | collective-permute-start | bytes 49160 | tf_op jit(solution)/shard_map/ppermute | solution.py:484

commit v5 on v4

--- a/solution.py
+++ b/solution.py
@@ -14,6 +14,8 @@
 HALO = 8
 EDGE = 16
 ORDER = (3, 1, 2)
+RETURN = (3, 1, 2)
+SPLIT = (1, 2)
 F32 = jnp.float32
 BF16 = jnp.bfloat16
 VMEM = pl.BlockSpec(memory_space=pltpu.VMEM)
@@ -40,7 +42,7 @@
         self.s_blocks = STATE // LANES
         self.base = self.x_blocks + self.s_blocks
         self.cols = self.base + self.s_blocks
-        self.message = (self.rows + max(HALO, self.heads), self.base * LANES)
+        self.high = self.rows + max(HALO, self.heads)
         self.dt_lanes = slice((self.base - 1) * LANES, self.base * LANES)
         self.halo_rows = -(-self.cols * (taps - 1) // 16) * 16
         self.pad_heads = max(8, self.per_group)
@@ -57,6 +59,10 @@
     return lax.rem(lax.axis_index("seq"), sz.places)
 
 
+def by_partner(own, others, order):
+    return [own] + [others[order.index(k)] for k in range(1, len(order) + 1)]
+
+
 def silu_half(half):
     return half + half * jnp.tanh(half)
 
@@ -72,24 +78,33 @@
     return copies
 
 
+def c_part(sz, k, m, extra):
+    if k in SPLIT:
+        return extra[SPLIT.index(k)]
+    return m.at[0 : sz.rows, sz.base * LANES :]
+
+
 def message_parts(sz, group, x, b, c, m, mc):
     rows, wide = sz.rows, sz.x_blocks * LANES
     tail = lanes_of(c, group, STATE).at[rows - HALO :, :]
     return [
         (lanes_of(x, group, wide), m.at[0:rows, 0:wide]),
-        (lanes_of(b, group, STATE), m.at[0:rows, wide:]),
+        (lanes_of(b, group, STATE), m.at[0:rows, wide : sz.base * LANES]),
         (tail, m.at[rows : rows + HALO, 0:STATE]),
         (lanes_of(c, group, STATE), mc),
     ]
 
 
 def pack_kernel(sz, x, b, c, dt, conv_x, conv_b, conv_c, bias, alog, skip,
-                m0, m1, m2, m3, c0, c1, c2, c3, taps_x, taps_b, taps_c, bias_here, alog_here, skip_here,
-                dt_here, sem):
+                m0, m1, m2, m3, *rest):
+    extra = rest[: len(SPLIT)]
+    taps_x, taps_b, taps_c, bias_here, alog_here, skip_here, dt_here, sem = rest[len(SPLIT) :]
     place = place_of(sz)
     pairs = [(dt, dt_here)]
-    for k, m, mc in ((3, m3, c3), (1, m1, c1), (2, m2, c2), (0, m0, c0)):
-        pairs += message_parts(sz, lax.bitwise_xor(place, k), x, b, c, m, mc)
+    sent = (m0, m1, m2, m3)
+    for k in (*ORDER, 0):
+        m = sent[k]
+        pairs += message_parts(sz, lax.bitwise_xor(place, k), x, b, c, m, c_part(sz, k, m, extra))
     pairs += [
         (lanes_of(conv_x, place, sz.x_blocks * LANES), taps_x),
         (lanes_of(conv_b, place, STATE), taps_b),
@@ -142,11 +157,10 @@
     return jnp.sum(jnp.where(spot == line + head0, row, 0.0), axis=1, keepdims=True)
 
 
-def state_kernel(sz, bias, alog, m0, m3, m1, m2, taps_x, taps_b, halo,
-                 msg, xc, bc, stats, first, xs, bs, dts, tails, packed):
+def convolve(sz, bias, alog, messages, taps_x, taps_b, halo, xc, bc, stats, first, xs, bs, dts):
     chain = sz.blocks > 2
     place = place_of(sz)
-    messages = (m0, m1, m2, m3)
+    m0, m1, m2, m3 = messages
     dt_at = slice(sz.rows, sz.rows + sz.heads)
     near, far = (
         p[dt_at, sz.dt_lanes].astype(F32) + q[dt_at, sz.dt_lanes].astype(F32)
@@ -189,13 +203,49 @@
         taps = halved_taps(taps_b, t, sz.taps)
         cols = slice(t * LANES, (t + 1) * LANES)
         bc[:, cols] = silu_half(conv_block(bs, BLOCK, taps, t)).astype(BF16)
-    states = []
     for t in range(sz.x_blocks):
         taps = halved_taps(taps_x, t, sz.taps)
         cols = slice(t * LANES, (t + 1) * LANES)
-        value = silu_half(conv_block(xs, BLOCK, taps, t)).astype(BF16)
-        xc[:, cols] = value
-        turned = jnp.transpose(value.astype(F32))
+        xc[:, cols] = silu_half(conv_block(xs, BLOCK, taps, t)).astype(BF16)
+    for t in range(sz.base):
+        buffer, u = (xs, t) if t < sz.x_blocks else (bs, t - sz.x_blocks)
+        cols = slice(u * LANES, (u + 1) * LANES)
+        first[t * HALO : (t + 1) * HALO, :] = buffer[HALO : 2 * HALO, cols]
+    return weight
+
+
+def in_first(sz):
+    return lax.axis_index("seq") < sz.places
+
+
+def in_last(sz):
+    return lax.axis_index("seq") >= (sz.blocks - 1) * sz.places
+
+
+def state_kernel(sz, bias, alog, m0, ma, mb, mc, taps_x, taps_b, halo,
+                 msg, xc, bc, stats, first, xs, bs, dts, tails, packed):
+    messages = by_partner(m0, (ma, mb, mc), ORDER)
+
+    def work():
+        weight = convolve(sz, bias, alog, messages, taps_x, taps_b, halo, xc, bc, stats, first, xs, bs, dts)
+        write_state(sz, messages, weight, msg, xc, bc, xs, bs, tails, packed)
+
+    if sz.blocks > 2:
+        work()
+    else:
+        pl.when(jnp.logical_not(in_last(sz)))(work)
+
+        @pl.when(in_last(sz))
+        def _():
+            msg[...] = jnp.zeros(msg.shape, msg.dtype)
+
+
+def write_state(sz, messages, weight, msg, xc, bc, xs, bs, tails, packed):
+    place = place_of(sz)
+    states = []
+    for t in range(sz.x_blocks):
+        cols = slice(t * LANES, (t + 1) * LANES)
+        turned = jnp.transpose(xc[:, cols].astype(F32))
         up = turned[0:HEAD_DIM] * weight[2 * t : 2 * t + 1]
         down = turned[HEAD_DIM:LANES] * weight[2 * t + 1 : 2 * t + 2]
         weighted = jnp.concatenate([up, down], axis=0).astype(BF16)
@@ -215,7 +265,6 @@
         if t < sz.base:
             buffer, u = (xs, t) if t < sz.x_blocks else (bs, t - sz.x_blocks)
             cols = slice(u * LANES, (u + 1) * LANES)
-            first[t * HALO : (t + 1) * HALO, :] = buffer[HALO : 2 * HALO, cols]
             last = buffer[BLOCK : BLOCK + HALO, cols]
         else:
             cols = slice((t - sz.base) * LANES, (t - sz.base + 1) * LANES)
@@ -224,15 +273,31 @@
     msg[base:, :] = packed[...].astype(msg.dtype)
 
 
-def inner_kernel(sz, skip, c0, c3, c1, c2, taps_c, xc, bc, stats, halo,
-                 out, growth, gains, cc, columns, first_c, cs, turned):
+def hand_out(sz, total, outs):
+    place = place_of(sz)
+    for k, o in enumerate(outs):
+        target = lax.bitwise_xor(place, k)
+        o[...] = total[pl.ds(pl.multiple_of(target * sz.rows, 8), sz.rows), :].astype(BF16)
+
+
+def inner_kernel(sz, _xc, _bc, _stats, _first, skip, bias, alog, m0, ma, mb, mc, taps_x, taps_b, taps_c, halo, *rest):
+    messages = by_partner(m0, (ma, mb, mc), ORDER)
+    extra = rest[: len(SPLIT)]
+    xc, bc, stats, first, *early, out, growth, gains, cc, columns, first_c, cs, turned, xs, bs, dts = rest[len(SPLIT) :]
     chain = sz.blocks > 2
+    if not chain:
+
+        @pl.when(in_last(sz))
+        def _():
+            convolve(sz, bias, alog, messages, taps_x, taps_b, halo, xc, bc, stats, first, xs, bs, dts)
+
     place = place_of(sz)
     g = sz.per_group
     turned[...] = jnp.transpose(stats[...])
     columns[...] = turned[0:EDGE, :]
     skips = of_heads(sz, skip, place * g)
-    gather(sz, cs, place, 0, sz.s_blocks, (c0, c1, c2, c3))
+    parts = [c_part(sz, k, m, extra) for k, m in enumerate(messages)]
+    gather(sz, cs, place, 0, sz.s_blocks, parts)
     for t in range(sz.s_blocks):
         cols = slice(t * LANES, (t + 1) * LANES)
         if chain:
@@ -243,7 +308,7 @@
         taps = halved_taps(taps_c, t, sz.taps)
         cc[:, cols] = silu_half(conv_block(cs, BLOCK, taps, t)).astype(BF16)
     half = BLOCK // 2
-    skip_keys = 0 if chain else EDGE
+    skip_keys = 0 if chain else jnp.where(in_first(sz), 0, EDGE)
     low_lanes = lax.broadcasted_iota(jnp.int32, (half, LANES), 1) < HEAD_DIM
     for t in range(sz.x_blocks):
         cols = slice(t * LANES, (t + 1) * LANES)
@@ -267,20 +332,20 @@
             out[at, cols] = both + gains[0:1, cols] * xc[at, cols].astype(F32)
             rise = 2 * g + 2 * t
             growth[at, cols] = jnp.where(low_lanes, turned[at, rise : rise + 1], turned[at, rise + 1 : rise + 2])
+    hand_out(sz, out, early)
 
 
 def outer_kernel(sz, taps_x, taps_b, taps_c, xc, bc, cc, stats, columns, first, first_c, growth, gains,
                  inner, arrived, o0, o1, o2, o3, edge, ahead, c_all, total):
     chain = sz.blocks > 2
     place = place_of(sz)
-    later = lax.axis_index("seq") >= sz.places
-    g, rows = sz.per_group, sz.rows
+    g = sz.per_group
     if chain:
         c_all[...] = cc[...]
     else:
         base = sz.x_blocks * STATE
         renewed, over = [], sz.taps - 1
-        ahead[...] = jnp.where(later, arrived[base:, :].astype(F32), 0.0)
+        ahead[...] = arrived[base:, :].astype(F32)
         for t in range(sz.cols):
             cols = slice(t * LANES, (t + 1) * LANES)
             edge[HALO - over : HALO, cols] = ahead[t * over : (t + 1) * over, :]
@@ -310,7 +375,7 @@
             arrived[(t * sz.s_blocks + s) * LANES : (t * sz.s_blocks + s + 1) * LANES, :]
             for s in range(sz.s_blocks)
         ]
-        state = jnp.where(later, jnp.concatenate(pieces, axis=1).astype(F32), 0.0).astype(BF16)
+        state = jnp.concatenate(pieces, axis=1)
         out = inner[:, cols] + dot(c_all[...], state, NT) * growth[:, cols]
         if not chain:
             mixed, values = [], []
@@ -330,29 +395,33 @@
             total[0:EDGE, cols] = out[0:EDGE] + change
         else:
             total[:, cols] = out
-    for k, o in enumerate((o0, o1, o2, o3)):
-        target = lax.bitwise_xor(place, k)
-        o[...] = total[pl.ds(pl.multiple_of(target * rows, 8), rows), :].astype(BF16)
-
-
-def norm_kernel(sz, o0, r3, r1, r2, z, gain, out):
+    hand_out(sz, total, (o0, o1, o2, o3))
+
+
+def norm_kernel(sz, o0, ra, rb, rc, e0, ea, eb, ec, z, gain, out, ready, sem):
     place = place_of(sz)
     width = sz.x_blocks * LANES
-    for k, part in enumerate((o0, r1, r2, r3)):
-        group = lax.bitwise_xor(place, k)
-        at = pl.ds(pl.multiple_of(group * width, LANES), width)
+    copies = []
+    early = by_partner(e0, (ea, eb, ec), RETURN)
+    for k, part in enumerate(by_partner(o0, (ra, rb, rc), RETURN)):
+        at = pl.ds(pl.multiple_of(lax.bitwise_xor(place, k) * width, LANES), width)
         gate = 0.5 * z[:, at].astype(F32)
-        value = part[...].astype(F32) * silu_half(gate)
+        value = jnp.where(in_first(sz), early[k][...], part[...]).astype(F32) * silu_half(gate)
         mean = jnp.sum(value * value, axis=-1, keepdims=True) * (1.0 / width)
-        out[:, at] = (value * lax.rsqrt(mean + 1e-05) * gain[0:1, at]).astype(BF16)
-
-
-def call(kernel, sz, outs, scratch, specs, name, flops=0, touched=0):
+        ready[k] = (value * lax.rsqrt(mean + 1e-05) * gain[0:1, at]).astype(BF16)
+        copies.append(pltpu.make_async_copy(ready.at[k], out.at[:, at], sem.at[k]))
+        copies[-1].start()
+    for copy in copies:
+        copy.wait()
+
+
+def call(kernel, sz, outs, scratch, specs, name, flops=0, touched=0, aliases=None, outputs=None):
     return pl.pallas_call(
         functools.partial(kernel, sz),
         out_shape=[jax.ShapeDtypeStruct(s, d) for s, d in outs],
         in_specs=specs,
-        out_specs=[VMEM] * len(outs),
+        out_specs=outputs or [VMEM] * len(outs),
+        input_output_aliases=aliases or {},
         scratch_shapes=[s if not isinstance(s, tuple) else pltpu.VMEM(*s) for s in scratch],
         compiler_params=pltpu.CompilerParams(vmem_limit_bytes=24 << 20),
         cost_estimate=pl.CostEstimate(flops=flops, bytes_accessed=touched, transcendentals=0),
@@ -365,28 +434,33 @@
     sz = Sizes(x_in, b_in, dt_raw, seq_total, conv_x.shape[0])
     n, rows = sz.places, sz.rows
     chain = sz.blocks > 2
-
-    def swap(k):
-        return [(i, i - i % n + ((i % n) ^ k)) for i in range(seq_total)]
+    cores = lax.axis_size("head")
+
+    def swap(k, first=0, end=seq_total):
+        pairs = []
+        for i in range(seq_total):
+            for core in range(cores):
+                there = (i - i % n + ((i % n) ^ k), core) if first <= i < end else (i, cores - 1 - core)
+                pairs.append((i * cores + core, there[0] * cores + there[1]))
+        return pairs
 
     def onward(k, wrap):
         pairs = [(i, i + n * k) for i in range(seq_total)]
         return [(i, j % seq_total) for i, j in pairs if wrap or j < seq_total]
 
-    def ordered(arrays):
-        return [arrays[0]] + [arrays[k] for k in ORDER]
+    def ordered(arrays, order):
+        return [arrays[0]] + [arrays[k] for k in order]
 
     def stay(*arrays):
         return [pltpu.with_memory_space_constraint(a, pltpu.HBM) for a in arrays]
 
     width = sz.x_blocks * LANES
-    to_c = ((rows, STATE), BF16)
     vectors = [v.reshape(1, -1) for v in (dt_bias, a_log, d_skip)]
     *sent, taps_x, taps_b, taps_c, bias, alog, skip = call(
         pack_kernel,
         sz,
-        [(sz.message, BF16)] * n
-        + [to_c] * n
+        [((sz.high, (sz.base + (0 if k in SPLIT else sz.s_blocks)) * LANES), BF16) for k in range(n)]
+        + [((rows, STATE), BF16)] * len(SPLIT)
         + [((sz.taps, width), BF16)]
         + [((sz.taps, STATE), BF16)] * 2
         + [((1, sz.heads), F32)] * 3,
@@ -394,13 +468,10 @@
         [HBM] * 10,
         "pack",
     )(*stay(x_in, b_in, c_in, dt_raw.T, conv_x, conv_b, conv_c, *vectors))
-    arrivals = {}
+    came = sent[:n]
     for k in ORDER:
-        arrivals[k] = lax.ppermute(sent[k], "seq", swap(k))
-    for k in ORDER:
-        arrivals[n + k] = lax.ppermute(sent[n + k], "seq", swap(k))
-    came = [sent[0]] + [arrivals[k] for k in range(1, n)]
-    came_c = [sent[n]] + [arrivals[n + k] for k in range(1, n)]
+        came[k] = lax.ppermute(sent[k], ("seq", "head"), swap(k))
+    extra = [lax.ppermute(sent[n + i], ("seq", "head"), swap(k)) for i, k in enumerate(SPLIT)]
 
     padded = BLOCK + HALO
     edge_rows = sz.halo_rows
@@ -408,38 +479,37 @@
         place = lax.rem(lax.axis_index("seq"), n)
         ends = []
         for m in came:
-            both = jnp.concatenate([m[rows - HALO : rows], m[rows : rows + HALO, :STATE]], axis=1)
+            both = jnp.concatenate([m[rows - HALO : rows, : sz.base * LANES], m[rows : rows + HALO, :STATE]], axis=1)
             ends.append(both.reshape(HALO, sz.cols, LANES).swapaxes(0, 1).reshape(-1, LANES))
         tail = lax.dynamic_index_in_dim(jnp.stack(ends), lax.bitwise_xor(place, n - 1), 0, keepdims=False)
         halo = lax.ppermute(tail, "seq", onward(1, False)).astype(F32)
     else:
         halo = jnp.zeros((8, LANES), F32)
 
-    msg, xc, bc, stats, first = call(
+    convolved = [
+        ((BLOCK, width), BF16),
+        ((BLOCK, STATE), BF16),
+        ((sz.stat_rows, BLOCK), F32),
+        ((sz.base * HALO, LANES), F32),
+    ]
+    buffers = [((padded, width), F32), ((padded, STATE), F32), ((sz.heads, BLOCK), F32)]
+    msg, *held = call(
         state_kernel,
         sz,
-        [
-            ((sz.x_blocks * STATE + edge_rows, LANES), F32 if chain else BF16),
-            ((BLOCK, width), BF16),
-            ((BLOCK, STATE), BF16),
-            ((sz.stat_rows, BLOCK), F32),
-            ((sz.base * HALO, LANES), F32),
-        ],
-        [
-            ((padded, width), F32),
-            ((padded, STATE), F32),
-            ((sz.heads, BLOCK), F32),
+        [((sz.x_blocks * STATE + edge_rows, LANES), F32 if chain else BF16)] + convolved,
+        buffers
+        + [
             ((n * HALO, STATE), F32),
             ((edge_rows, LANES), F32),
         ],
         [VMEM] * 9,
         "state",
-    )(bias, alog, *ordered(came), taps_x, taps_b, halo)
+    )(bias, alog, *ordered(came, ORDER), taps_x, taps_b, halo)
 
     if chain:
         cut = sz.x_blocks * STATE
         grown = msg[:cut].reshape(sz.x_blocks, sz.s_blocks, 2, HEAD_DIM, LANES)
-        fade = jnp.exp(stats[: sz.per_group, BLOCK - 1]).reshape(sz.x_blocks, 1, 2, 1, 1)
+        fade = jnp.exp(held[2][: sz.per_group, BLOCK - 1]).reshape(sz.x_blocks, 1, 2, 1, 1)
         k = 1
         while k < sz.blocks:
             grown = grown + fade * lax.ppermute(grown, "seq", onward(k, False))
@@ -448,10 +518,13 @@
         msg = jnp.concatenate([grown.reshape(cut, LANES), msg[cut:]], axis=0).astype(BF16)
     arrived = lax.ppermute(msg, "seq", onward(1, True))
 
-    inner, growth, gains, cc, columns, first_c = call(
+    pieces = [((rows, width), BF16)] * n
+    xc, bc, stats, first, *early, inner, growth, gains, cc, columns, first_c = call(
         inner_kernel,
         sz,
-        [
+        convolved
+        + pieces
+        + [
             ((BLOCK, width), F32),
             ((BLOCK, width), F32),
             ((8, width), F32),
@@ -459,17 +532,21 @@
             ((EDGE, sz.stat_rows), F32),
             ((sz.s_blocks * HALO, LANES), F32),
         ],
-        [((padded, STATE), F32), ((BLOCK, sz.stat_rows), F32)],
-        [VMEM] * 10,
+        [((padded, STATE), F32), ((BLOCK, sz.stat_rows), F32)] + buffers,
+        [VMEM] * (15 + len(SPLIT)),
         "inner",
+        aliases={i: i for i in range(4)},
         flops=1 << 30,
         touched=1 << 22,
-    )(skip, *ordered(came_c), taps_c, xc, bc, stats, halo)
+    )(*held, skip, bias, alog, *ordered(came, ORDER), taps_x, taps_b, taps_c, halo, *extra)
+
+    for k in RETURN:
+        early[k] = lax.ppermute(early[k], ("seq", "head"), swap(k, 0, n))
 
     back = call(
         outer_kernel,
         sz,
-        [((rows, width), BF16)] * 4,
+        pieces,
         [
             ((2 * HALO, sz.cols * LANES), F32),
             ((edge_rows, LANES), F32),
@@ -479,12 +556,20 @@
         [VMEM] * 14,
         "outer",
     )(taps_x, taps_b, taps_c, xc, bc, cc, stats, columns, first, first_c, growth, gains, inner, arrived)
-    home = list(back)
-    for k in ORDER:
-        home[k] = lax.ppermute(back[k], "seq", swap(k))
-
-    out = call(norm_kernel, sz, [(x_in.shape, BF16)], [], [VMEM] * 6, "norm")(
-        *ordered(home), z_in, norm_gain.reshape(1, -1)
+    back = list(back)
+    for k in RETURN:
+        back[k] = lax.ppermute(back[k], ("seq", "head"), swap(k, n))
+
+    out = call(
+        norm_kernel,
+        sz,
+        [(x_in.shape, BF16)],
+        [((n, rows, width), BF16), pltpu.SemaphoreType.DMA((n,))],
+        [VMEM] * 10,
+        "norm",
+        outputs=[HBM],
+    )(
+        *ordered(back, RETURN), *ordered(early, RETURN), z_in, norm_gain.reshape(1, -1)
     )
     return out[0]
 

time: 23.9 us -> 23.1 us (0.967)
  the two profiles are of different devices: /device:TPU:0 before, /device:TPU:16 now
where the time goes in v5:
time: 23.1 us; the launch traced here: 22.8 us
  starting transfers between devices  11.9 us (52%)
  waiting for transfers between devices  6.72 us (29%)
  Pallas kernels  3.53 us (15%)
  local copies, waits for them, and re-layouts  0.68 us (3%)
    ppermute x3, starting transfers between devices, body(): back[k] = lax.ppermute(back[k], ('seq', 'head'), swap(k, n))  3.55 us
    ppermute x3, starting transfers between devices, body(): came[k] = lax.ppermute(sent[k], ('seq', 'head'), swap(k))  3.55 us
    ppermute x3, waiting for transfers between devices, body(): back[k] = lax.ppermute(back[k], ('seq', 'head'), swap(k, n))  3.47 us
    ppermute x2, starting transfers between devices, body(): lax.ppermute(sent[n + i], ('seq', 'head'), swap(k))  3.07 us
    ppermute x1, waiting for transfers between devices, body(): arrived = lax.ppermute(msg, 'seq', onward(1, True))  1.96 us
    pallas_call x1, Pallas kernels, body(): call(pack_kernel, sz, [((sz.high, (sz.base + (0 if k in SPLIT else sz.s_b...  1.18 us
    pallas_call x1, Pallas kernels, body(): call(inner_kernel, sz, convolved + pieces + [((BLOCK, width), F32), ((BLO...  1.12 us
    ppermute x1, starting transfers between devices, body(): arrived = lax.ppermute(msg, 'seq', onward(1, True))  1.03 us
  transfers between devices with their start and end apart: 12, of which 7 were waited for; matrix products, arithmetic and copies ran while one was open for 0% of the time, Pallas kernels for 7%

profile of v5, /device:TPU:16, one launch (start us, length us, event | category | flops | bytes accessed | tf_op | source)
XLA Modules:
  0.0 22.8 jit_solution(5348051279142012823)
XLA Ops:
  0.0 1.2 %pack.1 = (bf16[72,640]{1,0:T(8,128)(2,1)S(1)}, bf16[72,384]{1,0:T(8,128)(2,1)S(1)}, bf16[72,384]{1,0:T(8,128)(2,1)S(1)}, bf16[72,640]{1,0:T(8,128)(2,1)S(1)}, b...) custom-call(bf16[64,512]{1,0:T(8,128)(2,1)} %x.1, ...), custom_call_target="tpu_custom_call" | custom-call | tf_op jit(solution)/shard_map/pack/pallas_call | solution.py:459
  1.2 2.6 %collective-permute-start = (bf16[72,640]{1,0:T(8,128)(2,1)S(1)}, bf16[72,640]{1,0:T(8,128)(2,1)S(1)}, u32[]{:S(2)}, u32[]{:S(2)}) collective-permute-start(bf16[72,640]{1,0:T(8,128)(2,1)S(1)} %get-tuple-element.46), channel_id=1, source_target_pairs={{0,6},{1,7},{2,4},{3,5},{4,2},{5,3},{6,0},{7,1},{8,14},{9,15},{10,... | collective-permute-start | bytes 276488 | tf_op jit(solution)/shard_map/ppermute | solution.py:473
  3.8 0.5 %collective-permute-start.1 = (bf16[72,384]{1,0:T(8,128)(2,1)S(1)}, bf16[72,384]{1,0:T(8,128)(2,1)S(1)}, u32[]{:S(2)}, u32[]{:S(2)}) collective-permute-start(bf16[72,384]{1,0:T(8,128)(2,1)S(1)} %get-tuple-element.47), channel_id=1, source_target_pairs={{0,2},{1,3},{2,0},{3,1},{4,6},{5,7},{6,4},{7,5},{8,10},{9,11},{10,... | collective-permute-start | bytes 165896 | tf_op jit(solution)/shard_map/ppermute | solution.py:473
  4.3 0.4 %collective-permute-start.2 = (bf16[72,384]{1,0:T(8,128)(2,1)S(1)}, bf16[72,384]{1,0:T(8,128)(2,1)S(1)}, u32[]{:S(2)}, u32[]{:S(2)}) collective-permute-start(bf16[72,384]{1,0:T(8,128)(2,1)S(1)} %get-tuple-element.48), channel_id=1, source_target_pairs={{0,4},{1,5},{2,6},{3,7},{4,0},{5,1},{6,2},{7,3},{8,12},{9,13},{10,... | collective-permute-start | bytes 165896 | tf_op jit(solution)/shard_map/ppermute | solution.py:473
  4.7 1.5 %collective-permute-start.3 = (bf16[64,256]{1,0:T(8,128)(2,1)S(1)}, bf16[64,256]{1,0:T(8,128)(2,1)S(1)}, u32[]{:S(2)}, u32[]{:S(2)}) collective-permute-start(bf16[64,256]{1,0:T(8,128)(2,1)S(1)} %get-tuple-element.54), channel_id=1, source_target_pairs={{0,2},{1,3},{2,0},{3,1},{4,6},{5,7},{6,4},{7,5},{8,10},{9,11},{10,... | collective-permute-start | bytes 98312 | tf_op jit(solution)/shard_map/ppermute | solution.py:474
  6.2 1.6 %collective-permute-start.4 = (bf16[64,256]{1,0:T(8,128)(2,1)S(1)}, bf16[64,256]{1,0:T(8,128)(2,1)S(1)}, u32[]{:S(2)}, u32[]{:S(2)}) collective-permute-start(bf16[64,256]{1,0:T(8,128)(2,1)S(1)} %get-tuple-element.55), channel_id=1, source_target_pairs={{0,4},{1,5},{2,6},{3,7},{4,0},{5,1},{6,2},{7,3},{8,12},{9,13},{10,... | collective-permute-start | bytes 98312 | tf_op jit(solution)/shard_map/ppermute | solution.py:474
  7.8 0.4 %collective-permute-done.1.mb = bf16[72,384]{1,0:T(8,128)(2,1)S(1)} collective-permute-done((bf16[72,384]{1,0:T(8,128)(2,1)S(1)}, bf16[72,384]{1,0:T(8,128)(2,1)S(1)}, u32[]{:S(2)}, u32[]{:S(2)}) %collective-permute-start.1) | collective-permute-done | bytes 55328 | tf_op jit(solution)/shard_map/ppermute | solution.py:473
  8.2 0.2 %collective-permute-done.2.mc = bf16[72,384]{1,0:T(8,128)(2,1)S(1)} collective-permute-done((bf16[72,384]{1,0:T(8,128)(2,1)S(1)}, bf16[72,384]{1,0:T(8,128)(2,1)S(1)}, u32[]{:S(2)}, u32[]{:S(2)}) %collective-permute-start.2) | collective-permute-done | bytes 55328 | tf_op jit(solution)/shard_map/ppermute | solution.py:473
  8.5 0.0 collective-permute-done.ma
  8.5 1.0 %collective-permute-start.5 = (bf16[272,128]{1,0:T(8,128)(2,1)S(1)}, bf16[272,128]{1,0:T(8,128)(2,1)S(1)}, u32[]{:S(2)}, u32[]{:S(2)}) collective-permute-start(bf16[272,128]{1,0:T(8,128)(2,1)S(1)} %get-tuple-element.66), channel_id=1, source_target_pairs={{0,8},{2,10},{4,12},{6,14},{8,0},{10,2},{12,4},{14,6},{1,9},{3,11}... | collective-permute-start | bytes 208904 | tf_op jit(solution)/shard_map/ppermute | solution.py:519
  9.5 0.0 collective-permute-done.3.rest_0_
  9.5 0.6 %collective-permute-done.4.rest_1_ = bf16[64,256]{1,0:T(8,128)(2,1)S(1)} collective-permute-done((bf16[64,256]{1,0:T(8,128)(2,1)S(1)}, bf16[64,256]{1,0:T(8,128)(2,1)S(1)}, u32[]{:S(2)}, u32[]{:S(2)}) %collective-permute-start.4) | collective-permute-done | bytes 32800 | tf_op jit(solution)/shard_map/ppermute | solution.py:474
  10.2 1.1 %inner.1 = (bf16[256,128]{1,0:T(8,128)(2,1)S(1)}, bf16[256,256]{1,0:T(8,128)(2,1)S(1)}, f32[8,256]{1,0:T(8,128)S(1)}, f32[24,128]{1,0:T(8,128)S(1)}, bf16[64,128...) custom-call(bf16[256,128]{1,0:T(8,128)(2,1)S(1)} %get-tuple-element., ...), custom_call_target="tpu_custom_call", output_to_operand_aliasing={{0}: (0, {}), {1}: (1, {}), {2}: (2, {}), {3}: (3, {})} | custom-call | flops 1073741824 | bytes 4194304 | tf_op jit(solution)/shard_map/inner/pallas_call | solution.py:522
  11.3 0.1 collective-permute-start.9
  11.4 0.5 %collective-permute-start.10 = (bf16[64,128]{1,0:T(8,128)(2,1)S(1)}, bf16[64,128]{1,0:T(8,128)(2,1)S(1)}, u32[]{:S(2)}, u32[]{:S(2)}) collective-permute-start(bf16[64,128]{1,0:T(8,128)(2,1)S(1)} %get-tuple-element.73), channel_id=1, source_target_pairs={{0,2},{1,3},{2,0},{3,1},{4,6},{5,7},{6,4},{7,5},{8,9},{9,8},{10,11... | collective-permute-start | bytes 49160 | tf_op jit(solution)/shard_map/ppermute | solution.py:544
  11.9 0.1 collective-permute-start.11
  11.9 2.0 %collective-permute-done.5.arrived = bf16[272,128]{1,0:T(8,128)(2,1)S(1)} collective-permute-done((bf16[272,128]{1,0:T(8,128)(2,1)S(1)}, bf16[272,128]{1,0:T(8,128)(2,1)S(1)}, u32[]{:S(2)}, u32[]{:S(2)}) %collective-permute-start.5) | collective-permute-done | bytes 69664 | tf_op jit(solution)/shard_map/ppermute | solution.py:519
  13.9 0.0 copy-start
  13.9 0.4 %outer.1 = (bf16[64,128]{1,0:T(8,128)(2,1)S(1)}, bf16[64,128]{1,0:T(8,128)(2,1)S(1)}, bf16[64,128]{1,0:T(8,128)(2,1)S(1)}, bf16[64,128]{1,0:T(8,128)(2,1)S(1)}) custom-call(bf16[4,128]{1,0:T(4,128)(2,1)S(1)} %get-tuple-element.40.taps_x, bf16[4,256]{1,0:T(4,128)(2,1)S(1)} %get-tuple-element.41.taps_b, bf16[4,256]{1,0:T(4,128)(2,1)S(1)} %get-tuple-element.42.taps_c, ...), custom_call_target="tpu_custom_call" | custom-call | tf_op jit(solution)/shard_map/outer/pallas_call | solution.py:546
  14.3 1.5 %collective-permute-start.6 = (bf16[64,128]{1,0:T(8,128)(2,1)S(1)}, bf16[64,128]{1,0:T(8,128)(2,1)S(1)}, u32[]{:S(2)}, u32[]{:S(2)}) collective-permute-start(bf16[64,128]{1,0:T(8,128)(2,1)S(1)} %get-tuple-element.68), channel_id=1, source_target_pairs={{0,1},{1,0},{2,3},{3,2},{4,5},{5,4},{6,7},{7,6},{8,14},{9,15},{10,... | collective-permute-start | bytes 49160 | tf_op jit(solution)/shard_map/ppermute | solution.py:561
  15.9 1.8 %collective-permute-start.7 = (bf16[64,128]{1,0:T(8,128)(2,1)S(1)}, bf16[64,128]{1,0:T(8,128)(2,1)S(1)}, u32[]{:S(2)}, u32[]{:S(2)}) collective-permute-start(bf16[64,128]{1,0:T(8,128)(2,1)S(1)} %get-tuple-element.69), channel_id=1, source_target_pairs={{0,1},{1,0},{2,3},{3,2},{4,5},{5,4},{6,7},{7,6},{8,10},{9,11},{10,... | collective-permute-start | bytes 49160 | tf_op jit(solution)/shard_map/ppermute | solution.py:561
  17.6 0.0 collective-permute-done.9.ea
  17.6 0.3 %collective-permute-start.8 = (bf16[64,128]{1,0:T(8,128)(2,1)S(1)}, bf16[64,128]{1,0:T(8,128)(2,1)S(1)}, u32[]{:S(2)}, u32[]{:S(2)}) collective-permute-start(bf16[64,128]{1,0:T(8,128)(2,1)S(1)} %get-tuple-element.70), channel_id=1, source_target_pairs={{0,1},{1,0},{2,3},{3,2},{4,5},{5,4},{6,7},{7,6},{8,12},{9,13},{10,... | collective-permute-start | bytes 49160 | tf_op jit(solution)/shard_map/ppermute | solution.py:561
  17.9 0.0 collective-permute-done.10.eb
  17.9 0.0 collective-permute-done.11.ec
  17.9 1.1 %collective-permute-done.6.ra = bf16[64,128]{1,0:T(8,128)(2,1)S(1)} collective-permute-done((bf16[64,128]{1,0:T(8,128)(2,1)S(1)}, bf16[64,128]{1,0:T(8,128)(2,1)S(1)}, u32[]{:S(2)}, u32[]{:S(2)}) %collective-permute-start.6) | collective-permute-done | bytes 16416 | tf_op jit(solution)/shard_map/ppermute | solution.py:561
  19.0 0.5 %collective-permute-done.7.rb = bf16[64,128]{1,0:T(8,128)(2,1)S(1)} collective-permute-done((bf16[64,128]{1,0:T(8,128)(2,1)S(1)}, bf16[64,128]{1,0:T(8,128)(2,1)S(1)}, u32[]{:S(2)}, u32[]{:S(2)}) %collective-permute-start.7) | collective-permute-done | bytes 16416 | tf_op jit(solution)/shard_map/ppermute | solution.py:561
  19.6 1.8 %collective-permute-done.8.rc = bf16[64,128]{1,0:T(8,128)(2,1)S(1)} collective-permute-done((bf16[64,128]{1,0:T(8,128)(2,1)S(1)}, bf16[64,128]{1,0:T(8,128)(2,1)S(1)}, u32[]{:S(2)}, u32[]{:S(2)}) %collective-permute-start.8) | collective-permute-done | bytes 16416 | tf_op jit(solution)/shard_map/ppermute | solution.py:561
  21.4 0.0 copy-start.1
  21.4 0.0 copy-done
  21.4 0.7 %copy-done.1 = f32[512]{0:T(512)S(1)} copy-done((f32[512]{0:T(512)S(1)}, f32[512]{0:T(512)}, u32[]{:S(2)}) %copy-start.1) | copy-done | bytes 2072
  22.1 0.8 %norm.1 = bf16[64,512]{1,0:T(8,128)(2,1)} custom-call(bf16[64,128]{1,0:T(8,128)(2,1)S(1)} %get-tuple-element.67.o0, bf16[64,128]{1,0:T(8,128)(2,1)S(1)} %collective-permute-done.6.ra, bf16[64,128]{1,0:T(8,128)(2,1)S(1)} %collective-permute-done.7.rb, bf16[64,128]{1,0:T(8,128)(2,1)S(1)} %collective-permute-done.8.rc, ...), custom_call_target="tpu_custom_call" | custom-call | tf_op jit(solution)/shard_map/norm/pallas_call | solution.py:563
  (2 shorter events, 0.0 us)
Async XLA Ops:
  1.2 7.3 %collective-permute-start = (bf16[72,640]{1,0:T(8,128)(2,1)S(1)}, bf16[72,640]{1,0:T(8,128)(2,1)S(1)}, u32[]{:S(2)}, u32[]{:S(2)}) collective-permute-start(bf16[72,640]{1,0:T(8,128)(2,1)S(1)} %get-tuple-element.46), channel_id=1, source_target_pairs={{0,6},{1,7},{2,4},{3,5},{4,2},{5,3},{6,0},{7,1},{8,14},{9,15},{10,... | collective-permute-start | bytes 276488 | tf_op jit(solution)/shard_map/ppermute | solution.py:473
  3.8 4.5 %collective-permute-start.1 = (bf16[72,384]{1,0:T(8,128)(2,1)S(1)}, bf16[72,384]{1,0:T(8,128)(2,1)S(1)}, u32[]{:S(2)}, u32[]{:S(2)}) collective-permute-start(bf16[72,384]{1,0:T(8,128)(2,1)S(1)} %get-tuple-element.47), channel_id=1, source_target_pairs={{0,2},{1,3},{2,0},{3,1},{4,6},{5,7},{6,4},{7,5},{8,10},{9,11},{10,... | collective-permute-start | bytes 165896 | tf_op jit(solution)/shard_map/ppermute | solution.py:473
  4.3 4.2 %collective-permute-start.2 = (bf16[72,384]{1,0:T(8,128)(2,1)S(1)}, bf16[72,384]{1,0:T(8,128)(2,1)S(1)}, u32[]{:S(2)}, u32[]{:S(2)}) collective-permute-start(bf16[72,384]{1,0:T(8,128)(2,1)S(1)} %get-tuple-element.48), channel_id=1, source_target_pairs={{0,4},{1,5},{2,6},{3,7},{4,0},{5,1},{6,2},{7,3},{8,12},{9,13},{10,... | collective-permute-start | bytes 165896 | tf_op jit(solution)/shard_map/ppermute | solution.py:473
  4.7 4.8 %collective-permute-start.3 = (bf16[64,256]{1,0:T(8,128)(2,1)S(1)}, bf16[64,256]{1,0:T(8,128)(2,1)S(1)}, u32[]{:S(2)}, u32[]{:S(2)}) collective-permute-start(bf16[64,256]{1,0:T(8,128)(2,1)S(1)} %get-tuple-element.54), channel_id=1, source_target_pairs={{0,2},{1,3},{2,0},{3,1},{4,6},{5,7},{6,4},{7,5},{8,10},{9,11},{10,... | collective-permute-start | bytes 98312 | tf_op jit(solution)/shard_map/ppermute | solution.py:474
  6.2 3.9 %collective-permute-start.4 = (bf16[64,256]{1,0:T(8,128)(2,1)S(1)}, bf16[64,256]{1,0:T(8,128)(2,1)S(1)}, u32[]{:S(2)}, u32[]{:S(2)}) collective-permute-start(bf16[64,256]{1,0:T(8,128)(2,1)S(1)} %get-tuple-element.55), channel_id=1, source_target_pairs={{0,4},{1,5},{2,6},{3,7},{4,0},{5,1},{6,2},{7,3},{8,12},{9,13},{10,... | collective-permute-start | bytes 98312 | tf_op jit(solution)/shard_map/ppermute | solution.py:474
  8.5 5.4 %collective-permute-start.5 = (bf16[272,128]{1,0:T(8,128)(2,1)S(1)}, bf16[272,128]{1,0:T(8,128)(2,1)S(1)}, u32[]{:S(2)}, u32[]{:S(2)}) collective-permute-start(bf16[272,128]{1,0:T(8,128)(2,1)S(1)} %get-tuple-element.66), channel_id=1, source_target_pairs={{0,8},{2,10},{4,12},{6,14},{8,0},{10,2},{12,4},{14,6},{1,9},{3,11}... | collective-permute-start | bytes 208904 | tf_op jit(solution)/shard_map/ppermute | solution.py:519
  11.3 6.4 %collective-permute-start.9 = (bf16[64,128]{1,0:T(8,128)(2,1)S(1)}, bf16[64,128]{1,0:T(8,128)(2,1)S(1)}, u32[]{:S(2)}, u32[]{:S(2)}) collective-permute-start(bf16[64,128]{1,0:T(8,128)(2,1)S(1)} %get-tuple-element.72), channel_id=1, source_target_pairs={{0,6},{1,7},{2,4},{3,5},{4,2},{5,3},{6,0},{7,1},{8,9},{9,8},{10,11... | collective-permute-start | bytes 49160 | tf_op jit(solution)/shard_map/ppermute | solution.py:544
  11.4 6.5 %collective-permute-start.10 = (bf16[64,128]{1,0:T(8,128)(2,1)S(1)}, bf16[64,128]{1,0:T(8,128)(2,1)S(1)}, u32[]{:S(2)}, u32[]{:S(2)}) collective-permute-start(bf16[64,128]{1,0:T(8,128)(2,1)S(1)} %get-tuple-element.73), channel_id=1, source_target_pairs={{0,2},{1,3},{2,0},{3,1},{4,6},{5,7},{6,4},{7,5},{8,9},{9,8},{10,11... | collective-permute-start | bytes 49160 | tf_op jit(solution)/shard_map/ppermute | solution.py:544
  11.9 6.1 %collective-permute-start.11 = (bf16[64,128]{1,0:T(8,128)(2,1)S(1)}, bf16[64,128]{1,0:T(8,128)(2,1)S(1)}, u32[]{:S(2)}, u32[]{:S(2)}) collective-permute-start(bf16[64,128]{1,0:T(8,128)(2,1)S(1)} %get-tuple-element.74), channel_id=1, source_target_pairs={{0,4},{1,5},{2,6},{3,7},{4,0},{5,1},{6,2},{7,3},{8,9},{9,8},{10,11... | collective-permute-start | bytes 49160 | tf_op jit(solution)/shard_map/ppermute | solution.py:544
  13.9 7.5 %copy-start = (bf16[64,512]{1,0:T(8,128)(2,1)S(1)}, bf16[64,512]{1,0:T(8,128)(2,1)}, u32[]{:S(2)}) copy-start(bf16[64,512]{1,0:T(8,128)(2,1)} %z.1) | copy-start | bytes 196612
  14.3 4.7 %collective-permute-start.6 = (bf16[64,128]{1,0:T(8,128)(2,1)S(1)}, bf16[64,128]{1,0:T(8,128)(2,1)S(1)}, u32[]{:S(2)}, u32[]{:S(2)}) collective-permute-start(bf16[64,128]{1,0:T(8,128)(2,1)S(1)} %get-tuple-element.68), channel_id=1, source_target_pairs={{0,1},{1,0},{2,3},{3,2},{4,5},{5,4},{6,7},{7,6},{8,14},{9,15},{10,... | collective-permute-start | bytes 49160 | tf_op jit(solution)/shard_map/ppermute | solution.py:561
  15.9 3.7 %collective-permute-start.7 = (bf16[64,128]{1,0:T(8,128)(2,1)S(1)}, bf16[64,128]{1,0:T(8,128)(2,1)S(1)}, u32[]{:S(2)}, u32[]{:S(2)}) collective-permute-start(bf16[64,128]{1,0:T(8,128)(2,1)S(1)} %get-tuple-element.69), channel_id=1, source_target_pairs={{0,1},{1,0},{2,3},{3,2},{4,5},{5,4},{6,7},{7,6},{8,10},{9,11},{10,... | collective-permute-start | bytes 49160 | tf_op jit(solution)/shard_map/ppermute | solution.py:561
  17.6 3.7 %collective-permute-start.8 = (bf16[64,128]{1,0:T(8,128)(2,1)S(1)}, bf16[64,128]{1,0:T(8,128)(2,1)S(1)}, u32[]{:S(2)}, u32[]{:S(2)}) collective-permute-start(bf16[64,128]{1,0:T(8,128)(2,1)S(1)} %get-tuple-element.70), channel_id=1, source_target_pairs={{0,1},{1,0},{2,3},{3,2},{4,5},{5,4},{6,7},{7,6},{8,12},{9,13},{10,... | collective-permute-start | bytes 49160 | tf_op jit(solution)/shard_map/ppermute | solution.py:561
  21.4 0.7 %copy-start.1 = (f32[512]{0:T(512)S(1)}, f32[512]{0:T(512)}, u32[]{:S(2)}) copy-start(f32[512]{0:T(512)} %param.23) | copy-start | bytes 6148
